TPU v7x, 256 devices: a whole 4x4x8 slice. The times are simulated.
256 devices in a mesh: section: 16 (over y, x), expert: 16 (over z, core).
Axes of the slice: x: 4, y: 4, z: 8, core: 2. Of those that a mesh axis runs over, the one named last changes fastest.
Arguments:
- layer_input: bfloat16 [16, 1024, 4096], P('section', 'expert'), may hold values from -6 to 6
- cotangent: bfloat16 [16, 1024, 4096], P('section', 'expert'), may hold values from -6 to 6
- gate_weight: bfloat16 [16, 4096, 6144], P('section', None, 'expert'), may hold values from -0.09375 to 0.09375
- up_weight: bfloat16 [16, 4096, 6144], P('section', None, 'expert'), may hold values from -0.09375 to 0.09375
- down_weight: bfloat16 [16, 6144, 4096], P('section', 'expert'), may hold values from -0.15625 to 0.15625
- stashed_pre: bfloat16 [16, 16, 24, 2, 6144], P('section', None, None, None, 'expert'), may hold values from -6 to 6
- first_ids: int32 [16, 1024, 1], P('section', 'expert'), may hold values from 0 to 3; in each aligned block of 64 rows (0 to 63, 64 to 127, ..., all dimensions but the last counted through in order) at most 24 rows name the same one
- first_gates: float32 [16, 1024, 1], P('section', 'expert'), may hold values from 0.3 to 1
- second_ids: int32 [16, 1024, 1], P('section', 'expert'), may hold values from 0 to 3; in each aligned block of 64 rows (0 to 63, 64 to 127, ..., all dimensions but the last counted through in order) at most 24 rows name the same one
- second_gates: float32 [16, 1024, 1], P('section', 'expert'), may hold values from 0.3 to 1
- keep_mask: int32 [16, 1024], P('section', 'expert'), may hold values 0 or 1
Outputs:
- next_input: bfloat16 [16, 1024, 4096], P('section', 'expert')
- prev_cotangent: bfloat16 [16, 1024, 4096], P('section', 'expert')
Inputs may be any that keep to these rules, and one draw needn't show every extreme that they name: `first_ids`: in each aligned block of 64 rows (the rows of one device) the picks of a row are distinct and no expert is named more than 24 times; in some blocks one expert is named exactly 24 times. `second_ids`: as for first_ids.
All inputs are finite; a program needn't handle non-finite values. No bound on the sum of `keep_mask` on one device may be relied on, other than what follows from the above.
Results may differ from a plain program's by a relative error of at most 0.0048.
Values may be sent and summed in bfloat16 or wider, within the bound.
No kernel may reach another device: no remote copies, remote signals or barrier semaphores. Data moves between devices by JAX's collectives and lax.ppermute only.
A program may use at most 128 MiB of HBM per device.

v0:
```python
import jax
import jax.numpy as jnp
from jax import lax
from jax.sharding import PartitionSpec as P

SHARDS = 4


def passed_along(block, axis, distance):
    devices = range(lax.axis_size(axis))
    route = [((i - distance) % len(devices), i) for i in devices]
    return lax.ppermute(block, axis, route)


def positions(route_ids, expert_count, capacity):
    flat_ids = route_ids.reshape(-1)
    onehot = (flat_ids[:, None] == jnp.arange(expert_count, dtype=jnp.int32)[None, :]).astype(
        jnp.int32
    )
    earlier = jnp.cumsum(onehot, axis=0) - onehot
    slot_count = jnp.sum(earlier * onehot, axis=1)
    return (flat_ids * capacity + slot_count).reshape(route_ids.shape)


def placement(slot_at, slot_total):
    match_table = jnp.arange(slot_total, dtype=jnp.int32)[:, None, None] == slot_at[None, :, :]
    return jnp.any(match_table, axis=2).astype(jnp.bfloat16)


def expert_forward(routed, gate_cols, up_cols, down_rows):
    gate_pre = jnp.dot(routed, gate_cols, preferred_element_type=jnp.float32)
    up_pre = jnp.dot(routed, up_cols, preferred_element_type=jnp.float32)
    hidden = (jax.nn.silu(gate_pre) * up_pre).astype(jnp.bfloat16)
    return jnp.dot(hidden, down_rows, preferred_element_type=jnp.float32).astype(jnp.bfloat16)


def expert_backward(routed, stash_rows, gate_cols, up_cols, down_rows):
    hidden_grad = jnp.dot(routed, down_rows.T, preferred_element_type=jnp.float32)
    gate_pre = stash_rows[:, 0, :].astype(jnp.float32)
    up_pre = stash_rows[:, 1, :].astype(jnp.float32)
    sigmoid_gate = jax.nn.sigmoid(gate_pre)
    grad_gate = (
        hidden_grad * up_pre * sigmoid_gate * (1.0 + gate_pre * (1.0 - sigmoid_gate))
    ).astype(jnp.bfloat16)
    grad_up = (hidden_grad * gate_pre * sigmoid_gate).astype(jnp.bfloat16)
    input_grad = jnp.dot(grad_gate, gate_cols.T, preferred_element_type=jnp.float32)
    input_grad = input_grad + jnp.dot(grad_up, up_cols.T, preferred_element_type=jnp.float32)
    return input_grad.astype(jnp.bfloat16)


def gather_back(summed, slot_at, gate_values):
    picked = jnp.take(summed, slot_at, axis=0).astype(jnp.float32)
    return jnp.sum(picked * gate_values[:, :, None], axis=1)


def local(
    layer_input,
    cotangent,
    gate_weight,
    up_weight,
    down_weight,
    stashed_pre,
    first_ids,
    first_gates,
    second_ids,
    second_gates,
    keep_mask,
):
    devices = lax.axis_size("expert")
    experts = devices // SHARDS
    capacity = stashed_pre.shape[2]
    model_width = layer_input.shape[2]
    hidden_local = gate_weight.shape[2]
    tokens_in = layer_input[0]
    keep_rows = keep_mask[0]
    kept_grads = cotangent[0] * keep_rows[:, None].astype(jnp.bfloat16)
    first_at = positions(first_ids[0], experts, capacity)
    second_at = positions(second_ids[0], experts, capacity)
    first_rows = jnp.dot(
        placement(first_at, experts * capacity), tokens_in, preferred_element_type=jnp.float32
    ).astype(jnp.bfloat16)
    second_rows = jnp.dot(
        placement(second_at, experts * capacity), kept_grads, preferred_element_type=jnp.float32
    ).astype(jnp.bfloat16)
    gate_cols = gate_weight[0]
    up_cols = up_weight[0]
    down_rows = down_weight[0]
    stash_local = stashed_pre[0].reshape(-1, 2, hidden_local)
    send_first = jnp.repeat(first_rows.reshape(experts, capacity, model_width), SHARDS, axis=0)
    send_second = jnp.repeat(second_rows.reshape(experts, capacity, model_width), SHARDS, axis=0)
    held_first, held_second = (
        lax.all_to_all(send_first, "expert", split_axis=0, concat_axis=0, tiled=True),
        lax.all_to_all(send_second, "expert", split_axis=0, concat_axis=0, tiled=True),
    )
    made_first = expert_forward(held_first.reshape(-1, model_width), gate_cols, up_cols, down_rows)
    made_second = expert_backward(
        held_second.reshape(-1, model_width), stash_local, gate_cols, up_cols, down_rows
    )
    back_first, back_second = (
        lax.all_to_all(
            made_first.reshape(devices, capacity, model_width),
            "expert",
            split_axis=0,
            concat_axis=0,
            tiled=True,
        ),
        lax.all_to_all(
            made_second.reshape(devices, capacity, model_width),
            "expert",
            split_axis=0,
            concat_axis=0,
            tiled=True,
        ),
    )
    summed_first = (
        jnp.sum(
            back_first.reshape(experts, SHARDS, capacity, model_width).astype(jnp.float32), axis=1
        )
        .astype(jnp.bfloat16)
        .reshape(-1, model_width)
    )
    summed_second = (
        jnp.sum(
            back_second.reshape(experts, SHARDS, capacity, model_width).astype(jnp.float32), axis=1
        )
        .astype(jnp.bfloat16)
        .reshape(-1, model_width)
    )
    first_branch = gather_back(summed_first, first_at, first_gates[0])
    second_branch = gather_back(summed_second, second_at, second_gates[0])
    mixed_out = (tokens_in.astype(jnp.float32) + first_branch).astype(jnp.bfloat16)
    keep_float = keep_rows[:, None].astype(jnp.float32)
    grad_out = (keep_float * (cotangent[0].astype(jnp.float32) + second_branch)).astype(
        jnp.bfloat16
    )
    moved_on = passed_along(mixed_out[None], "section", 1)
    moved_back = passed_along(grad_out[None], "section", -1)
    return (moved_on, moved_back)


def solution(mesh):
    placed = (
        P("section", "expert", None),
        P("section", "expert", None),
        P("section", None, "expert"),
        P("section", None, "expert"),
        P("section", "expert", None),
        P("section", None, None, None, "expert"),
        P("section", "expert", None),
        P("section", "expert", None),
        P("section", "expert", None),
        P("section", "expert", None),
        P("section", "expert"),
    )
    return jax.shard_map(
        local,
        mesh=mesh,
        in_specs=placed,
        out_specs=(P("section", "expert", None), P("section", "expert", None)),
        check_vma=False,
    )
```

profile of v0, /device:TPU:1, one launch (start us, length us, event | category | flops | bytes accessed | tf_op | source)
XLA Modules:
  0.0 348.9 jit_solution(3264317126432523698)
XLA Ops:
  5.3 2.1 broadcast_in_dim.22
  7.4 10.1 %all-to-all-start.2 = ((bf16[16,24,4096]{2,1,0:T(8,128)(2,1)}), bf16[16,24,4096]{2,1,0:T(8,128)(2,1)}, u32[]{:S(2)}, u32[]{:S(2)}) async-start(bf16[16,24,4096]{2,1,0:T(8,128)(2,1)} %bitcast.123), calls=%async_computation.2 | async-start | bytes 6291456 | tf_op jit(solution)/shard_map/all_to_all | solution.py:93
  17.9 2.3 convolution_convert_fusion.2
  20.1 68.4 %all-to-all-done.2 = bf16[16,24,4096]{2,1,0:T(8,128)(2,1)} async-done(((bf16[16,24,4096]{2,1,0:T(8,128)(2,1)}), bf16[16,24,4096]{2,1,0:T(8,128)(2,1)}, u32[]{:S(2)}, u32[]{:S(2)}) %all-to-all-start.2) | async-done | bytes 3145760 | tf_op jit(solution)/shard_map/all_to_all | solution.py:93
  88.6 3.2 broadcast_in_dim.13
  91.8 5.4 %all-to-all-start = ((bf16[16,24,4096]{2,1,0:T(8,128)(2,1)}), bf16[16,24,4096]{2,1,0:T(8,128)(2,1)}, u32[]{:S(2)}, u32[]{:S(2)}) async-start(bf16[16,24,4096]{2,1,0:T(8,128)(2,1)} %bitcast.124), calls=%async_computation | async-start | bytes 6291456 | tf_op jit(solution)/shard_map/all_to_all | solution.py:92
  98.4 4.8 %fusion = f32[384,384]{1,0:T(8,128)S(1)} fusion(bf16[384,4096]{1,0:T(8,128)(2,1)} %bitcast.31, bf16[1,384,4096]{2,1,0:T(8,128)(2,1)} %param.17), kind=kOutput, calls=%fused_computation.8 | convolution fusion | flops 1207959552 | bytes 6881280 | tf_op jit(solution)/shard_map/dot_general | solution.py:38
  103.2 1.9 fusion.6
  105.1 3.5 %add_convert_fusion = bf16[384,4096]{1,0:T(8,128)(2,1)} fusion(f32[384,4096]{1,0:T(8,128)S(1)} %fusion.6, bf16[1,4096,384]{2,1,0:T(8,128)(2,1)S(1)} %copy-done, f32[384,384]{1,0:T(8,128)S(1)} %fusion, bf16[384,2,384]{2,0,1:T(8,128)(2,1)S(1)} %bitcast.129), kind=kOutput, calls=%fused_computation.2 | convolution fusion | flops 1212137472 | bytes 13467648 | tf_op jit(solution)/shard_map/dot_general | solution.py:47
  108.6 59.7 %all-to-all-done = bf16[16,24,4096]{2,1,0:T(8,128)(2,1)} async-done(((bf16[16,24,4096]{2,1,0:T(8,128)(2,1)}), bf16[16,24,4096]{2,1,0:T(8,128)(2,1)}, u32[]{:S(2)}, u32[]{:S(2)}) %all-to-all-start) | async-done | bytes 3145760 | tf_op jit(solution)/shard_map/all_to_all | solution.py:92
  168.3 5.4 %all-to-all-start.3 = ((bf16[16,24,4096]{2,1,0:T(8,128)(2,1)}), bf16[16,24,4096]{2,1,0:T(8,128)(2,1)}, u32[]{:S(2)}, u32[]{:S(2)}) async-start(bf16[16,24,4096]{2,1,0:T(8,128)(2,1)} %bitcast.122), calls=%async_computation.3 | async-start | bytes 6291456 | tf_op jit(solution)/shard_map/all_to_all | solution.py:107
  173.8 5.5 %fusion.8 = f32[384,384]{1,0:T(8,128)} fusion(bf16[384,4096]{1,0:T(8,128)(2,1)} %bitcast.9, bf16[1,4096,384]{2,1,0:T(8,128)(2,1)} %param.15), kind=kOutput, calls=%fused_computation.16 | convolution fusion | flops 1207959552 | bytes 6881280 | tf_op jit(solution)/shard_map/dot_general | solution.py:31
  179.2 8.2 %convolution_convert_fusion = bf16[384,4096]{1,0:T(8,128)(2,1)} fusion(bf16[1,384,4096]{2,1,0:T(8,128)(2,1)} %param.17, bf16[384,4096]{1,0:T(8,128)(2,1)} %bitcast.9, bf16[1,4096,384]{2,1,0:T(8,128)(2,1)S(1)} %copy-done, f32[384,384]{1,0:T(8,128)} %fusion.8), kind=kOutput, calls=%fused_computation.3 | convolution fusion | flops 2418376704 | bytes 13172736 | tf_op jit(solution)/shard_map/dot_general | solution.py:34
  187.4 57.4 %all-to-all-done.3 = bf16[16,24,4096]{2,1,0:T(8,128)(2,1)} async-done(((bf16[16,24,4096]{2,1,0:T(8,128)(2,1)}), bf16[16,24,4096]{2,1,0:T(8,128)(2,1)}, u32[]{:S(2)}, u32[]{:S(2)}) %all-to-all-start.3) | async-done | bytes 3145760 | tf_op jit(solution)/shard_map/all_to_all | solution.py:107
  244.8 5.6 %all-to-all-start.1 = ((bf16[16,24,4096]{2,1,0:T(8,128)(2,1)}), bf16[16,24,4096]{2,1,0:T(8,128)(2,1)}, u32[]{:S(2)}, u32[]{:S(2)}) async-start(bf16[16,24,4096]{2,1,0:T(8,128)(2,1)} %bitcast.125), calls=%async_computation.1 | async-start | bytes 6291456 | tf_op jit(solution)/shard_map/all_to_all | solution.py:100
  250.5 3.6 %bitcast_reduce_fusion = bf16[4,24,4096]{2,1,0:T(8,128)(2,1)} fusion(bf16[16,24,4096]{2,1,0:T(8,128)(2,1)} %all-to-all-done.3), kind=kLoop, calls=%fused_computation.6 | loop fusion | flops 1179648 | bytes 3932160 | tf_op jit(solution)/shard_map/reduce_sum | solution.py:123
  254.0 3.4 gather_fusion.1
  257.5 2.3 fusion.17
  259.7 4.9 %collective-permute-start.1 = (bf16[1,64,4096]{2,1,0:T(8,128)(2,1)}, bf16[1,64,4096]{2,1,0:T(8,128)(2,1)}, u32[]{:S(2)}, u32[]{:S(2)}) collective-permute-start(bf16[1,64,4096]{2,1,0:T(8,128)(2,1)} %fusion.17), channel_id=1, source_target_pairs={{16,0},{32,16},{48,32},{64,48},{80,64},{96,80},{112,96},{128,112},... | collective-permute-start | bytes 1572872 | tf_op jit(solution)/shard_map/ppermute | solution.py:12
  264.7 56.8 %all-to-all-done.1 = bf16[16,24,4096]{2,1,0:T(8,128)(2,1)} async-done(((bf16[16,24,4096]{2,1,0:T(8,128)(2,1)}), bf16[16,24,4096]{2,1,0:T(8,128)(2,1)}, u32[]{:S(2)}, u32[]{:S(2)}) %all-to-all-start.1) | async-done | bytes 3145760 | tf_op jit(solution)/shard_map/all_to_all | solution.py:100
  321.5 3.5 %bitcast_reduce_fusion.1 = bf16[4,24,4096]{2,1,0:T(8,128)(2,1)} fusion(bf16[16,24,4096]{2,1,0:T(8,128)(2,1)} %all-to-all-done.1), kind=kLoop, calls=%fused_computation.7 | loop fusion | flops 1179648 | bytes 3932160 | tf_op jit(solution)/shard_map/reduce_sum | solution.py:116
  325.1 3.4 gather_fusion
  331.2 15.0 %collective-permute-done = bf16[1,64,4096]{2,1,0:T(8,128)(2,1)S(1)} collective-permute-done((bf16[1,64,4096]{2,1,0:T(8,128)(2,1)S(1)}, bf16[1,64,4096]{2,1,0:T(8,128)(2,1)S(1)}, u32[]{:S(2)}, u32[]{:S(2)}) %collective-permute-start) | collective-permute-done | bytes 524320 | tf_op jit(solution)/shard_map/ppermute | solution.py:12
  347.0 1.9 copy.17
  (31 shorter events, 9.8 us)
Async XLA Ops:
  0.6 104.4 %copy-start = (bf16[1,4096,384]{2,1,0:T(8,128)(2,1)S(1)}, bf16[1,4096,384]{2,1,0:T(8,128)(2,1)}, u32[]{:S(2)}) copy-start(bf16[1,4096,384]{2,1,0:T(8,128)(2,1)} %param.16) | copy-start | bytes 9437188
  7.4 10.1 %copy-start.3 = (s32[1,64,1]{1,2,0:T(1,128)S(1)}, s32[1,64,1]{1,2,0:T(1,128)}, u32[]{:S(2)}) copy-start(s32[1,64,1]{1,2,0:T(1,128)} %param.19) | copy-start | bytes 772
  7.4 81.2 %all-to-all-start.2 = ((bf16[16,24,4096]{2,1,0:T(8,128)(2,1)}), bf16[16,24,4096]{2,1,0:T(8,128)(2,1)}, u32[]{:S(2)}, u32[]{:S(2)}) async-start(bf16[16,24,4096]{2,1,0:T(8,128)(2,1)} %bitcast.123), calls=%async_computation.2 | async-start | bytes 6291456 | tf_op jit(solution)/shard_map/all_to_all | solution.py:93
  91.8 76.5 %all-to-all-start = ((bf16[16,24,4096]{2,1,0:T(8,128)(2,1)}), bf16[16,24,4096]{2,1,0:T(8,128)(2,1)}, u32[]{:S(2)}, u32[]{:S(2)}) async-start(bf16[16,24,4096]{2,1,0:T(8,128)(2,1)} %bitcast.124), calls=%async_computation | async-start | bytes 6291456 | tf_op jit(solution)/shard_map/all_to_all | solution.py:92
  98.4 4.8 %copy-start.1 = (bf16[1,4096,384]{2,1,0:T(8,128)(2,1)S(1)}, bf16[1,4096,384]{2,1,0:T(8,128)(2,1)}, u32[]{:S(2)}) copy-start(bf16[1,4096,384]{2,1,0:T(8,128)(2,1)} %param.15) | copy-start | bytes 9437188
  168.3 76.5 %all-to-all-start.3 = ((bf16[16,24,4096]{2,1,0:T(8,128)(2,1)}), bf16[16,24,4096]{2,1,0:T(8,128)(2,1)}, u32[]{:S(2)}, u32[]{:S(2)}) async-start(bf16[16,24,4096]{2,1,0:T(8,128)(2,1)} %bitcast.122), calls=%async_computation.3 | async-start | bytes 6291456 | tf_op jit(solution)/shard_map/all_to_all | solution.py:107
  244.8 5.6 %copy-start.2 = (s32[1,64,1]{1,2,0:T(1,128)S(1)}, s32[1,64,1]{1,2,0:T(1,128)}, u32[]{:S(2)}) copy-start(s32[1,64,1]{1,2,0:T(1,128)} %param.21) | copy-start | bytes 772
  244.8 76.7 %all-to-all-start.1 = ((bf16[16,24,4096]{2,1,0:T(8,128)(2,1)}), bf16[16,24,4096]{2,1,0:T(8,128)(2,1)}, u32[]{:S(2)}, u32[]{:S(2)}) async-start(bf16[16,24,4096]{2,1,0:T(8,128)(2,1)} %bitcast.125), calls=%async_computation.1 | async-start | bytes 6291456 | tf_op jit(solution)/shard_map/all_to_all | solution.py:100
  254.0 3.4 copy-start.4
  259.7 71.5 %collective-permute-start.1 = (bf16[1,64,4096]{2,1,0:T(8,128)(2,1)}, bf16[1,64,4096]{2,1,0:T(8,128)(2,1)}, u32[]{:S(2)}, u32[]{:S(2)}) collective-permute-start(bf16[1,64,4096]{2,1,0:T(8,128)(2,1)} %fusion.17), channel_id=1, source_target_pairs={{16,0},{32,16},{48,32},{64,48},{80,64},{96,80},{112,96},{128,112},... | collective-permute-start | bytes 1572872 | tf_op jit(solution)/shard_map/ppermute | solution.py:12
  325.1 3.4 copy-start.5
  329.9 16.3 %collective-permute-start = (bf16[1,64,4096]{2,1,0:T(8,128)(2,1)S(1)}, bf16[1,64,4096]{2,1,0:T(8,128)(2,1)S(1)}, u32[]{:S(2)}, u32[]{:S(2)}) collective-permute-start(bf16[1,64,4096]{2,1,0:T(8,128)(2,1)S(1)} %fusion.18), channel_id=1, source_target_pairs={{240,0},{0,16},{16,32},{32,48},{48,64},{64,80},{80,96},{96,112},{1... | collective-permute-start | bytes 1572872 | tf_op jit(solution)/shard_map/ppermute | solution.py:12
where the time goes:
time: 350 us; the launch traced here: 349 us
  waiting for transfers between devices  257 us (73%)
  starting transfers between devices  32.8 us (9%)
  matrix products  27.6 us (8%)
  local copies, waits for them, and re-layouts  15.9 us (5%)
  other arithmetic  14.4 us (4%)
    all_to_all x1, waiting for transfers between devices, local(): lax.all_to_all(send_second, 'expert', split_axis=0, concat_axis=0, tiled=...  68.4 us
    all_to_all x1, waiting for transfers between devices, local(): lax.all_to_all(send_first, 'expert', split_axis=0, concat_axis=0, tiled=T...  59.7 us
    all_to_all x1, waiting for transfers between devices, local(): lax.all_to_all(made_second.reshape(devices, capacity, model_width), 'expe...  57.4 us
    all_to_all x1, waiting for transfers between devices, local(): lax.all_to_all(made_first.reshape(devices, capacity, model_width), 'exper...  56.8 us
    ppermute x2, waiting for transfers between devices, passed_along(): return lax.ppermute(block, axis, route)  15 us
    all_to_all x1, starting transfers between devices, local(): lax.all_to_all(send_second, 'expert', split_axis=0, concat_axis=0, tiled=...  10.1 us
    dot_general x1, matrix products, expert_forward(): jnp.dot(hidden, down_rows, preferred_element_type=jnp.float32)  8.16 us
  transfers between devices with their start and end apart: 6, of which 5 were waited for; matrix products, arithmetic and copies ran while one was open for 13% of the time, Pallas kernels for 0%

commit v1 on v0

v1 whole, which is shorter than its diff:
```python
import jax
import jax.numpy as jnp
from jax import lax
from jax.sharding import PartitionSpec as P

REACH = 4


def routes(devices):
    chips = devices // 2

    def near(step, back):
        route = []
        for chip in range(chips):
            origin = (chip + (step if chip % 2 else -step)) % chips
            for core in range(2):
                pair = (2 * origin + core, 2 * chip + core)
                route.append(pair[::-1] if back else pair)
        return route

    across = [(i, i ^ 2) for i in range(devices)]
    beside = [(i, i ^ 1) for i in range(devices)]
    return near, across, beside


def message_of(ids, chip, pairs):
    ahead = (ids - chip // 2) % pairs
    even = jnp.where(ahead == 3, 1, jnp.where(ahead == 1, 2, jnp.where(ahead == 2, 3, 0)))
    odd = jnp.where(ahead == 1, 1, jnp.where(ahead == 3, 2, jnp.where(ahead == 2, 3, 0)))
    return jnp.where(chip % 2 == 0, even, odd)


def places(route_ids, chip, pairs, capacity):
    ids = route_ids.reshape(-1)
    count = ids.shape[0]
    row = lax.broadcasted_iota(jnp.int32, (count, count), 0)
    column = lax.broadcasted_iota(jnp.int32, (count, count), 1)
    earlier = (ids[:, None] == ids[None, :]) & (row < column)
    slot = jnp.sum(earlier.astype(jnp.int32), axis=0)
    return message_of(ids, chip, pairs) * capacity + slot


def placement(slot_at, slot_total):
    rows = lax.broadcasted_iota(jnp.int32, (slot_total, slot_at.shape[0]), 0)
    return (rows == slot_at[None, :]).astype(jnp.bfloat16)


def expert_forward(routed, gate_cols, up_cols, down_rows):
    gate_pre = jnp.dot(routed, gate_cols, preferred_element_type=jnp.float32)
    up_pre = jnp.dot(routed, up_cols, preferred_element_type=jnp.float32)
    hidden = (jax.nn.silu(gate_pre) * up_pre).astype(jnp.bfloat16)
    return jnp.dot(hidden, down_rows, preferred_element_type=jnp.float32).astype(jnp.bfloat16)


def expert_backward(routed, stash_rows, gate_cols, up_cols, down_rows):
    hidden_grad = jnp.dot(routed, down_rows.T, preferred_element_type=jnp.float32)
    gate_pre = stash_rows[:, 0, :].astype(jnp.float32)
    up_pre = stash_rows[:, 1, :].astype(jnp.float32)
    sigmoid_gate = jax.nn.sigmoid(gate_pre)
    grad_gate = (
        hidden_grad * up_pre * sigmoid_gate * (1.0 + gate_pre * (1.0 - sigmoid_gate))
    ).astype(jnp.bfloat16)
    grad_up = (hidden_grad * gate_pre * sigmoid_gate).astype(jnp.bfloat16)
    input_grad = jnp.dot(grad_gate, gate_cols.T, preferred_element_type=jnp.float32)
    input_grad = input_grad + jnp.dot(grad_up, up_cols.T, preferred_element_type=jnp.float32)
    return input_grad.astype(jnp.bfloat16)


def dispatch(rows, capacity, near, across, beside):
    parts = [rows[:capacity]] + [
        lax.ppermute(rows[k * capacity : (k + 1) * capacity], "expert", near(k, False))
        for k in range(1, REACH)
    ]
    close = jnp.concatenate(parts, axis=0)
    distant = lax.ppermute(close, "expert", across)
    half = jnp.concatenate([close, distant], axis=0)
    return jnp.concatenate([half, lax.ppermute(half, "expert", beside)], axis=0)


def collect(made, capacity, near, across, beside):
    half_rows = made.shape[0] // 2
    near_rows = half_rows // 2
    half = made[:half_rows].astype(jnp.float32) + lax.ppermute(
        made[half_rows:], "expert", beside
    ).astype(jnp.float32)
    distant = lax.ppermute(half[near_rows:].astype(jnp.bfloat16), "expert", across)
    close = (half[:near_rows] + distant.astype(jnp.float32)).astype(jnp.bfloat16)
    parts = [close[:capacity]] + [
        lax.ppermute(close[k * capacity : (k + 1) * capacity], "expert", near(k, True))
        for k in range(1, REACH)
    ]
    return jnp.concatenate(parts, axis=0)


def combine(placed, back, gate_values):
    picked = lax.dot_general(
        placed, back, (((0,), (0,)), ((), ())), preferred_element_type=jnp.float32
    )
    return picked * gate_values


def local(
    layer_input,
    cotangent,
    gate_weight,
    up_weight,
    down_weight,
    stashed_pre,
    first_ids,
    first_gates,
    second_ids,
    second_gates,
    keep_mask,
):
    devices = lax.axis_size("expert")
    sections = lax.axis_size("section")
    chips = devices // 2
    pairs = chips // 2
    capacity = stashed_pre.shape[2]
    slots = pairs * capacity
    hidden_local = gate_weight.shape[2]
    near, across, beside = routes(devices)
    me = lax.axis_index("expert")
    chip, core = me // 2, me % 2
    tokens_in = layer_input[0]
    keep_rows = keep_mask[0]
    kept_grads = cotangent[0] * keep_rows[:, None].astype(jnp.bfloat16)
    first_placed = placement(places(first_ids[0], chip, pairs, capacity), slots)
    second_placed = placement(places(second_ids[0], chip, pairs, capacity), slots)
    first_rows = jnp.dot(first_placed, tokens_in, preferred_element_type=jnp.float32).astype(
        jnp.bfloat16
    )
    second_rows = jnp.dot(second_placed, kept_grads, preferred_element_type=jnp.float32).astype(
        jnp.bfloat16
    )
    order = []
    for which in (core, 1 - core):
        for here in (chip, chip ^ 1):
            for step in range(REACH):
                origin = (here + jnp.where(here % 2 == 0, -step, step)) % chips
                order.append(2 * origin + which)
    stash_local = jnp.concatenate(
        [lax.dynamic_index_in_dim(stashed_pre[0], block, 0, False) for block in order]
    )
    gate_cols = gate_weight[0]
    up_cols = up_weight[0]
    down_rows = down_weight[0]

    held_second = dispatch(second_rows, capacity, near, across, beside)
    held_first = dispatch(first_rows, capacity, near, across, beside)
    made_second = expert_backward(held_second, stash_local, gate_cols, up_cols, down_rows)
    made_first = expert_forward(held_first, gate_cols, up_cols, down_rows)
    back_second = collect(made_second, capacity, near, across, beside)
    back_first = collect(made_first, capacity, near, across, beside)
    first_branch = combine(first_placed, back_first, first_gates[0])
    second_branch = combine(second_placed, back_second, second_gates[0])
    mixed_out = (tokens_in.astype(jnp.float32) + first_branch).astype(jnp.bfloat16)
    keep_float = keep_rows[:, None].astype(jnp.float32)
    grad_out = (keep_float * (cotangent[0].astype(jnp.float32) + second_branch)).astype(
        jnp.bfloat16
    )
    onward = [(i, (i + 1) % sections) for i in range(sections)]
    backward = [((i + 1) % sections, i) for i in range(sections)]
    moved_back = lax.ppermute(grad_out[None], "section", backward)
    moved_on = lax.ppermute(mixed_out[None], "section", onward)
    return (moved_on, moved_back)


def solution(mesh):
    placed = (
        P("section", "expert", None),
        P("section", "expert", None),
        P("section", None, "expert"),
        P("section", None, "expert"),
        P("section", "expert", None),
        P("section", None, None, None, "expert"),
        P("section", "expert", None),
        P("section", "expert", None),
        P("section", "expert", None),
        P("section", "expert", None),
        P("section", "expert"),
    )
    return jax.shard_map(
        local,
        mesh=mesh,
        in_specs=placed,
        out_specs=(P("section", "expert", None), P("section", "expert", None)),
        check_vma=False,
    )
```

time: 350 us -> 187 us (0.53)
  waiting for transfers between devices: 257 us -> 96.3 us
  starting transfers between devices: 32.8 us -> 45.2 us
  other arithmetic: 14.4 us -> 4.27 us
  matrix products: 27.6 us -> 18.9 us
  local copies, waits for them, and re-layouts: 15.9 us -> 20.1 us
    all_to_all x4 -> x0, waiting for transfers between devices: 242 us -> none  [the longest x1 68.4 us: local(): lax.all_to_all(send_second, 'expert', split_axis=0, concat_axis=0, tiled=...]
    ppermute x2 -> x22, waiting for transfers between devices: 15 us -> 96.3 us  [the longest x2 34.5 us: collect(): lax.ppermute(half[near_rows:].astype(jnp.bfloat16), 'expert', across)]
    ppermute x2 -> x22, starting transfers between devices: 6.22 us -> 45.2 us  [the longest x6 13.1 us: collect(): lax.ppermute(close[k * capacity:(k + 1) * capacity], 'expert', near(k, Tr...]
    all_to_all x4 -> x0, starting transfers between devices: 26.6 us -> none  [the longest x1 10.1 us: local(): lax.all_to_all(send_second, 'expert', split_axis=0, concat_axis=0, tiled=...]
    unnamed x15 -> x65, local copies, waits for them, and re-layouts: 3.83 us -> 13.1 us
    reduce_sum x4 -> x2, other arithmetic: 8.11 us -> 1.01 us  [places(): slot = jnp.sum(earlier.astype(jnp.int32), axis=0)]
    gather x2 -> x0, local copies, waits for them, and re-layouts: 6.82 us -> none  [gather_back(): picked = jnp.take(summed, slot_at, axis=0).astype(jnp.float32)]
    broadcast_in_dim x2 -> x0, local copies, waits for them, and re-layouts: 5.24 us -> none  [the longest x1 3.19 us: local(): jnp.repeat(first_rows.reshape(experts, capacity, model_width), SHARDS, ax...]
  transfers between devices with their start and end apart: 6 -> 22, of which waited for: 5 -> 12; matrix products, arithmetic and copies ran while one was open for 13% -> 18% of each run, Pallas kernels for 0% -> 0%
where the time goes in v1:
time: 187 us; the launch traced here: 186 us
  waiting for transfers between devices  96.3 us (51%)
  starting transfers between devices  45.2 us (24%)
  local copies, waits for them, and re-layouts  20.1 us (11%)
  matrix products  18.9 us (10%)
  other arithmetic  4.27 us (2%)
    ppermute x2, waiting for transfers between devices, collect(): lax.ppermute(half[near_rows:].astype(jnp.bfloat16), 'expert', across)  34.5 us
    ppermute x6, waiting for transfers between devices, dispatch(): lax.ppermute(rows[k * capacity:(k + 1) * capacity], 'expert', near(k, Fal...  19.6 us
    ppermute x2, waiting for transfers between devices, dispatch(): distant = lax.ppermute(close, 'expert', across)  18.1 us
    ppermute x6, waiting for transfers between devices, collect(): lax.ppermute(close[k * capacity:(k + 1) * capacity], 'expert', near(k, Tr...  13.7 us
    unnamed x65, local copies, waits for them, and re-layouts  13.1 us
    ppermute x6, starting transfers between devices, collect(): lax.ppermute(close[k * capacity:(k + 1) * capacity], 'expert', near(k, Tr...  13.1 us
    ppermute x6, starting transfers between devices, dispatch(): lax.ppermute(rows[k * capacity:(k + 1) * capacity], 'expert', near(k, Fal...  12.5 us
    ppermute x1, waiting for transfers between devices, local(): moved_back = lax.ppermute(grad_out[None], 'section', backward)  10.3 us
  transfers between devices with their start and end apart: 22, of which 12 were waited for; matrix products, arithmetic and copies ran while one was open for 18% of the time, Pallas kernels for 0%

profile of v1, /device:TPU:1, one launch (start us, length us, event | category | flops | bytes accessed | tf_op | source)
XLA Modules:
  0.0 185.8 jit_solution(2863975292536385707)
XLA Ops:
  4.8 6.4 %collective-permute-start = (bf16[24,4096]{1,0:T(8,128)(2,1)}, bf16[24,4096]{1,0:T(8,128)(2,1)}, u32[]{:S(2)}, u32[]{:S(2)}) collective-permute-start(bf16[24,4096]{1,0:T(8,128)(2,1)} %get-tuple-element.24), channel_id=1, source_target_pairs={{14,0},{15,1},{4,2},{5,3},{2,4},{3,5},{8,6},{9,7},{6,8},{7,9},{12,... | collective-permute-start | bytes 589832 | tf_op jit(solution)/shard_map/ppermute | solution.py:71
  11.3 4.0 %collective-permute-start.2 = (bf16[24,4096]{1,0:T(8,128)(2,1)}, bf16[24,4096]{1,0:T(8,128)(2,1)}, u32[]{:S(2)}, u32[]{:S(2)}) collective-permute-start(bf16[24,4096]{1,0:T(8,128)(2,1)} %get-tuple-element.22), channel_id=1, source_target_pairs={{10,0},{11,1},{8,2},{9,3},{14,4},{15,5},{12,6},{13,7},{2,8},{3,9},... | collective-permute-start | bytes 589832 | tf_op jit(solution)/shard_map/ppermute | solution.py:71
  23.0 9.1 %collective-permute-done.2 = bf16[24,4096]{1,0:T(8,128)(2,1)} collective-permute-done((bf16[24,4096]{1,0:T(8,128)(2,1)}, bf16[24,4096]{1,0:T(8,128)(2,1)}, u32[]{:S(2)}, u32[]{:S(2)}) %collective-permute-start.2) | collective-permute-done | bytes 196640 | tf_op jit(solution)/shard_map/ppermute | solution.py:71
  33.4 3.0 %collective-permute-start.3 = (bf16[96,4096]{1,0:T(8,128)(2,1)S(1)}, bf16[96,4096]{1,0:T(8,128)(2,1)S(1)}, u32[]{:S(2)}, u32[]{:S(2)}) collective-permute-start(bf16[96,4096]{1,0:T(8,128)(2,1)S(1)} %pad_maximum_fusion), channel_id=1, source_target_pairs={{0,2},{1,3},{2,0},{3,1},{4,6},{5,7},{6,4},{7,5},{8,10},{9,11},{10,... | collective-permute-start | bytes 2359304 | tf_op jit(solution)/shard_map/ppermute | solution.py:75
  36.4 4.0 %collective-permute-done.11 = bf16[24,4096]{1,0:T(8,128)(2,1)S(1)} collective-permute-done((bf16[24,4096]{1,0:T(8,128)(2,1)}, bf16[24,4096]{1,0:T(8,128)(2,1)S(1)}, u32[]{:S(2)}, u32[]{:S(2)}) %collective-permute-start.11) | collective-permute-done | bytes 196640 | tf_op jit(solution)/shard_map/ppermute | solution.py:71
  40.4 4.4 %collective-permute-done.13 = bf16[24,4096]{1,0:T(8,128)(2,1)S(1)} collective-permute-done((bf16[24,4096]{1,0:T(8,128)(2,1)}, bf16[24,4096]{1,0:T(8,128)(2,1)S(1)}, u32[]{:S(2)}, u32[]{:S(2)}) %collective-permute-start.13) | collective-permute-done | bytes 196640 | tf_op jit(solution)/shard_map/ppermute | solution.py:71
  44.8 2.9 %collective-permute-start.14 = (bf16[96,4096]{1,0:T(8,128)(2,1)S(1)}, bf16[96,4096]{1,0:T(8,128)(2,1)S(1)}, u32[]{:S(2)}, u32[]{:S(2)}) collective-permute-start(bf16[96,4096]{1,0:T(8,128)(2,1)S(1)} %pad_maximum_fusion.1), channel_id=1, source_target_pairs={{0,2},{1,3},{2,0},{3,1},{4,6},{5,7},{6,4},{7,5},{8,10},{9,11},{10,... | collective-permute-start | bytes 2359304 | tf_op jit(solution)/shard_map/ppermute | solution.py:75
  50.6 6.2 %collective-permute-done.3 = bf16[96,4096]{1,0:T(8,128)(2,1)S(1)} collective-permute-done((bf16[96,4096]{1,0:T(8,128)(2,1)S(1)}, bf16[96,4096]{1,0:T(8,128)(2,1)S(1)}, u32[]{:S(2)}, u32[]{:S(2)}) %collective-permute-start.3) | collective-permute-done | bytes 786464 | tf_op jit(solution)/shard_map/ppermute | solution.py:75
  57.0 2.4 %collective-permute-start.4 = (bf16[192,4096]{1,0:T(8,128)(2,1)S(1)}, bf16[192,4096]{1,0:T(8,128)(2,1)S(1)}, u32[]{:S(2)}, u32[]{:S(2)}) collective-permute-start(bf16[192,4096]{1,0:T(8,128)(2,1)S(1)} %get-tuple-element.18), channel_id=1, source_target_pairs={{0,1},{1,0},{2,3},{3,2},{4,5},{5,4},{6,7},{7,6},{8,9},{9,8},{10,11... | collective-permute-start | bytes 4718600 | tf_op jit(solution)/shard_map/ppermute | solution.py:77
  61.7 11.9 %collective-permute-done.14 = bf16[96,4096]{1,0:T(8,128)(2,1)S(1)} collective-permute-done((bf16[96,4096]{1,0:T(8,128)(2,1)S(1)}, bf16[96,4096]{1,0:T(8,128)(2,1)S(1)}, u32[]{:S(2)}, u32[]{:S(2)}) %collective-permute-start.14) | collective-permute-done | bytes 786464 | tf_op jit(solution)/shard_map/ppermute | solution.py:75
  78.3 2.6 %fusion.11 = f32[384,384]{1,0:T(8,128)} fusion(bf16[384,4096]{1,0:T(8,128)(2,1)S(1)} %constant_dynamic-update-slice_fusion.5, bf16[1,4096,384]{2,1,0:T(8,128)(2,1)S(1)} %copy-done.3), kind=kOutput, calls=%fused_computation.17 | convolution fusion | flops 1207959552 | bytes 6881280 | tf_op jit(solution)/shard_map/dot_general | solution.py:50
  80.9 8.2 %convolution_convert_fusion = bf16[384,4096]{1,0:T(8,128)(2,1)} fusion(bf16[1,384,4096]{2,1,0:T(8,128)(2,1)} %param.15, f32[384,384]{1,0:T(8,128)} %fusion.11, bf16[384,4096]{1,0:T(8,128)(2,1)} %copy-done.14, bf16[1,4096,384]{2,1,0:T(8,128)(2,1)S(1)} %copy-done), kind=kOutput, calls=%fused_computation.1 | convolution fusion | flops 2418376704 | bytes 13172736 | tf_op jit(solution)/shard_map/dot_general | solution.py:52
  101.0 2.3 %collective-permute-start.6 = (bf16[96,4096]{1,0:T(8,128)(2,1)S(1)}, bf16[96,4096]{1,0:T(8,128)(2,1)S(1)}, u32[]{:S(2)}, u32[]{:S(2)}) collective-permute-start(bf16[96,4096]{1,0:T(8,128)(2,1)S(1)} %slice.158), channel_id=1, source_target_pairs={{0,2},{1,3},{2,0},{3,1},{4,6},{5,7},{6,4},{7,5},{8,10},{9,11},{10,... | collective-permute-start | bytes 2359304 | tf_op jit(solution)/shard_map/ppermute | solution.py:86
  105.1 16.1 %collective-permute-done.6 = bf16[96,4096]{1,0:T(8,128)(2,1)S(1)} collective-permute-done((bf16[96,4096]{1,0:T(8,128)(2,1)S(1)}, bf16[96,4096]{1,0:T(8,128)(2,1)S(1)}, u32[]{:S(2)}, u32[]{:S(2)}) %collective-permute-start.6) | collective-permute-done | bytes 786464 | tf_op jit(solution)/shard_map/ppermute | solution.py:86
  121.5 4.0 %collective-permute-start.9 = (bf16[24,4096]{1,0:T(8,128)(2,1)S(1)}, bf16[24,4096]{1,0:T(8,128)(2,1)S(1)}, u32[]{:S(2)}, u32[]{:S(2)}) collective-permute-start(bf16[24,4096]{1,0:T(8,128)(2,1)S(1)} %get-tuple-element.15), channel_id=1, source_target_pairs={{0,10},{1,11},{2,8},{3,9},{4,14},{5,15},{6,12},{7,13},{8,2},{9,3},... | collective-permute-start | bytes 589832 | tf_op jit(solution)/shard_map/ppermute | solution.py:89
  125.8 2.3 %collective-permute-start.7 = (bf16[24,4096]{1,0:T(8,128)(2,1)S(1)}, bf16[24,4096]{1,0:T(8,128)(2,1)S(1)}, u32[]{:S(2)}, u32[]{:S(2)}) collective-permute-start(bf16[24,4096]{1,0:T(8,128)(2,1)S(1)} %get-tuple-element.17), channel_id=1, source_target_pairs={{0,14},{1,15},{2,4},{3,5},{4,2},{5,3},{6,8},{7,9},{8,6},{9,7},{10,... | collective-permute-start | bytes 589832 | tf_op jit(solution)/shard_map/ppermute | solution.py:89
  128.1 18.4 %collective-permute-done.17 = bf16[96,4096]{1,0:T(8,128)(2,1)S(1)} collective-permute-done((bf16[96,4096]{1,0:T(8,128)(2,1)S(1)}, bf16[96,4096]{1,0:T(8,128)(2,1)S(1)}, u32[]{:S(2)}, u32[]{:S(2)}) %collective-permute-start.17) | collective-permute-done | bytes 786464 | tf_op jit(solution)/shard_map/ppermute | solution.py:86
  146.8 3.8 %collective-permute-start.20 = (bf16[24,4096]{1,0:T(8,128)(2,1)S(1)}, bf16[24,4096]{1,0:T(8,128)(2,1)S(1)}, u32[]{:S(2)}, u32[]{:S(2)}) collective-permute-start(bf16[24,4096]{1,0:T(8,128)(2,1)S(1)} %get-tuple-element.3), channel_id=1, source_target_pairs={{0,10},{1,11},{2,8},{3,9},{4,14},{5,15},{6,12},{7,13},{8,2},{9,3},... | collective-permute-start | bytes 589832 | tf_op jit(solution)/shard_map/ppermute | solution.py:89
  150.9 2.3 %collective-permute-start.18 = (bf16[24,4096]{1,0:T(8,128)(2,1)S(1)}, bf16[24,4096]{1,0:T(8,128)(2,1)S(1)}, u32[]{:S(2)}, u32[]{:S(2)}) collective-permute-start(bf16[24,4096]{1,0:T(8,128)(2,1)S(1)} %get-tuple-element.5), channel_id=1, source_target_pairs={{0,14},{1,15},{2,4},{3,5},{4,2},{5,3},{6,8},{7,9},{8,6},{9,7},{10,... | collective-permute-start | bytes 589832 | tf_op jit(solution)/shard_map/ppermute | solution.py:89
  154.9 3.9 %collective-permute-done.20 = bf16[24,4096]{1,0:T(8,128)(2,1)S(1)} collective-permute-done((bf16[24,4096]{1,0:T(8,128)(2,1)S(1)}, bf16[24,4096]{1,0:T(8,128)(2,1)S(1)}, u32[]{:S(2)}, u32[]{:S(2)}) %collective-permute-start.20) | collective-permute-done | bytes 196640 | tf_op jit(solution)/shard_map/ppermute | solution.py:89
  158.8 5.2 %collective-permute-done.19 = bf16[24,4096]{1,0:T(8,128)(2,1)S(1)} collective-permute-done((bf16[24,4096]{1,0:T(8,128)(2,1)S(1)}, bf16[24,4096]{1,0:T(8,128)(2,1)S(1)}, u32[]{:S(2)}, u32[]{:S(2)}) %collective-permute-start.19) | collective-permute-done | bytes 196640 | tf_op jit(solution)/shard_map/ppermute | solution.py:89
  164.1 4.5 %collective-permute-done.18 = bf16[24,4096]{1,0:T(8,128)(2,1)S(1)} collective-permute-done((bf16[24,4096]{1,0:T(8,128)(2,1)S(1)}, bf16[24,4096]{1,0:T(8,128)(2,1)S(1)}, u32[]{:S(2)}, u32[]{:S(2)}) %collective-permute-start.18) | collective-permute-done | bytes 196640 | tf_op jit(solution)/shard_map/ppermute | solution.py:89
  169.0 5.0 %collective-permute-start.21 = (bf16[1,64,4096]{2,1,0:T(8,128)(2,1)S(1)}, bf16[1,64,4096]{2,1,0:T(8,128)(2,1)S(1)}, u32[]{:S(2)}, u32[]{:S(2)}) collective-permute-start(bf16[1,64,4096]{2,1,0:T(8,128)(2,1)S(1)} %fusion.5), channel_id=1, source_target_pairs={{16,0},{32,16},{48,32},{64,48},{80,64},{96,80},{112,96},{128,112},... | collective-permute-start | bytes 1572872 | tf_op jit(solution)/shard_map/ppermute | solution.py:164
  173.9 10.3 %collective-permute-done.21 = bf16[1,64,4096]{2,1,0:T(8,128)(2,1)S(1)} collective-permute-done((bf16[1,64,4096]{2,1,0:T(8,128)(2,1)S(1)}, bf16[1,64,4096]{2,1,0:T(8,128)(2,1)S(1)}, u32[]{:S(2)}, u32[]{:S(2)}) %collective-permute-start.21) | collective-permute-done | bytes 524320 | tf_op jit(solution)/shard_map/ppermute | solution.py:164
  (117 shorter events, 41.3 us)
Async XLA Ops:
  0.6 80.2 %copy-start = (bf16[1,4096,384]{2,1,0:T(8,128)(2,1)S(1)}, bf16[1,4096,384]{2,1,0:T(8,128)(2,1)}, u32[]{:S(2)}) copy-start(bf16[1,4096,384]{2,1,0:T(8,128)(2,1)} %param.13) | copy-start | bytes 9437188
  4.8 16.8 %collective-permute-start = (bf16[24,4096]{1,0:T(8,128)(2,1)}, bf16[24,4096]{1,0:T(8,128)(2,1)}, u32[]{:S(2)}, u32[]{:S(2)}) collective-permute-start(bf16[24,4096]{1,0:T(8,128)(2,1)} %get-tuple-element.24), channel_id=1, source_target_pairs={{14,0},{15,1},{4,2},{5,3},{2,4},{3,5},{8,6},{9,7},{6,8},{7,9},{12,... | collective-permute-start | bytes 589832 | tf_op jit(solution)/shard_map/ppermute | solution.py:71
  11.2 11.7 %collective-permute-start.1 = (bf16[24,4096]{1,0:T(8,128)(2,1)}, bf16[24,4096]{1,0:T(8,128)(2,1)}, u32[]{:S(2)}, u32[]{:S(2)}) collective-permute-start(bf16[24,4096]{1,0:T(8,128)(2,1)} %get-tuple-element.23), channel_id=1, source_target_pairs={{12,0},{13,1},{6,2},{7,3},{0,4},{1,5},{10,6},{11,7},{4,8},{5,9},{1... | collective-permute-start | bytes 589832 | tf_op jit(solution)/shard_map/ppermute | solution.py:71
  11.3 20.9 %collective-permute-start.2 = (bf16[24,4096]{1,0:T(8,128)(2,1)}, bf16[24,4096]{1,0:T(8,128)(2,1)}, u32[]{:S(2)}, u32[]{:S(2)}) collective-permute-start(bf16[24,4096]{1,0:T(8,128)(2,1)} %get-tuple-element.22), channel_id=1, source_target_pairs={{10,0},{11,1},{8,2},{9,3},{14,4},{15,5},{12,6},{13,7},{2,8},{3,9},... | collective-permute-start | bytes 589832 | tf_op jit(solution)/shard_map/ppermute | solution.py:71
  16.9 23.5 %collective-permute-start.11 = (bf16[24,4096]{1,0:T(8,128)(2,1)}, bf16[24,4096]{1,0:T(8,128)(2,1)S(1)}, u32[]{:S(2)}, u32[]{:S(2)}) collective-permute-start(bf16[24,4096]{1,0:T(8,128)(2,1)} %get-tuple-element.12), channel_id=1, source_target_pairs={{14,0},{15,1},{4,2},{5,3},{2,4},{3,5},{8,6},{9,7},{6,8},{7,9},{12,... | collective-permute-start | bytes 589832 | tf_op jit(solution)/shard_map/ppermute | solution.py:71
  16.9 23.5 %collective-permute-start.12 = (bf16[24,4096]{1,0:T(8,128)(2,1)}, bf16[24,4096]{1,0:T(8,128)(2,1)S(1)}, u32[]{:S(2)}, u32[]{:S(2)}) collective-permute-start(bf16[24,4096]{1,0:T(8,128)(2,1)} %get-tuple-element.11), channel_id=1, source_target_pairs={{12,0},{13,1},{6,2},{7,3},{0,4},{1,5},{10,6},{11,7},{4,8},{5,9},{1... | collective-permute-start | bytes 589832 | tf_op jit(solution)/shard_map/ppermute | solution.py:71
  21.6 23.1 %collective-permute-start.13 = (bf16[24,4096]{1,0:T(8,128)(2,1)}, bf16[24,4096]{1,0:T(8,128)(2,1)S(1)}, u32[]{:S(2)}, u32[]{:S(2)}) collective-permute-start(bf16[24,4096]{1,0:T(8,128)(2,1)} %get-tuple-element.10), channel_id=1, source_target_pairs={{10,0},{11,1},{8,2},{9,3},{14,4},{15,5},{12,6},{13,7},{2,8},{3,9},... | collective-permute-start | bytes 589832 | tf_op jit(solution)/shard_map/ppermute | solution.py:71
  33.4 23.4 %collective-permute-start.3 = (bf16[96,4096]{1,0:T(8,128)(2,1)S(1)}, bf16[96,4096]{1,0:T(8,128)(2,1)S(1)}, u32[]{:S(2)}, u32[]{:S(2)}) collective-permute-start(bf16[96,4096]{1,0:T(8,128)(2,1)S(1)} %pad_maximum_fusion), channel_id=1, source_target_pairs={{0,2},{1,3},{2,0},{3,1},{4,6},{5,7},{6,4},{7,5},{8,10},{9,11},{10,... | collective-permute-start | bytes 2359304 | tf_op jit(solution)/shard_map/ppermute | solution.py:75
  44.8 28.8 %collective-permute-start.14 = (bf16[96,4096]{1,0:T(8,128)(2,1)S(1)}, bf16[96,4096]{1,0:T(8,128)(2,1)S(1)}, u32[]{:S(2)}, u32[]{:S(2)}) collective-permute-start(bf16[96,4096]{1,0:T(8,128)(2,1)S(1)} %pad_maximum_fusion.1), channel_id=1, source_target_pairs={{0,2},{1,3},{2,0},{3,1},{4,6},{5,7},{6,4},{7,5},{8,10},{9,11},{10,... | collective-permute-start | bytes 2359304 | tf_op jit(solution)/shard_map/ppermute | solution.py:75
  57.0 19.4 %collective-permute-start.4 = (bf16[192,4096]{1,0:T(8,128)(2,1)S(1)}, bf16[192,4096]{1,0:T(8,128)(2,1)S(1)}, u32[]{:S(2)}, u32[]{:S(2)}) collective-permute-start(bf16[192,4096]{1,0:T(8,128)(2,1)S(1)} %get-tuple-element.18), channel_id=1, source_target_pairs={{0,1},{1,0},{2,3},{3,2},{4,5},{5,4},{6,7},{7,6},{8,9},{9,8},{10,11... | collective-permute-start | bytes 4718600 | tf_op jit(solution)/shard_map/ppermute | solution.py:77
  75.0 15.8 %collective-permute-start.15 = (bf16[192,4096]{1,0:T(8,128)(2,1)}, bf16[192,4096]{1,0:T(8,128)(2,1)}, u32[]{:S(2)}, u32[]{:S(2)}) collective-permute-start(bf16[192,4096]{1,0:T(8,128)(2,1)} %get-tuple-element.6), channel_id=1, source_target_pairs={{0,1},{1,0},{2,3},{3,2},{4,5},{5,4},{6,7},{7,6},{8,9},{9,8},{10,11... | collective-permute-start | bytes 4718600 | tf_op jit(solution)/shard_map/ppermute | solution.py:77
  90.8 8.1 %collective-permute-start.5 = (bf16[192,4096]{1,0:T(8,128)(2,1)S(1)}, bf16[192,4096]{1,0:T(8,128)(2,1)S(1)}, u32[]{:S(2)}, u32[]{:S(2)}) collective-permute-start(bf16[192,4096]{1,0:T(8,128)(2,1)S(1)} %slice.111), channel_id=1, source_target_pairs={{0,1},{1,0},{2,3},{3,2},{4,5},{5,4},{6,7},{7,6},{8,9},{9,8},{10,11... | collective-permute-start | bytes 4718600 | tf_op jit(solution)/shard_map/ppermute | solution.py:83
  98.7 4.6 %collective-permute-start.16 = (bf16[192,4096]{1,0:T(8,128)(2,1)S(1)}, bf16[192,4096]{1,0:T(8,128)(2,1)S(1)}, u32[]{:S(2)}, u32[]{:S(2)}) collective-permute-start(bf16[192,4096]{1,0:T(8,128)(2,1)S(1)} %slice.125), channel_id=1, source_target_pairs={{0,1},{1,0},{2,3},{3,2},{4,5},{5,4},{6,7},{7,6},{8,9},{9,8},{10,11... | collective-permute-start | bytes 4718600 | tf_op jit(solution)/shard_map/ppermute | solution.py:83
  101.0 20.2 %collective-permute-start.6 = (bf16[96,4096]{1,0:T(8,128)(2,1)S(1)}, bf16[96,4096]{1,0:T(8,128)(2,1)S(1)}, u32[]{:S(2)}, u32[]{:S(2)}) collective-permute-start(bf16[96,4096]{1,0:T(8,128)(2,1)S(1)} %slice.158), channel_id=1, source_target_pairs={{0,2},{1,3},{2,0},{3,1},{4,6},{5,7},{6,4},{7,5},{8,10},{9,11},{10,... | collective-permute-start | bytes 2359304 | tf_op jit(solution)/shard_map/ppermute | solution.py:86
  103.8 42.7 %collective-permute-start.17 = (bf16[96,4096]{1,0:T(8,128)(2,1)S(1)}, bf16[96,4096]{1,0:T(8,128)(2,1)S(1)}, u32[]{:S(2)}, u32[]{:S(2)}) collective-permute-start(bf16[96,4096]{1,0:T(8,128)(2,1)S(1)} %slice.157), channel_id=1, source_target_pairs={{0,2},{1,3},{2,0},{3,1},{4,6},{5,7},{6,4},{7,5},{8,10},{9,11},{10,... | collective-permute-start | bytes 2359304 | tf_op jit(solution)/shard_map/ppermute | solution.py:86
  121.5 29.4 %collective-permute-start.9 = (bf16[24,4096]{1,0:T(8,128)(2,1)S(1)}, bf16[24,4096]{1,0:T(8,128)(2,1)S(1)}, u32[]{:S(2)}, u32[]{:S(2)}) collective-permute-start(bf16[24,4096]{1,0:T(8,128)(2,1)S(1)} %get-tuple-element.15), channel_id=1, source_target_pairs={{0,10},{1,11},{2,8},{3,9},{4,14},{5,15},{6,12},{7,13},{8,2},{9,3},... | collective-permute-start | bytes 589832 | tf_op jit(solution)/shard_map/ppermute | solution.py:89
  125.5 27.7 %collective-permute-start.8 = (bf16[24,4096]{1,0:T(8,128)(2,1)S(1)}, bf16[24,4096]{1,0:T(8,128)(2,1)S(1)}, u32[]{:S(2)}, u32[]{:S(2)}) collective-permute-start(bf16[24,4096]{1,0:T(8,128)(2,1)S(1)} %get-tuple-element.16), channel_id=1, source_target_pairs={{0,12},{1,13},{2,6},{3,7},{4,0},{5,1},{6,10},{7,11},{8,4},{9,5},{1... | collective-permute-start | bytes 589832 | tf_op jit(solution)/shard_map/ppermute | solution.py:89
  125.8 27.4 %collective-permute-start.7 = (bf16[24,4096]{1,0:T(8,128)(2,1)S(1)}, bf16[24,4096]{1,0:T(8,128)(2,1)S(1)}, u32[]{:S(2)}, u32[]{:S(2)}) collective-permute-start(bf16[24,4096]{1,0:T(8,128)(2,1)S(1)} %get-tuple-element.17), channel_id=1, source_target_pairs={{0,14},{1,15},{2,4},{3,5},{4,2},{5,3},{6,8},{7,9},{8,6},{9,7},{10,... | collective-permute-start | bytes 589832 | tf_op jit(solution)/shard_map/ppermute | solution.py:89
  146.8 12.0 %collective-permute-start.20 = (bf16[24,4096]{1,0:T(8,128)(2,1)S(1)}, bf16[24,4096]{1,0:T(8,128)(2,1)S(1)}, u32[]{:S(2)}, u32[]{:S(2)}) collective-permute-start(bf16[24,4096]{1,0:T(8,128)(2,1)S(1)} %get-tuple-element.3), channel_id=1, source_target_pairs={{0,10},{1,11},{2,8},{3,9},{4,14},{5,15},{6,12},{7,13},{8,2},{9,3},... | collective-permute-start | bytes 589832 | tf_op jit(solution)/shard_map/ppermute | solution.py:89
  150.6 13.5 %collective-permute-start.19 = (bf16[24,4096]{1,0:T(8,128)(2,1)S(1)}, bf16[24,4096]{1,0:T(8,128)(2,1)S(1)}, u32[]{:S(2)}, u32[]{:S(2)}) collective-permute-start(bf16[24,4096]{1,0:T(8,128)(2,1)S(1)} %get-tuple-element.4), channel_id=1, source_target_pairs={{0,12},{1,13},{2,6},{3,7},{4,0},{5,1},{6,10},{7,11},{8,4},{9,5},{1... | collective-permute-start | bytes 589832 | tf_op jit(solution)/shard_map/ppermute | solution.py:89
  150.9 17.7 %collective-permute-start.18 = (bf16[24,4096]{1,0:T(8,128)(2,1)S(1)}, bf16[24,4096]{1,0:T(8,128)(2,1)S(1)}, u32[]{:S(2)}, u32[]{:S(2)}) collective-permute-start(bf16[24,4096]{1,0:T(8,128)(2,1)S(1)} %get-tuple-element.5), channel_id=1, source_target_pairs={{0,14},{1,15},{2,4},{3,5},{4,2},{5,3},{6,8},{7,9},{8,6},{9,7},{10,... | collective-permute-start | bytes 589832 | tf_op jit(solution)/shard_map/ppermute | solution.py:89
  153.2 32.6 %copy-start.1 = (bf16[1,4096,384]{2,1,0:T(8,128)(2,1)S(1)}, bf16[1,4096,384]{2,1,0:T(8,128)(2,1)}, u32[]{:S(2)}) copy-start(bf16[1,4096,384]{2,1,0:T(8,128)(2,1)} %param.13) | copy-start | bytes 9437188
  153.6 20.3 %collective-permute-start.10 = (bf16[1,64,4096]{2,1,0:T(8,128)(2,1)S(1)}, bf16[1,64,4096]{2,1,0:T(8,128)(2,1)S(1)}, u32[]{:S(2)}, u32[]{:S(2)}) collective-permute-start(bf16[1,64,4096]{2,1,0:T(8,128)(2,1)S(1)} %fusion.6), channel_id=1, source_target_pairs={{0,16},{16,32},{32,48},{48,64},{64,80},{80,96},{96,112},{112,128},... | collective-permute-start | bytes 1572872 | tf_op jit(solution)/shard_map/ppermute | solution.py:165
  169.0 15.3 %collective-permute-start.21 = (bf16[1,64,4096]{2,1,0:T(8,128)(2,1)S(1)}, bf16[1,64,4096]{2,1,0:T(8,128)(2,1)S(1)}, u32[]{:S(2)}, u32[]{:S(2)}) collective-permute-start(bf16[1,64,4096]{2,1,0:T(8,128)(2,1)S(1)} %fusion.5), channel_id=1, source_target_pairs={{16,0},{32,16},{48,32},{64,48},{80,64},{96,80},{112,96},{128,112},... | collective-permute-start | bytes 1572872 | tf_op jit(solution)/shard_map/ppermute | solution.py:164
  (18 other events, 281.1 us)

commit v2 on v1

v2 whole, which is shorter than its diff:
```python
import jax
import jax.numpy as jnp
from jax import lax
from jax.sharding import PartitionSpec as P

REACH = 4


def routes(devices, sections):
    chips = devices // 2

    def nearer(step):
        for chip in range(chips):
            origin = (chip + (step if chip % 2 else -step)) % chips
            for core in range(2):
                yield 2 * origin + core, 2 * chip + core

    def out(step):
        return list(nearer(step))

    def home(step, onward):
        return [
            (s * devices + there, (s + onward) % sections * devices + origin)
            for s in range(sections)
            for origin, there in nearer(step)
        ]

    across = [(i, i ^ 2) for i in range(devices)]
    beside = [(i, i ^ 1) for i in range(devices)]
    return out, home, across, beside


def message_of(ids, chip, pairs):
    ahead = (ids - chip // 2) % pairs
    even = jnp.where(ahead == 3, 1, jnp.where(ahead == 1, 2, jnp.where(ahead == 2, 3, 0)))
    odd = jnp.where(ahead == 1, 1, jnp.where(ahead == 3, 2, jnp.where(ahead == 2, 3, 0)))
    return jnp.where(chip % 2 == 0, even, odd)


def places(route_ids, chip, pairs, capacity):
    ids = route_ids.reshape(-1)
    count = ids.shape[0]
    row = lax.broadcasted_iota(jnp.int32, (count, count), 0)
    column = lax.broadcasted_iota(jnp.int32, (count, count), 1)
    earlier = (ids[:, None] == ids[None, :]) & (row < column)
    slot = jnp.sum(earlier.astype(jnp.int32), axis=0)
    return message_of(ids, chip, pairs) * capacity + slot


def placement(slot_at, slot_total):
    rows = lax.broadcasted_iota(jnp.int32, (slot_total, slot_at.shape[0]), 0)
    return (rows == slot_at[None, :]).astype(jnp.bfloat16)


def after(value, *others):
    return lax.optimization_barrier((value, *others))[0]


def hidden_forward(routed, gate_cols, up_cols):
    gate_pre = jnp.dot(routed, gate_cols, preferred_element_type=jnp.float32)
    up_pre = jnp.dot(routed, up_cols, preferred_element_type=jnp.float32)
    return ((jax.nn.silu(gate_pre) * up_pre).astype(jnp.bfloat16),)


def made_forward(hidden, down_rows):
    return jnp.dot(hidden[0], down_rows, preferred_element_type=jnp.float32).astype(jnp.bfloat16)


def hidden_backward(routed, stash_rows, down_rows):
    hidden_grad = jnp.dot(routed, down_rows.T, preferred_element_type=jnp.float32)
    gate_pre = stash_rows[:, 0, :].astype(jnp.float32)
    up_pre = stash_rows[:, 1, :].astype(jnp.float32)
    sigmoid_gate = jax.nn.sigmoid(gate_pre)
    grad_gate = (
        hidden_grad * up_pre * sigmoid_gate * (1.0 + gate_pre * (1.0 - sigmoid_gate))
    ).astype(jnp.bfloat16)
    grad_up = (hidden_grad * gate_pre * sigmoid_gate).astype(jnp.bfloat16)
    return grad_gate, grad_up


def made_backward(hidden, gate_cols, up_cols):
    total = jnp.dot(hidden[0], gate_cols.T, preferred_element_type=jnp.float32)
    total = total + jnp.dot(hidden[1], up_cols.T, preferred_element_type=jnp.float32)
    return total.astype(jnp.bfloat16)


def dispatch(placed, rows, capacity, out, across):
    def picked(k):
        part = placed[k * capacity : (k + 1) * capacity]
        return jnp.dot(part, rows, preferred_element_type=jnp.float32).astype(jnp.bfloat16)

    own = picked(0)
    own_distant = lax.ppermute(own, "expert", across)
    near = jnp.concatenate(
        [lax.ppermute(picked(k), "expert", out(k)) for k in range(1, REACH)], axis=0
    )
    distant = lax.ppermute(near, "expert", across)
    return jnp.concatenate([own, own_distant, near, distant], axis=0)


def collect(mine, given, capacity, onward, sections, home, across, beside):
    came = lax.ppermute(given, "expert", beside)
    summed = mine.astype(jnp.float32) + came.astype(jnp.float32)
    own_near, own_far = summed[:capacity], summed[capacity : 2 * capacity]
    width = (REACH - 1) * capacity
    near, far = summed[2 * capacity : 2 * capacity + width], summed[2 * capacity + width :]
    near = near + lax.ppermute(far.astype(jnp.bfloat16), "expert", across).astype(jnp.float32)
    near = near.astype(jnp.bfloat16)
    own_came = lax.ppermute(own_far.astype(jnp.bfloat16), "expert", across)
    pieces = [near[k * capacity : (k + 1) * capacity] for k in range(REACH - 1)]
    own = (own_near + after(own_came, *pieces).astype(jnp.float32)).astype(jnp.bfloat16)
    parts = [
        lax.ppermute(piece, ("section", "expert"), home(k + 1, onward))
        for k, piece in enumerate(pieces)
    ]
    parts.insert(0, lax.ppermute(own, ("section", "expert"), home(0, onward)))
    return jnp.concatenate(parts, axis=0)


def combine(placed, back, gate_values):
    picked = lax.dot_general(
        placed, back, (((0,), (0,)), ((), ())), preferred_element_type=jnp.float32
    )
    return picked * gate_values


def local(
    layer_input,
    cotangent,
    gate_weight,
    up_weight,
    down_weight,
    stashed_pre,
    first_ids,
    first_gates,
    second_ids,
    second_gates,
    keep_mask,
):
    devices = lax.axis_size("expert")
    sections = lax.axis_size("section")
    chips = devices // 2
    pairs = chips // 2
    capacity = stashed_pre.shape[2]
    slots = pairs * capacity
    hidden_local = gate_weight.shape[2]
    out, home, across, beside = routes(devices, sections)
    me = lax.axis_index("expert")
    chip, core = me // 2, me % 2
    tokens_in = layer_input[0]
    keep_rows = keep_mask[0]
    kept_grads = cotangent[0] * keep_rows[:, None].astype(jnp.bfloat16)
    first_at = places(first_ids[0], chip, pairs, capacity)
    second_at = places(second_ids[0], chip, pairs, capacity)
    ahead = [(i, (i + 1) % sections) for i in range(sections)]
    behind = [((i + 1) % sections, i) for i in range(sections)]
    origins = [
        [(here + jnp.where(here % 2 == 0, -step, step)) % chips for step in range(REACH)]
        for here in (chip, chip ^ 1)
    ]
    origins = [origins[0][0], origins[1][0], *origins[0][1:], *origins[1][1:]]
    stash_halves = [
        jnp.concatenate(
            [
                lax.dynamic_index_in_dim(stashed_pre[0], 2 * origin + which, 0, False)
                for origin in origins
            ]
        )
        for which in (core, 1 - core)
    ]
    gate_cols = gate_weight[0]
    up_cols = up_weight[0]
    down_rows = down_weight[0]

    held_first = dispatch(placement(first_at, slots), tokens_in, capacity, out, across)
    held_second = dispatch(placement(second_at, slots), kept_grads, capacity, out, across)
    beside_first = lax.ppermute(held_first, "expert", beside)
    relayed_tokens = lax.ppermute(after(tokens_in, held_first), "section", ahead)
    relayed_grads = lax.ppermute(after(cotangent[0], held_first), "section", behind)
    first_told = lax.ppermute(
        jnp.stack([after(first_at, held_first).astype(jnp.float32), first_gates[0, :, 0]]), "section", ahead
    )
    second_told = lax.ppermute(
        jnp.stack(
            [
                after(second_at, held_first).astype(jnp.float32),
                second_gates[0, :, 0],
                keep_rows.astype(jnp.float32),
            ]
        ),
        "section",
        behind,
    )
    first_mine = hidden_forward(held_first, gate_cols, up_cols)
    first_given = hidden_forward(beside_first, gate_cols, up_cols)
    first_mine, first_given = lax.optimization_barrier((first_mine, first_given))
    given_first = made_forward(first_given, down_rows)
    made_first = lax.optimization_barrier(made_forward(first_mine, down_rows))
    back_first = collect(
        made_first, given_first, capacity, 1, sections, home, across, beside
    )
    beside_second = lax.ppermute(held_second, "expert", beside)
    second_mine = hidden_backward(held_second, stash_halves[0], down_rows)
    second_given = hidden_backward(beside_second, stash_halves[1], down_rows)
    second_mine, second_given = lax.optimization_barrier((second_mine, second_given))
    given_second = made_backward(second_given, gate_cols, up_cols)
    made_second = lax.optimization_barrier(made_backward(second_mine, gate_cols, up_cols))
    back_second = collect(
        made_second, given_second, capacity, -1, sections, home, across, beside
    )
    first_branch = combine(
        placement(first_told[0].astype(jnp.int32), slots), back_first, first_told[1][:, None]
    )
    second_branch = combine(
        placement(second_told[0].astype(jnp.int32), slots), back_second, second_told[1][:, None]
    )
    mixed_out = (relayed_tokens.astype(jnp.float32) + first_branch).astype(jnp.bfloat16)
    grad_out = (
        second_told[2][:, None] * (relayed_grads.astype(jnp.float32) + second_branch)
    ).astype(jnp.bfloat16)
    return (mixed_out[None], grad_out[None])


def solution(mesh):
    placed = (
        P("section", "expert", None),
        P("section", "expert", None),
        P("section", None, "expert"),
        P("section", None, "expert"),
        P("section", "expert", None),
        P("section", None, None, None, "expert"),
        P("section", "expert", None),
        P("section", "expert", None),
        P("section", "expert", None),
        P("section", "expert", None),
        P("section", "expert"),
    )
    return jax.shard_map(
        local,
        mesh=mesh,
        in_specs=placed,
        out_specs=(P("section", "expert", None), P("section", "expert", None)),
        check_vma=False,
    )
```

time: 187 us -> 184 us (0.984)
  starting transfers between devices: 45.2 us -> 61.8 us
  waiting for transfers between devices: 96.3 us -> 80.1 us
  local copies, waits for them, and re-layouts: 20.1 us -> 6.41 us
  matrix products: 18.9 us -> 27.6 us
    ppermute x22 -> x30, starting transfers between devices: 45.2 us -> 61.8 us  [the longest x6 14.5 us: dispatch(): lax.ppermute(picked(k), 'expert', out(k))]
    ppermute x22 -> x30, waiting for transfers between devices: 96.3 us -> 80.1 us  [the longest x2 30.8 us: collect(): lax.ppermute(far.astype(jnp.bfloat16), 'expert', across).astype(jnp.float32)]
    unnamed x65 -> x67, local copies, waits for them, and re-layouts: 13.1 us -> 4.59 us
    dot_general x7 -> x20, matrix products: 18.1 us -> 25.3 us  [the longest x8 11.8 us: picked(): jnp.dot(part, rows, preferred_element_type=jnp.float32).astype(jnp.bfloat16)]
    concatenate x5 -> x4, local copies, waits for them, and re-layouts: 3.26 us -> 0.11 us  [the longest x2 0.08 us: dispatch(): return jnp.concatenate([own, own_distant, near, distant], axis=0)]
    slice x6, local copies, waits for them, and re-layouts: 2.13 us -> 0.19 us  [the longest x2 0.08 us: collect(): pieces = [near[k * capacity:(k + 1) * capacity] for k in range(REACH - 1)]]
  transfers between devices with their start and end apart: 22 -> 30, of which waited for: 12 -> 8; matrix products, arithmetic and copies ran while one was open for 18% -> 18% of each run, Pallas kernels for 0% -> 0%
where the time goes in v2:
time: 184 us; the launch traced here: 183 us
  waiting for transfers between devices  80.1 us (44%)
  starting transfers between devices  61.8 us (34%)
  matrix products  27.6 us (15%)
  local copies, waits for them, and re-layouts  6.41 us (3%)
  other arithmetic  5.91 us (3%)
    ppermute x2, waiting for transfers between devices, collect(): lax.ppermute(far.astype(jnp.bfloat16), 'expert', across).astype(jnp.float32)  30.8 us
    ppermute x2, waiting for transfers between devices, collect(): parts.insert(0, lax.ppermute(own, ('section', 'expert'), home(0, onward)))  29 us
    ppermute x6, starting transfers between devices, dispatch(): lax.ppermute(picked(k), 'expert', out(k))  14.5 us
    ppermute x2, waiting for transfers between devices, dispatch(): distant = lax.ppermute(near, 'expert', across)  13.4 us
    dot_general x8, matrix products, picked(): jnp.dot(part, rows, preferred_element_type=jnp.float32).astype(jnp.bfloat16)  11.8 us
    ppermute x6, starting transfers between devices, collect(): lax.ppermute(piece, ('section', 'expert'), home(k + 1, onward))  8.57 us
    ppermute x6, waiting for transfers between devices, dispatch(): lax.ppermute(picked(k), 'expert', out(k))  6.88 us
    ppermute x2, starting transfers between devices, collect(): parts.insert(0, lax.ppermute(own, ('section', 'expert'), home(0, onward)))  6.66 us
  transfers between devices with their start and end apart: 30, of which 8 were waited for; matrix products, arithmetic and copies ran while one was open for 18% of the time, Pallas kernels for 0%

profile of v2, /device:TPU:1, one launch (start us, length us, event | category | flops | bytes accessed | tf_op | source)
XLA Modules:
  0.0 183.2 jit_solution(16997948058320734839)
XLA Ops:
  2.9 1.9 %convolution_convert_fusion.8 = bf16[24,4096]{1,0:T(8,128)(2,1)} fusion(pred[96,64]{1,0:T(8,128)(4,1)S(1)} %iota_compare_fusion.3, bf16[1,64,4096]{2,1,0:T(8,128)(2,1)} %param.11), kind=kOutput, calls=%fused_computation.14 | convolution fusion | flops 12681216 | bytes 723968 | tf_op jit(solution)/shard_map/dot_general | solution.py:90
  4.8 6.4 %collective-permute-start.1 = (bf16[24,4096]{1,0:T(8,128)(2,1)}, bf16[24,4096]{1,0:T(8,128)(2,1)S(1)}, u32[]{:S(2)}, u32[]{:S(2)}) collective-permute-start(bf16[24,4096]{1,0:T(8,128)(2,1)} %convolution_convert_fusion.8), channel_id=1, source_target_pairs={{14,0},{15,1},{4,2},{5,3},{2,4},{3,5},{8,6},{9,7},{6,8},{7,9},{12,... | collective-permute-start | bytes 589832 | tf_op jit(solution)/shard_map/ppermute | solution.py:95
  14.1 4.0 %collective-permute-start.3 = (bf16[24,4096]{1,0:T(8,128)(2,1)}, bf16[24,4096]{1,0:T(8,128)(2,1)}, u32[]{:S(2)}, u32[]{:S(2)}) collective-permute-start(bf16[24,4096]{1,0:T(8,128)(2,1)} %convolution_convert_fusion.6), channel_id=1, source_target_pairs={{10,0},{11,1},{8,2},{9,3},{14,4},{15,5},{12,6},{13,7},{2,8},{3,9},... | collective-permute-start | bytes 589832 | tf_op jit(solution)/shard_map/ppermute | solution.py:95
  21.4 2.1 %convolution_convert_fusion.2 = bf16[24,4096]{1,0:T(8,128)(2,1)} fusion(bf16[64]{0:T(256)(128)(2,1)S(1)} %get-tuple-element.61, pred[96,64]{1,0:T(8,128)(4,1)} %copy-done.12, bf16[1,64,4096]{2,1,0:T(8,128)(2,1)} %param.12), kind=kOutput, calls=%fused_computation.8 | convolution fusion | flops 12943360 | bytes 724096 | tf_op jit(solution)/shard_map/dot_general | solution.py:90
  23.5 2.1 %constant_dynamic-update-slice_fusion.11 = (bf16[192,4096]{1,0:T(8,128)(2,1)}, bf16[24,4096]{1,0:T(8,128)(2,1)}) fusion(bf16[64]{0:T(256)(128)(2,1)S(1)} %get-tuple-element.61, bf16[1,64,4096]{2,1,0:T(8,128)(2,1)} %param.12, pred[96,64]{1,0:T(8,128)(4,1)} %copy-done.12), kind=kOutput, calls=%fused_computation.117 | convolution fusion | flops 12943359 | bytes 920704 | tf_op jit(solution)/shard_map/dot_general | solution.py:90
  28.4 3.4 %collective-permute-start.20 = (bf16[24,4096]{1,0:T(8,128)(2,1)S(1)}, bf16[24,4096]{1,0:T(8,128)(2,1)S(1)}, u32[]{:S(2)}, u32[]{:S(2)}) collective-permute-start(bf16[24,4096]{1,0:T(8,128)(2,1)S(1)} %copy-done.10), channel_id=1, source_target_pairs={{10,0},{11,1},{8,2},{9,3},{14,4},{15,5},{12,6},{13,7},{2,8},{3,9},... | collective-permute-start | bytes 589832 | tf_op jit(solution)/shard_map/ppermute | solution.py:95
  32.1 4.6 %collective-permute-start = (bf16[24,4096]{1,0:T(8,128)(2,1)S(1)}, bf16[24,4096]{1,0:T(8,128)(2,1)S(1)}, u32[]{:S(2)}, u32[]{:S(2)}) collective-permute-start(bf16[24,4096]{1,0:T(8,128)(2,1)S(1)} %copy-done.9), channel_id=1, source_target_pairs={{0,2},{1,3},{2,0},{3,1},{4,6},{5,7},{6,4},{7,5},{8,10},{9,11},{10,... | collective-permute-start | bytes 589832 | tf_op jit(solution)/shard_map/ppermute | solution.py:93
  39.3 5.2 %collective-permute-done.20 = bf16[24,4096]{1,0:T(8,128)(2,1)S(1)} collective-permute-done((bf16[24,4096]{1,0:T(8,128)(2,1)S(1)}, bf16[24,4096]{1,0:T(8,128)(2,1)S(1)}, u32[]{:S(2)}, u32[]{:S(2)}) %collective-permute-start.20) | collective-permute-done | bytes 196640 | tf_op jit(solution)/shard_map/ppermute | solution.py:95
  45.6 4.8 %collective-permute-start.21 = (bf16[72,4096]{1,0:T(8,128)(2,1)S(1)}, bf16[72,4096]{1,0:T(8,128)(2,1)S(1)}, u32[]{:S(2)}, u32[]{:S(2)}) collective-permute-start(bf16[72,4096]{1,0:T(8,128)(2,1)S(1)} %pad_maximum_fusion.1), channel_id=1, source_target_pairs={{0,2},{1,3},{2,0},{3,1},{4,6},{5,7},{6,4},{7,5},{8,10},{9,11},{10,... | collective-permute-start | bytes 1769480 | tf_op jit(solution)/shard_map/ppermute | solution.py:97
  53.5 4.8 %collective-permute-done.4 = bf16[72,4096]{1,0:T(8,128)(2,1)S(1)} collective-permute-done((bf16[72,4096]{1,0:T(8,128)(2,1)S(1)}, bf16[72,4096]{1,0:T(8,128)(2,1)S(1)}, u32[]{:S(2)}, u32[]{:S(2)}) %collective-permute-start.4) | collective-permute-done | bytes 589856 | tf_op jit(solution)/shard_map/ppermute | solution.py:97
  58.3 3.9 %collective-permute-start.7 = (bf16[192,4096]{1,0:T(8,128)(2,1)S(1)}, bf16[192,4096]{1,0:T(8,128)(2,1)S(1)}, u32[]{:S(2)}, u32[]{:S(2)}) collective-permute-start(bf16[192,4096]{1,0:T(8,128)(2,1)S(1)} %constant_dynamic-update-slice_fusion), channel_id=1, source_target_pairs={{0,1},{1,0},{2,3},{3,2},{4,5},{5,4},{6,7},{7,6},{8,9},{9,8},{10,11... | collective-permute-start | bytes 4718600 | tf_op jit(solution)/shard_map/ppermute | solution.py:177
  62.2 8.7 %collective-permute-done.21 = bf16[72,4096]{1,0:T(8,128)(2,1)S(1)} collective-permute-done((bf16[72,4096]{1,0:T(8,128)(2,1)S(1)}, bf16[72,4096]{1,0:T(8,128)(2,1)S(1)}, u32[]{:S(2)}, u32[]{:S(2)}) %collective-permute-start.21) | collective-permute-done | bytes 589856 | tf_op jit(solution)/shard_map/ppermute | solution.py:97
  70.9 2.2 %collective-permute-start.22 = (bf16[192,4096]{1,0:T(8,128)(2,1)S(1)}, bf16[192,4096]{1,0:T(8,128)(2,1)S(1)}, u32[]{:S(2)}, u32[]{:S(2)}) collective-permute-start(bf16[192,4096]{1,0:T(8,128)(2,1)S(1)} %constant_dynamic-update-slice_fusion.6), channel_id=1, source_target_pairs={{0,1},{1,0},{2,3},{3,2},{4,5},{5,4},{6,7},{7,6},{8,9},{9,8},{10,11... | collective-permute-start | bytes 4718600 | tf_op jit(solution)/shard_map/ppermute | solution.py:202
  74.5 3.8 %collective-permute-start.15 = (f32[3,64]{1,0:T(4,128)S(1)}, f32[3,64]{1,0:T(4,128)S(1)}, u32[]{:S(2)}, u32[]{:S(2)}) collective-permute-start(f32[3,64]{1,0:T(4,128)S(1)} %pad_maximum_fusion.2), channel_id=1, source_target_pairs={{16,0},{32,16},{48,32},{64,48},{80,64},{96,80},{112,96},{128,112},... | collective-permute-start | bytes 2312 | tf_op jit(solution)/shard_map/ppermute | solution.py:183
  82.6 4.9 %collective-permute-start.16 = (bf16[64,4096]{1,0:T(8,128)(2,1)S(1)}, bf16[64,4096]{1,0:T(8,128)(2,1)S(1)}, u32[]{:S(2)}, u32[]{:S(2)}) collective-permute-start(bf16[64,4096]{1,0:T(8,128)(2,1)S(1)} %bitcast.159), channel_id=1, source_target_pairs={{16,0},{32,16},{48,32},{64,48},{80,64},{96,80},{112,96},{128,112},... | collective-permute-start | bytes 1572872 | tf_op jit(solution)/shard_map/ppermute | solution.py:179
  99.9 2.1 %collective-permute-start.10 = (bf16[72,4096]{1,0:T(8,128)(2,1)S(1)}, bf16[72,4096]{1,0:T(8,128)(2,1)S(1)}, u32[]{:S(2)}, u32[]{:S(2)}) collective-permute-start(bf16[72,4096]{1,0:T(8,128)(2,1)S(1)} %slice.135), channel_id=1, source_target_pairs={{0,2},{1,3},{2,0},{3,1},{4,6},{5,7},{6,4},{7,5},{8,10},{9,11},{10,... | collective-permute-start | bytes 1769480 | tf_op jit(solution)/shard_map/ppermute | solution.py:107
  104.2 11.0 %collective-permute-done.10 = bf16[72,4096]{1,0:T(8,128)(2,1)S(1)} collective-permute-done((bf16[72,4096]{1,0:T(8,128)(2,1)S(1)}, bf16[72,4096]{1,0:T(8,128)(2,1)S(1)}, u32[]{:S(2)}, u32[]{:S(2)}) %collective-permute-start.10) | collective-permute-done | bytes 589856 | tf_op jit(solution)/shard_map/ppermute | solution.py:107
  116.6 19.7 %collective-permute-done.25 = bf16[72,4096]{1,0:T(8,128)(2,1)S(1)} collective-permute-done((bf16[72,4096]{1,0:T(8,128)(2,1)S(1)}, bf16[72,4096]{1,0:T(8,128)(2,1)S(1)}, u32[]{:S(2)}, u32[]{:S(2)}) %collective-permute-start.25) | collective-permute-done | bytes 589856 | tf_op jit(solution)/shard_map/ppermute | solution.py:107
  136.6 3.0 %collective-permute-start.13 = (bf16[24,4096]{1,0:T(8,128)(2,1)S(1)}, bf16[24,4096]{1,0:T(8,128)(2,1)S(1)}, u32[]{:S(2)}, u32[]{:S(2)}) collective-permute-start(bf16[24,4096]{1,0:T(8,128)(2,1)S(1)} %get-tuple-element.55), channel_id=1, source_target_pairs={{0,28},{1,29},{2,22},{3,23},{4,16},{5,17},{6,26},{7,27},{8,20},{9,... | collective-permute-start | bytes 589832 | tf_op jit(solution)/shard_map/ppermute | solution.py:113
  139.7 3.9 %collective-permute-start.11 = (bf16[24,4096]{1,0:T(8,128)(2,1)S(1)}, bf16[24,4096]{1,0:T(8,128)(2,1)S(1)}, u32[]{:S(2)}, u32[]{:S(2)}) collective-permute-start(bf16[24,4096]{1,0:T(8,128)(2,1)S(1)} %fusion.45), channel_id=1, source_target_pairs={{0,16},{1,17},{2,18},{3,19},{4,20},{5,21},{6,22},{7,23},{8,24},{9,... | collective-permute-start | bytes 589832 | tf_op jit(solution)/shard_map/ppermute | solution.py:116
  143.6 16.2 %collective-permute-done.11 = bf16[24,4096]{1,0:T(8,128)(2,1)S(1)} collective-permute-done((bf16[24,4096]{1,0:T(8,128)(2,1)S(1)}, bf16[24,4096]{1,0:T(8,128)(2,1)S(1)}, u32[]{:S(2)}, u32[]{:S(2)}) %collective-permute-start.11) | collective-permute-done | bytes 196640 | tf_op jit(solution)/shard_map/ppermute | solution.py:116
  161.0 4.3 %collective-permute-start.28 = (bf16[24,4096]{1,0:T(8,128)(2,1)S(1)}, bf16[24,4096]{1,0:T(8,128)(2,1)S(1)}, u32[]{:S(2)}, u32[]{:S(2)}) collective-permute-start(bf16[24,4096]{1,0:T(8,128)(2,1)S(1)} %get-tuple-element.32), channel_id=1, source_target_pairs={{0,252},{1,253},{2,246},{3,247},{4,240},{5,241},{6,250},{7,251},{8... | collective-permute-start | bytes 589832 | tf_op jit(solution)/shard_map/ppermute | solution.py:113
  165.3 2.8 %collective-permute-start.26 = (bf16[24,4096]{1,0:T(8,128)(2,1)S(1)}, bf16[24,4096]{1,0:T(8,128)(2,1)S(1)}, u32[]{:S(2)}, u32[]{:S(2)}) collective-permute-start(bf16[24,4096]{1,0:T(8,128)(2,1)S(1)} %fusion.44), channel_id=1, source_target_pairs={{0,240},{1,241},{2,242},{3,243},{4,244},{5,245},{6,246},{7,247},{8... | collective-permute-start | bytes 589832 | tf_op jit(solution)/shard_map/ppermute | solution.py:116
  169.2 12.8 %collective-permute-done.26 = bf16[24,4096]{1,0:T(8,128)(2,1)S(1)} collective-permute-done((bf16[24,4096]{1,0:T(8,128)(2,1)S(1)}, bf16[24,4096]{1,0:T(8,128)(2,1)S(1)}, u32[]{:S(2)}, u32[]{:S(2)}) %collective-permute-start.26) | collective-permute-done | bytes 196640 | tf_op jit(solution)/shard_map/ppermute | solution.py:116
  (157 shorter events, 43.3 us)
Async XLA Ops:
  4.8 23.5 %collective-permute-start.1 = (bf16[24,4096]{1,0:T(8,128)(2,1)}, bf16[24,4096]{1,0:T(8,128)(2,1)S(1)}, u32[]{:S(2)}, u32[]{:S(2)}) collective-permute-start(bf16[24,4096]{1,0:T(8,128)(2,1)} %convolution_convert_fusion.8), channel_id=1, source_target_pairs={{14,0},{15,1},{4,2},{5,3},{2,4},{3,5},{8,6},{9,7},{6,8},{7,9},{12,... | collective-permute-start | bytes 589832 | tf_op jit(solution)/shard_map/ppermute | solution.py:95
  13.2 18.6 %collective-permute-start.2 = (bf16[24,4096]{1,0:T(8,128)(2,1)}, bf16[24,4096]{1,0:T(8,128)(2,1)S(1)}, u32[]{:S(2)}, u32[]{:S(2)}) collective-permute-start(bf16[24,4096]{1,0:T(8,128)(2,1)} %convolution_convert_fusion.7), channel_id=1, source_target_pairs={{12,0},{13,1},{6,2},{7,3},{0,4},{1,5},{10,6},{11,7},{4,8},{5,9},{1... | collective-permute-start | bytes 589832 | tf_op jit(solution)/shard_map/ppermute | solution.py:95
  14.1 18.0 %collective-permute-start.3 = (bf16[24,4096]{1,0:T(8,128)(2,1)}, bf16[24,4096]{1,0:T(8,128)(2,1)}, u32[]{:S(2)}, u32[]{:S(2)}) collective-permute-start(bf16[24,4096]{1,0:T(8,128)(2,1)} %convolution_convert_fusion.6), channel_id=1, source_target_pairs={{10,0},{11,1},{8,2},{9,3},{14,4},{15,5},{12,6},{13,7},{2,8},{3,9},... | collective-permute-start | bytes 589832 | tf_op jit(solution)/shard_map/ppermute | solution.py:95
  19.7 19.6 %collective-permute-start.18 = (bf16[24,4096]{1,0:T(8,128)(2,1)}, bf16[24,4096]{1,0:T(8,128)(2,1)}, u32[]{:S(2)}, u32[]{:S(2)}) collective-permute-start(bf16[24,4096]{1,0:T(8,128)(2,1)} %convolution_convert_fusion.4), channel_id=1, source_target_pairs={{14,0},{15,1},{4,2},{5,3},{2,4},{3,5},{8,6},{9,7},{6,8},{7,9},{12,... | collective-permute-start | bytes 589832 | tf_op jit(solution)/shard_map/ppermute | solution.py:95
  20.7 18.6 %collective-permute-start.19 = (bf16[24,4096]{1,0:T(8,128)(2,1)}, bf16[24,4096]{1,0:T(8,128)(2,1)}, u32[]{:S(2)}, u32[]{:S(2)}) collective-permute-start(bf16[24,4096]{1,0:T(8,128)(2,1)} %convolution_convert_fusion.3), channel_id=1, source_target_pairs={{12,0},{13,1},{6,2},{7,3},{0,4},{1,5},{10,6},{11,7},{4,8},{5,9},{1... | collective-permute-start | bytes 589832 | tf_op jit(solution)/shard_map/ppermute | solution.py:95
  31.8 18.6 %collective-permute-start.17 = (bf16[24,4096]{1,0:T(8,128)(2,1)S(1)}, bf16[24,4096]{1,0:T(8,128)(2,1)S(1)}, u32[]{:S(2)}, u32[]{:S(2)}) collective-permute-start(bf16[24,4096]{1,0:T(8,128)(2,1)S(1)} %copy-done.11), channel_id=1, source_target_pairs={{0,2},{1,3},{2,0},{3,1},{4,6},{5,7},{6,4},{7,5},{8,10},{9,11},{10,... | collective-permute-start | bytes 589832 | tf_op jit(solution)/shard_map/ppermute | solution.py:93
  32.1 20.2 %collective-permute-start = (bf16[24,4096]{1,0:T(8,128)(2,1)S(1)}, bf16[24,4096]{1,0:T(8,128)(2,1)S(1)}, u32[]{:S(2)}, u32[]{:S(2)}) collective-permute-start(bf16[24,4096]{1,0:T(8,128)(2,1)S(1)} %copy-done.9), channel_id=1, source_target_pairs={{0,2},{1,3},{2,0},{3,1},{4,6},{5,7},{6,4},{7,5},{8,10},{9,11},{10,... | collective-permute-start | bytes 589832 | tf_op jit(solution)/shard_map/ppermute | solution.py:93
  39.3 18.9 %collective-permute-start.4 = (bf16[72,4096]{1,0:T(8,128)(2,1)S(1)}, bf16[72,4096]{1,0:T(8,128)(2,1)S(1)}, u32[]{:S(2)}, u32[]{:S(2)}) collective-permute-start(bf16[72,4096]{1,0:T(8,128)(2,1)S(1)} %pad_maximum_fusion), channel_id=1, source_target_pairs={{0,2},{1,3},{2,0},{3,1},{4,6},{5,7},{6,4},{7,5},{8,10},{9,11},{10,... | collective-permute-start | bytes 1769480 | tf_op jit(solution)/shard_map/ppermute | solution.py:97
  45.6 25.3 %collective-permute-start.21 = (bf16[72,4096]{1,0:T(8,128)(2,1)S(1)}, bf16[72,4096]{1,0:T(8,128)(2,1)S(1)}, u32[]{:S(2)}, u32[]{:S(2)}) collective-permute-start(bf16[72,4096]{1,0:T(8,128)(2,1)S(1)} %pad_maximum_fusion.1), channel_id=1, source_target_pairs={{0,2},{1,3},{2,0},{3,1},{4,6},{5,7},{6,4},{7,5},{8,10},{9,11},{10,... | collective-permute-start | bytes 1769480 | tf_op jit(solution)/shard_map/ppermute | solution.py:97
  58.3 30.4 %collective-permute-start.7 = (bf16[192,4096]{1,0:T(8,128)(2,1)S(1)}, bf16[192,4096]{1,0:T(8,128)(2,1)S(1)}, u32[]{:S(2)}, u32[]{:S(2)}) collective-permute-start(bf16[192,4096]{1,0:T(8,128)(2,1)S(1)} %constant_dynamic-update-slice_fusion), channel_id=1, source_target_pairs={{0,1},{1,0},{2,3},{3,2},{4,5},{5,4},{6,7},{7,6},{8,9},{9,8},{10,11... | collective-permute-start | bytes 4718600 | tf_op jit(solution)/shard_map/ppermute | solution.py:177
  70.9 16.5 %collective-permute-start.22 = (bf16[192,4096]{1,0:T(8,128)(2,1)S(1)}, bf16[192,4096]{1,0:T(8,128)(2,1)S(1)}, u32[]{:S(2)}, u32[]{:S(2)}) collective-permute-start(bf16[192,4096]{1,0:T(8,128)(2,1)S(1)} %constant_dynamic-update-slice_fusion.6), channel_id=1, source_target_pairs={{0,1},{1,0},{2,3},{3,2},{4,5},{5,4},{6,7},{7,6},{8,9},{9,8},{10,11... | collective-permute-start | bytes 4718600 | tf_op jit(solution)/shard_map/ppermute | solution.py:202
  78.4 61.3 %collective-permute-start.5 = (bf16[64,4096]{1,0:T(8,128)(2,1)S(1)}, bf16[64,4096]{1,0:T(8,128)(2,1)S(1)}, u32[]{:S(2)}, u32[]{:S(2)}) collective-permute-start(bf16[64,4096]{1,0:T(8,128)(2,1)S(1)} %bitcast.160), channel_id=1, source_target_pairs={{0,16},{16,32},{32,48},{48,64},{64,80},{80,96},{96,112},{112,128},... | collective-permute-start | bytes 1572872 | tf_op jit(solution)/shard_map/ppermute | solution.py:178
  82.6 86.6 %collective-permute-start.16 = (bf16[64,4096]{1,0:T(8,128)(2,1)S(1)}, bf16[64,4096]{1,0:T(8,128)(2,1)S(1)}, u32[]{:S(2)}, u32[]{:S(2)}) collective-permute-start(bf16[64,4096]{1,0:T(8,128)(2,1)S(1)} %bitcast.159), channel_id=1, source_target_pairs={{16,0},{32,16},{48,32},{64,48},{80,64},{96,80},{112,96},{128,112},... | collective-permute-start | bytes 1572872 | tf_op jit(solution)/shard_map/ppermute | solution.py:179
  102.7 33.8 %collective-permute-start.9 = (bf16[24,4096]{1,0:T(8,128)(2,1)S(1)}, bf16[24,4096]{1,0:T(8,128)(2,1)S(1)}, u32[]{:S(2)}, u32[]{:S(2)}) collective-permute-start(bf16[24,4096]{1,0:T(8,128)(2,1)S(1)} %slice.133), channel_id=1, source_target_pairs={{0,2},{1,3},{2,0},{3,1},{4,6},{5,7},{6,4},{7,5},{8,10},{9,11},{10,... | collective-permute-start | bytes 589832 | tf_op jit(solution)/shard_map/ppermute | solution.py:109
  102.8 33.8 %collective-permute-start.24 = (bf16[24,4096]{1,0:T(8,128)(2,1)S(1)}, bf16[24,4096]{1,0:T(8,128)(2,1)S(1)}, u32[]{:S(2)}, u32[]{:S(2)}) collective-permute-start(bf16[24,4096]{1,0:T(8,128)(2,1)S(1)} %slice.148), channel_id=1, source_target_pairs={{0,2},{1,3},{2,0},{3,1},{4,6},{5,7},{6,4},{7,5},{8,10},{9,11},{10,... | collective-permute-start | bytes 589832 | tf_op jit(solution)/shard_map/ppermute | solution.py:109
  115.3 21.1 %collective-permute-start.25 = (bf16[72,4096]{1,0:T(8,128)(2,1)S(1)}, bf16[72,4096]{1,0:T(8,128)(2,1)S(1)}, u32[]{:S(2)}, u32[]{:S(2)}) collective-permute-start(bf16[72,4096]{1,0:T(8,128)(2,1)S(1)} %slice.150), channel_id=1, source_target_pairs={{0,2},{1,3},{2,0},{3,1},{4,6},{5,7},{6,4},{7,5},{8,10},{9,11},{10,... | collective-permute-start | bytes 1769480 | tf_op jit(solution)/shard_map/ppermute | solution.py:107
  136.3 24.7 %collective-permute-start.12 = (bf16[24,4096]{1,0:T(8,128)(2,1)S(1)}, bf16[24,4096]{1,0:T(8,128)(2,1)S(1)}, u32[]{:S(2)}, u32[]{:S(2)}) collective-permute-start(bf16[24,4096]{1,0:T(8,128)(2,1)S(1)} %get-tuple-element.53), channel_id=1, source_target_pairs={{0,30},{1,31},{2,20},{3,21},{4,18},{5,19},{6,24},{7,25},{8,22},{9,... | collective-permute-start | bytes 589832 | tf_op jit(solution)/shard_map/ppermute | solution.py:113
  136.5 24.5 %collective-permute-start.14 = (bf16[24,4096]{1,0:T(8,128)(2,1)S(1)}, bf16[24,4096]{1,0:T(8,128)(2,1)S(1)}, u32[]{:S(2)}, u32[]{:S(2)}) collective-permute-start(bf16[24,4096]{1,0:T(8,128)(2,1)S(1)} %get-tuple-element.54), channel_id=1, source_target_pairs={{0,26},{1,27},{2,24},{3,25},{4,30},{5,31},{6,28},{7,29},{8,18},{9,... | collective-permute-start | bytes 589832 | tf_op jit(solution)/shard_map/ppermute | solution.py:113
  136.6 28.7 %collective-permute-start.13 = (bf16[24,4096]{1,0:T(8,128)(2,1)S(1)}, bf16[24,4096]{1,0:T(8,128)(2,1)S(1)}, u32[]{:S(2)}, u32[]{:S(2)}) collective-permute-start(bf16[24,4096]{1,0:T(8,128)(2,1)S(1)} %get-tuple-element.55), channel_id=1, source_target_pairs={{0,28},{1,29},{2,22},{3,23},{4,16},{5,17},{6,26},{7,27},{8,20},{9,... | collective-permute-start | bytes 589832 | tf_op jit(solution)/shard_map/ppermute | solution.py:113
  139.7 20.1 %collective-permute-start.11 = (bf16[24,4096]{1,0:T(8,128)(2,1)S(1)}, bf16[24,4096]{1,0:T(8,128)(2,1)S(1)}, u32[]{:S(2)}, u32[]{:S(2)}) collective-permute-start(bf16[24,4096]{1,0:T(8,128)(2,1)S(1)} %fusion.45), channel_id=1, source_target_pairs={{0,16},{1,17},{2,18},{3,19},{4,20},{5,21},{6,22},{7,23},{8,24},{9,... | collective-permute-start | bytes 589832 | tf_op jit(solution)/shard_map/ppermute | solution.py:116
  159.8 22.2 %collective-permute-start.27 = (bf16[24,4096]{1,0:T(8,128)(2,1)S(1)}, bf16[24,4096]{1,0:T(8,128)(2,1)S(1)}, u32[]{:S(2)}, u32[]{:S(2)}) collective-permute-start(bf16[24,4096]{1,0:T(8,128)(2,1)S(1)} %get-tuple-element.30), channel_id=1, source_target_pairs={{0,254},{1,255},{2,244},{3,245},{4,242},{5,243},{6,248},{7,249},{8... | collective-permute-start | bytes 589832 | tf_op jit(solution)/shard_map/ppermute | solution.py:113
  161.0 21.0 %collective-permute-start.29 = (bf16[24,4096]{1,0:T(8,128)(2,1)S(1)}, bf16[24,4096]{1,0:T(8,128)(2,1)S(1)}, u32[]{:S(2)}, u32[]{:S(2)}) collective-permute-start(bf16[24,4096]{1,0:T(8,128)(2,1)S(1)} %get-tuple-element.31), channel_id=1, source_target_pairs={{0,250},{1,251},{2,248},{3,249},{4,254},{5,255},{6,252},{7,253},{8... | collective-permute-start | bytes 589832 | tf_op jit(solution)/shard_map/ppermute | solution.py:113
  161.0 21.0 %collective-permute-start.28 = (bf16[24,4096]{1,0:T(8,128)(2,1)S(1)}, bf16[24,4096]{1,0:T(8,128)(2,1)S(1)}, u32[]{:S(2)}, u32[]{:S(2)}) collective-permute-start(bf16[24,4096]{1,0:T(8,128)(2,1)S(1)} %get-tuple-element.32), channel_id=1, source_target_pairs={{0,252},{1,253},{2,246},{3,247},{4,240},{5,241},{6,250},{7,251},{8... | collective-permute-start | bytes 589832 | tf_op jit(solution)/shard_map/ppermute | solution.py:113
  165.3 16.7 %collective-permute-start.26 = (bf16[24,4096]{1,0:T(8,128)(2,1)S(1)}, bf16[24,4096]{1,0:T(8,128)(2,1)S(1)}, u32[]{:S(2)}, u32[]{:S(2)}) collective-permute-start(bf16[24,4096]{1,0:T(8,128)(2,1)S(1)} %fusion.44), channel_id=1, source_target_pairs={{0,240},{1,241},{2,242},{3,243},{4,244},{5,245},{6,246},{7,247},{8... | collective-permute-start | bytes 589832 | tf_op jit(solution)/shard_map/ppermute | solution.py:116
  (29 other events, 405.3 us)

commit v3 on v2

--- a/solution.py
+++ b/solution.py
@@ -1,6 +1,10 @@
+import functools
+
 import jax
 import jax.numpy as jnp
 from jax import lax
+from jax.experimental import pallas as pl
+from jax.experimental.pallas import tpu as pltpu
 from jax.sharding import PartitionSpec as P
 
 REACH = 4
@@ -30,21 +34,60 @@
     return out, home, across, beside
 
 
-def message_of(ids, chip, pairs):
-    ahead = (ids - chip // 2) % pairs
-    even = jnp.where(ahead == 3, 1, jnp.where(ahead == 1, 2, jnp.where(ahead == 2, 3, 0)))
-    odd = jnp.where(ahead == 1, 1, jnp.where(ahead == 3, 2, jnp.where(ahead == 2, 3, 0)))
-    return jnp.where(chip % 2 == 0, even, odd)
-
-
-def places(route_ids, chip, pairs, capacity):
-    ids = route_ids.reshape(-1)
-    count = ids.shape[0]
-    row = lax.broadcasted_iota(jnp.int32, (count, count), 0)
-    column = lax.broadcasted_iota(jnp.int32, (count, count), 1)
-    earlier = (ids[:, None] == ids[None, :]) & (row < column)
-    slot = jnp.sum(earlier.astype(jnp.int32), axis=0)
-    return message_of(ids, chip, pairs) * capacity + slot
+def prepare_kernel(pairs, capacity, chip_ref, *refs):
+    count = refs[0].shape[1]
+    chip = chip_ref[0]
+    odd = lax.rem(chip, 2)
+    before = lax.broadcasted_iota(jnp.int32, (count, count), 0)
+    before = (before < lax.broadcasted_iota(jnp.int32, (count, count), 1)).astype(jnp.bfloat16)
+
+    def fill(ids, rows, keep, parts):
+        ahead = ids - lax.div(chip, 2)
+        ahead = jnp.where(ahead < 0, ahead + pairs, ahead)
+        near = jnp.where(odd == 1, 1, pairs - 1)
+        step = jnp.where(ahead == 0, 0, jnp.where(ahead == 2, 3, jnp.where(ahead == near, 1, 2)))
+        chosen = lax.broadcasted_iota(jnp.int32, (8, count), 0) == step
+        chosen = jnp.where(chosen, 1.0, 0.0)
+        earlier = jnp.dot(
+            chosen.astype(jnp.bfloat16), before, preferred_element_type=jnp.float32
+        )
+        slot = jnp.sum(chosen * earlier, axis=0, keepdims=True).astype(jnp.int32)
+        place = step * capacity + slot
+        for k, part in enumerate(parts):
+            here = lax.broadcasted_iota(jnp.int32, (capacity, count), 0) + k * capacity == place
+            here = jnp.where(here, keep, 0.0).astype(jnp.bfloat16)
+            part[...] = jnp.dot(here, rows, preferred_element_type=jnp.float32).astype(part.dtype)
+        return place.astype(jnp.float32)
+
+    ids1, gates1, ids2, gates2, keep, rows1, rows2 = refs[:7]
+    outs = refs[7:]
+    kept = keep[...].astype(jnp.float32)
+    outs[8][0:1, :] = fill(ids1[...], rows1[...], jnp.ones_like(kept), outs[:REACH])
+    outs[8][1:2, :] = gates1[...]
+    outs[9][0:1, :] = fill(ids2[...], rows2[...], kept, outs[REACH : 2 * REACH])
+    outs[9][1:2, :] = gates2[...]
+    outs[9][2:3, :] = kept
+
+
+def prepare(chip, pairs, capacity, ids1, gates1, ids2, gates2, keep, rows1, rows2):
+    count, width = rows1.shape
+    piece = jax.ShapeDtypeStruct((capacity, width), jnp.bfloat16)
+    whole = pl.BlockSpec(memory_space=pltpu.VMEM)
+    made = pl.pallas_call(
+        functools.partial(prepare_kernel, pairs, capacity),
+        out_shape=[piece] * (2 * REACH)
+        + [
+            jax.ShapeDtypeStruct((2, count), jnp.float32),
+            jax.ShapeDtypeStruct((3, count), jnp.float32),
+        ],
+        in_specs=[pl.BlockSpec(memory_space=pltpu.SMEM)] + [whole] * 7,
+        out_specs=[whole] * (2 * REACH + 2),
+        cost_estimate=pl.CostEstimate(
+            flops=4 * REACH * capacity * count * width, bytes_accessed=8 * count * width, transcendentals=0
+        ),
+        name="prepare",
+    )(chip[None], ids1, gates1, ids2, gates2, keep, rows1, rows2)
+    return made[:REACH], made[REACH : 2 * REACH], made[8], made[9]
 
 
 def placement(slot_at, slot_total):
@@ -84,28 +127,24 @@
     return total.astype(jnp.bfloat16)
 
 
-def dispatch(placed, rows, capacity, out, across):
-    def picked(k):
-        part = placed[k * capacity : (k + 1) * capacity]
-        return jnp.dot(part, rows, preferred_element_type=jnp.float32).astype(jnp.bfloat16)
-
-    own = picked(0)
-    own_distant = lax.ppermute(own, "expert", across)
+def dispatch(pieces, out, across):
+    own_distant = lax.ppermute(pieces[0], "expert", across)
     near = jnp.concatenate(
-        [lax.ppermute(picked(k), "expert", out(k)) for k in range(1, REACH)], axis=0
+        [lax.ppermute(pieces[k], "expert", out(k)) for k in range(1, REACH)], axis=0
     )
     distant = lax.ppermute(near, "expert", across)
-    return jnp.concatenate([own, own_distant, near, distant], axis=0)
-
-
-def collect(mine, given, capacity, onward, sections, home, across, beside):
+    return jnp.concatenate([pieces[0], own_distant, near, distant], axis=0), own_distant
+
+
+def collect(mine, given, capacity, onward, sections, home, across, beside, earlier):
     came = lax.ppermute(given, "expert", beside)
     summed = mine.astype(jnp.float32) + came.astype(jnp.float32)
     own_near, own_far = summed[:capacity], summed[capacity : 2 * capacity]
     width = (REACH - 1) * capacity
     near, far = summed[2 * capacity : 2 * capacity + width], summed[2 * capacity + width :]
-    near = near + lax.ppermute(far.astype(jnp.bfloat16), "expert", across).astype(jnp.float32)
-    near = near.astype(jnp.bfloat16)
+    far = after(far.astype(jnp.bfloat16), *earlier[0])
+    near = near + lax.ppermute(far, "expert", across).astype(jnp.float32)
+    near = after(near.astype(jnp.bfloat16), *earlier[1])
     own_came = lax.ppermute(own_far.astype(jnp.bfloat16), "expert", across)
     pieces = [near[k * capacity : (k + 1) * capacity] for k in range(REACH - 1)]
     own = (own_near + after(own_came, *pieces).astype(jnp.float32)).astype(jnp.bfloat16)
@@ -114,7 +153,7 @@
         for k, piece in enumerate(pieces)
     ]
     parts.insert(0, lax.ppermute(own, ("section", "expert"), home(0, onward)))
-    return jnp.concatenate(parts, axis=0)
+    return parts
 
 
 def combine(placed, back, gate_values):
@@ -147,13 +186,20 @@
     out, home, across, beside = routes(devices, sections)
     me = lax.axis_index("expert")
     chip, core = me // 2, me % 2
-    tokens_in = layer_input[0]
-    keep_rows = keep_mask[0]
-    kept_grads = cotangent[0] * keep_rows[:, None].astype(jnp.bfloat16)
-    first_at = places(first_ids[0], chip, pairs, capacity)
-    second_at = places(second_ids[0], chip, pairs, capacity)
     ahead = [(i, (i + 1) % sections) for i in range(sections)]
     behind = [((i + 1) % sections, i) for i in range(sections)]
+    first_pieces, second_pieces, first_told, second_told = prepare(
+        chip,
+        pairs,
+        capacity,
+        first_ids[..., 0],
+        first_gates[..., 0],
+        second_ids[..., 0],
+        second_gates[..., 0],
+        keep_mask,
+        layer_input[0],
+        cotangent[0],
+    )
     origins = [
         [(here + jnp.where(here % 2 == 0, -step, step)) % chips for step in range(REACH)]
         for here in (chip, chip ^ 1)
@@ -172,33 +218,26 @@
     up_cols = up_weight[0]
     down_rows = down_weight[0]
 
-    held_first = dispatch(placement(first_at, slots), tokens_in, capacity, out, across)
-    held_second = dispatch(placement(second_at, slots), kept_grads, capacity, out, across)
+    held_first, own_distant = dispatch(first_pieces, out, across)
+    second_pieces = lax.optimization_barrier((*second_pieces, own_distant))[:REACH]
+    held_second, _ = dispatch(second_pieces, out, across)
+    tokens, grads, first_told, second_told, _ = lax.optimization_barrier(
+        (layer_input[0], cotangent[0], first_told, second_told, held_first)
+    )
+    first_told = lax.ppermute(first_told, "section", ahead)
+    second_told = lax.ppermute(second_told, "section", behind)
+    tokens = lax.ppermute(tokens, "section", ahead)
+    grads = lax.ppermute(grads, "section", behind)
     beside_first = lax.ppermute(held_first, "expert", beside)
-    relayed_tokens = lax.ppermute(after(tokens_in, held_first), "section", ahead)
-    relayed_grads = lax.ppermute(after(cotangent[0], held_first), "section", behind)
-    first_told = lax.ppermute(
-        jnp.stack([after(first_at, held_first).astype(jnp.float32), first_gates[0, :, 0]]), "section", ahead
-    )
-    second_told = lax.ppermute(
-        jnp.stack(
-            [
-                after(second_at, held_first).astype(jnp.float32),
-                second_gates[0, :, 0],
-                keep_rows.astype(jnp.float32),
-            ]
-        ),
-        "section",
-        behind,
-    )
     first_mine = hidden_forward(held_first, gate_cols, up_cols)
     first_given = hidden_forward(beside_first, gate_cols, up_cols)
     first_mine, first_given = lax.optimization_barrier((first_mine, first_given))
     given_first = made_forward(first_given, down_rows)
     made_first = lax.optimization_barrier(made_forward(first_mine, down_rows))
     back_first = collect(
-        made_first, given_first, capacity, 1, sections, home, across, beside
-    )
+        made_first, given_first, capacity, 1, sections, home, across, beside, ((), ())
+    )
+    held_second = after(held_second, made_first, given_first)
     beside_second = lax.ppermute(held_second, "expert", beside)
     second_mine = hidden_backward(held_second, stash_halves[0], down_rows)
     second_given = hidden_backward(beside_second, stash_halves[1], down_rows)
@@ -206,17 +245,25 @@
     given_second = made_backward(second_given, gate_cols, up_cols)
     made_second = lax.optimization_barrier(made_backward(second_mine, gate_cols, up_cols))
     back_second = collect(
-        made_second, given_second, capacity, -1, sections, home, across, beside
+        made_second,
+        given_second,
+        capacity,
+        -1,
+        sections,
+        home,
+        across,
+        beside,
+        ((tokens, grads, first_told, second_told), back_first),
     )
     first_branch = combine(
-        placement(first_told[0].astype(jnp.int32), slots), back_first, first_told[1][:, None]
+        placement(first_told[0].astype(jnp.int32), slots), jnp.concatenate(back_first), first_told[1][:, None]
     )
     second_branch = combine(
-        placement(second_told[0].astype(jnp.int32), slots), back_second, second_told[1][:, None]
-    )
-    mixed_out = (relayed_tokens.astype(jnp.float32) + first_branch).astype(jnp.bfloat16)
+        placement(second_told[0].astype(jnp.int32), slots), jnp.concatenate(back_second), second_told[1][:, None]
+    )
+    mixed_out = (tokens.astype(jnp.float32) + first_branch).astype(jnp.bfloat16)
     grad_out = (
-        second_told[2][:, None] * (relayed_grads.astype(jnp.float32) + second_branch)
+        second_told[2][:, None] * (grads.astype(jnp.float32) + second_branch)
     ).astype(jnp.bfloat16)
     return (mixed_out[None], grad_out[None])
 

time: 184 us -> 151 us (0.82)
  matrix products: 27.6 us -> 16 us
  waiting for transfers between devices: 80.1 us -> 68.5 us
  starting transfers between devices: 61.8 us -> 53.5 us
  other arithmetic: 5.91 us -> 2.54 us
  Pallas kernels: 0 us -> 3.11 us
    ppermute x2, waiting for transfers between devices: 29 us -> 12 us  [collect(): parts.insert(0, lax.ppermute(own, ('section', 'expert'), home(0, onward)))]
    ppermute x14, waiting for transfers between devices: 37.7 us -> 50.1 us  [the longest x2 28.6 us: collect(): near = near + lax.ppermute(far, 'expert', across).astype(jnp.float32)]
    dot_general x8 -> x0, matrix products: 11.8 us -> none  [picked(): jnp.dot(part, rows, preferred_element_type=jnp.float32).astype(jnp.bfloat16)]
    ppermute x2, waiting for transfers between devices: 13.4 us -> 4.15 us  [dispatch(): distant = lax.ppermute(near, 'expert', across)]
    ppermute x6, starting transfers between devices: 8.57 us -> 15.8 us  [collect(): lax.ppermute(piece, ('section', 'expert'), home(k + 1, onward))]
    ppermute x14, starting transfers between devices: 32.6 us -> 27.2 us  [the longest x6 16.2 us: dispatch(): lax.ppermute(pieces[k], 'expert', out(k))]
    ppermute x2, starting transfers between devices: 4.81 us -> 0.43 us  [dispatch(): distant = lax.ppermute(near, 'expert', across)]
    pallas_call x0 -> x1, Pallas kernels: none -> 3.11 us  [prepare(): pl.pallas_call(functools.partial(prepare_kernel, pairs, capacity), out_sh...]
  transfers between devices with their start and end apart: 30 -> 30, of which waited for: 8 -> 9; matrix products, arithmetic and copies ran while one was open for 18% -> 15% of each run, Pallas kernels for 0% -> 0%
where the time goes in v3:
time: 151 us
  waiting for transfers between devices  68.5 us (45%)
  starting transfers between devices  53.5 us (35%)
  matrix products  16 us (11%)
  local copies, waits for them, and re-layouts  5.8 us (4%)
  Pallas kernels  3.11 us (2%)
  other arithmetic  2.54 us (2%)
    ppermute x2, waiting for transfers between devices, collect(): near = near + lax.ppermute(far, 'expert', across).astype(jnp.float32)  28.6 us
    ppermute x6, starting transfers between devices, dispatch(): lax.ppermute(pieces[k], 'expert', out(k))  16.2 us
    ppermute x6, starting transfers between devices, collect(): lax.ppermute(piece, ('section', 'expert'), home(k + 1, onward))  15.8 us
    ppermute x6, waiting for transfers between devices, dispatch(): lax.ppermute(pieces[k], 'expert', out(k))  14 us
    ppermute x2, waiting for transfers between devices, collect(): parts.insert(0, lax.ppermute(own, ('section', 'expert'), home(0, onward)))  12 us
    ppermute x2, waiting for transfers between devices, dispatch(): own_distant = lax.ppermute(pieces[0], 'expert', across)  7.43 us
    ppermute x1, starting transfers between devices, local(): grads = lax.ppermute(grads, 'section', behind)  4.86 us
    ppermute x2, waiting for transfers between devices, dispatch(): distant = lax.ppermute(near, 'expert', across)  4.15 us
  transfers between devices with their start and end apart: 30, of which 9 were waited for; matrix products, arithmetic and copies ran while one was open for 15% of the time, Pallas kernels for 0%

profile of v3, /device:TPU:1, one launch (start us, length us, event | category | flops | bytes accessed | tf_op | source)
XLA Modules:
  0.0 150.6 jit_solution(4670955009449360941)
XLA Ops:
  0.7 3.1 %prepare.1 = (bf16[24,4096]{1,0:T(8,128)(2,1)}, bf16[24,4096]{1,0:T(8,128)(2,1)}, bf16[24,4096]{1,0:T(8,128)(2,1)}, bf16[24,4096]{1,0:T(8,128)(2,1)}, bf16[24,40...) custom-call(s32[1]{0:T(128)} %bitcast.2.chip_ref, ...), custom_call_target="tpu_custom_call" | custom-call | flops 100663296 | bytes 2097152 | tf_op jit(solution)/shard_map/prepare/pallas_call | solution.py:76
  3.8 6.4 %collective-permute-start.1 = (bf16[24,4096]{1,0:T(8,128)(2,1)}, bf16[24,4096]{1,0:T(8,128)(2,1)S(1)}, u32[]{:S(2)}, u32[]{:S(2)}) collective-permute-start(bf16[24,4096]{1,0:T(8,128)(2,1)} %get-tuple-element.34), channel_id=1, source_target_pairs={{14,0},{15,1},{4,2},{5,3},{2,4},{3,5},{8,6},{9,7},{6,8},{7,9},{12,... | collective-permute-start | bytes 589832 | tf_op jit(solution)/shard_map/ppermute | solution.py:133
  10.2 4.0 %collective-permute-start.3 = (bf16[24,4096]{1,0:T(8,128)(2,1)}, bf16[24,4096]{1,0:T(8,128)(2,1)}, u32[]{:S(2)}, u32[]{:S(2)}) collective-permute-start(bf16[24,4096]{1,0:T(8,128)(2,1)} %get-tuple-element.36), channel_id=1, source_target_pairs={{10,0},{11,1},{8,2},{9,3},{14,4},{15,5},{12,6},{13,7},{2,8},{3,9},... | collective-permute-start | bytes 589832 | tf_op jit(solution)/shard_map/ppermute | solution.py:133
  14.2 1.6 %constant_dynamic-update-slice_fusion.5 = bf16[192,4096]{1,0:T(8,128)(2,1)} fusion(bf16[24,4096]{1,0:T(8,128)(2,1)} %get-tuple-element.33), kind=kLoop, calls=%fused_computation.95 | loop fusion | bytes 393216
  15.8 1.6 %constant_dynamic-slice_fusion = (bf16[1,1,24,2,384]{4,3,2,1,0:T(2,128)(2,1)S(1)}, bf16[1,1,24,2,384]{4,3,2,1,0:T(2,128)(2,1)S(1)}, bf16[1,1,24,2,384]{4,3,2,1,0...) fusion(bf16[1,16,24,2,384]{4,3,2,1,0:T(2,128)(2,1)} %param.16, ...), kind=kLoop, calls=%fused_computation.122 | loop fusion | bytes 1179712 | tf_op jit(solution)/shard_map/jit(dynamic_index_in_dim)/dynamic_slice | solution.py:211
  17.8 7.4 %collective-permute-done = bf16[24,4096]{1,0:T(8,128)(2,1)} collective-permute-done((bf16[24,4096]{1,0:T(8,128)(2,1)}, bf16[24,4096]{1,0:T(8,128)(2,1)}, u32[]{:S(2)}, u32[]{:S(2)}) %collective-permute-start) | collective-permute-done | bytes 196640 | tf_op jit(solution)/shard_map/ppermute | solution.py:131
  25.2 1.7 %collective-permute-start.18 = (bf16[24,4096]{1,0:T(8,128)(2,1)S(1)}, bf16[24,4096]{1,0:T(8,128)(2,1)S(1)}, u32[]{:S(2)}, u32[]{:S(2)}) collective-permute-start(bf16[24,4096]{1,0:T(8,128)(2,1)S(1)} %copy-done.9), channel_id=1, source_target_pairs={{14,0},{15,1},{4,2},{5,3},{2,4},{3,5},{8,6},{9,7},{6,8},{7,9},{12,... | collective-permute-start | bytes 589832 | tf_op jit(solution)/shard_map/ppermute | solution.py:133
  28.0 3.0 %collective-permute-start.20 = (bf16[24,4096]{1,0:T(8,128)(2,1)S(1)}, bf16[24,4096]{1,0:T(8,128)(2,1)S(1)}, u32[]{:S(2)}, u32[]{:S(2)}) collective-permute-start(bf16[24,4096]{1,0:T(8,128)(2,1)S(1)} %copy-done.7), channel_id=1, source_target_pairs={{10,0},{11,1},{8,2},{9,3},{14,4},{15,5},{12,6},{13,7},{2,8},{3,9},... | collective-permute-start | bytes 589832 | tf_op jit(solution)/shard_map/ppermute | solution.py:133
  34.3 2.3 %collective-permute-done.19 = bf16[24,4096]{1,0:T(8,128)(2,1)S(1)} collective-permute-done((bf16[24,4096]{1,0:T(8,128)(2,1)S(1)}, bf16[24,4096]{1,0:T(8,128)(2,1)S(1)}, u32[]{:S(2)}, u32[]{:S(2)}) %collective-permute-start.19) | collective-permute-done | bytes 196640 | tf_op jit(solution)/shard_map/ppermute | solution.py:133
  36.6 11.7 %collective-permute-done.20 = bf16[24,4096]{1,0:T(8,128)(2,1)S(1)} collective-permute-done((bf16[24,4096]{1,0:T(8,128)(2,1)S(1)}, bf16[24,4096]{1,0:T(8,128)(2,1)S(1)}, u32[]{:S(2)}, u32[]{:S(2)}) %collective-permute-start.20) | collective-permute-done | bytes 196640 | tf_op jit(solution)/shard_map/ppermute | solution.py:133
  48.5 4.1 %collective-permute-done.4 = bf16[72,4096]{1,0:T(8,128)(2,1)S(1)} collective-permute-done((bf16[72,4096]{1,0:T(8,128)(2,1)S(1)}, bf16[72,4096]{1,0:T(8,128)(2,1)S(1)}, u32[]{:S(2)}, u32[]{:S(2)}) %collective-permute-start.4) | collective-permute-done | bytes 589856 | tf_op jit(solution)/shard_map/ppermute | solution.py:135
  52.7 2.4 %collective-permute-start.7 = (bf16[192,4096]{1,0:T(8,128)(2,1)S(1)}, bf16[192,4096]{1,0:T(8,128)(2,1)S(1)}, u32[]{:S(2)}, u32[]{:S(2)}) collective-permute-start(bf16[192,4096]{1,0:T(8,128)(2,1)S(1)} %constant_dynamic-update-slice_fusion), channel_id=1, source_target_pairs={{0,1},{1,0},{2,3},{3,2},{4,5},{5,4},{6,7},{7,6},{8,9},{9,8},{10,11... | collective-permute-start | bytes 4718600 | tf_op jit(solution)/shard_map/ppermute | solution.py:231
  56.5 3.8 %collective-permute-start.15 = (f32[3,64]{1,0:T(4,128)S(1)}, f32[3,64]{1,0:T(4,128)S(1)}, u32[]{:S(2)}, u32[]{:S(2)}) collective-permute-start(f32[3,64]{1,0:T(4,128)S(1)} %copy-done.10), channel_id=1, source_target_pairs={{16,0},{32,16},{48,32},{64,48},{80,64},{96,80},{112,96},{128,112},... | collective-permute-start | bytes 2312 | tf_op jit(solution)/shard_map/ppermute | solution.py:228
  62.4 4.9 %collective-permute-start.16 = (bf16[64,4096]{1,0:T(8,128)(2,1)S(1)}, bf16[64,4096]{1,0:T(8,128)(2,1)S(1)}, u32[]{:S(2)}, u32[]{:S(2)}) collective-permute-start(bf16[64,4096]{1,0:T(8,128)(2,1)S(1)} %bitcast.127), channel_id=1, source_target_pairs={{16,0},{32,16},{48,32},{64,48},{80,64},{96,80},{112,96},{128,112},... | collective-permute-start | bytes 1572872 | tf_op jit(solution)/shard_map/ppermute | solution.py:230
  75.1 1.6 %collective-permute-done.22 = bf16[192,4096]{1,0:T(8,128)(2,1)S(1)} collective-permute-done((bf16[192,4096]{1,0:T(8,128)(2,1)S(1)}, bf16[192,4096]{1,0:T(8,128)(2,1)S(1)}, u32[]{:S(2)}, u32[]{:S(2)}) %collective-permute-start.22) | collective-permute-done | bytes 1572896 | tf_op jit(solution)/shard_map/ppermute | solution.py:241
  80.7 1.3 fusion
  85.5 11.2 %collective-permute-done.10 = bf16[72,4096]{1,0:T(8,128)(2,1)S(1)} collective-permute-done((bf16[72,4096]{1,0:T(8,128)(2,1)S(1)}, bf16[72,4096]{1,0:T(8,128)(2,1)S(1)}, u32[]{:S(2)}, u32[]{:S(2)}) %collective-permute-start.10) | collective-permute-done | bytes 589856 | tf_op jit(solution)/shard_map/ppermute | solution.py:146
  97.9 2.8 %collective-permute-start.13 = (bf16[24,4096]{1,0:T(8,128)(2,1)S(1)}, bf16[24,4096]{1,0:T(8,128)(2,1)S(1)}, u32[]{:S(2)}, u32[]{:S(2)}) collective-permute-start(bf16[24,4096]{1,0:T(8,128)(2,1)S(1)} %get-tuple-element.89), channel_id=1, source_target_pairs={{0,28},{1,29},{2,22},{3,23},{4,16},{5,17},{6,26},{7,27},{8,20},{9,... | collective-permute-start | bytes 589832 | tf_op jit(solution)/shard_map/ppermute | solution.py:152
  101.5 3.9 %collective-permute-start.11 = (bf16[24,4096]{1,0:T(8,128)(2,1)S(1)}, bf16[24,4096]{1,0:T(8,128)(2,1)S(1)}, u32[]{:S(2)}, u32[]{:S(2)}) collective-permute-start(bf16[24,4096]{1,0:T(8,128)(2,1)S(1)} %fusion.45), channel_id=1, source_target_pairs={{0,16},{1,17},{2,18},{3,19},{4,20},{5,21},{6,22},{7,23},{8,24},{9,... | collective-permute-start | bytes 589832 | tf_op jit(solution)/shard_map/ppermute | solution.py:155
  105.5 17.4 %collective-permute-done.25 = bf16[72,4096]{1,0:T(8,128)(2,1)S(1)} collective-permute-done((bf16[72,4096]{1,0:T(8,128)(2,1)S(1)}, bf16[72,4096]{1,0:T(8,128)(2,1)S(1)}, u32[]{:S(2)}, u32[]{:S(2)}) %collective-permute-start.25) | collective-permute-done | bytes 589856 | tf_op jit(solution)/shard_map/ppermute | solution.py:146
  124.1 4.3 %collective-permute-start.27 = (bf16[24,4096]{1,0:T(8,128)(2,1)S(1)}, bf16[24,4096]{1,0:T(8,128)(2,1)S(1)}, u32[]{:S(2)}, u32[]{:S(2)}) collective-permute-start(bf16[24,4096]{1,0:T(8,128)(2,1)S(1)} %get-tuple-element.64), channel_id=1, source_target_pairs={{0,254},{1,255},{2,244},{3,245},{4,242},{5,243},{6,248},{7,249},{8... | collective-permute-start | bytes 589832 | tf_op jit(solution)/shard_map/ppermute | solution.py:152
  128.4 5.0 %collective-permute-start.29 = (bf16[24,4096]{1,0:T(8,128)(2,1)S(1)}, bf16[24,4096]{1,0:T(8,128)(2,1)S(1)}, u32[]{:S(2)}, u32[]{:S(2)}) collective-permute-start(bf16[24,4096]{1,0:T(8,128)(2,1)S(1)} %get-tuple-element.65), channel_id=1, source_target_pairs={{0,250},{1,251},{2,248},{3,249},{4,254},{5,255},{6,252},{7,253},{8... | collective-permute-start | bytes 589832 | tf_op jit(solution)/shard_map/ppermute | solution.py:152
  133.4 2.7 %collective-permute-start.28 = (bf16[24,4096]{1,0:T(8,128)(2,1)S(1)}, bf16[24,4096]{1,0:T(8,128)(2,1)S(1)}, u32[]{:S(2)}, u32[]{:S(2)}) collective-permute-start(bf16[24,4096]{1,0:T(8,128)(2,1)S(1)} %get-tuple-element.66), channel_id=1, source_target_pairs={{0,252},{1,253},{2,246},{3,247},{4,240},{5,241},{6,250},{7,251},{8... | collective-permute-start | bytes 589832 | tf_op jit(solution)/shard_map/ppermute | solution.py:152
  137.4 12.0 %collective-permute-done.26 = bf16[24,4096]{1,0:T(8,128)(2,1)S(1)} collective-permute-done((bf16[24,4096]{1,0:T(8,128)(2,1)S(1)}, bf16[24,4096]{1,0:T(8,128)(2,1)S(1)}, u32[]{:S(2)}, u32[]{:S(2)}) %collective-permute-start.26) | collective-permute-done | bytes 196640 | tf_op jit(solution)/shard_map/ppermute | solution.py:155
  (119 shorter events, 29.0 us)
Async XLA Ops:
  3.8 23.2 %collective-permute-start.1 = (bf16[24,4096]{1,0:T(8,128)(2,1)}, bf16[24,4096]{1,0:T(8,128)(2,1)S(1)}, u32[]{:S(2)}, u32[]{:S(2)}) collective-permute-start(bf16[24,4096]{1,0:T(8,128)(2,1)} %get-tuple-element.34), channel_id=1, source_target_pairs={{14,0},{15,1},{4,2},{5,3},{2,4},{3,5},{8,6},{9,7},{6,8},{7,9},{12,... | collective-permute-start | bytes 589832 | tf_op jit(solution)/shard_map/ppermute | solution.py:133
  10.2 17.8 %collective-permute-start.2 = (bf16[24,4096]{1,0:T(8,128)(2,1)}, bf16[24,4096]{1,0:T(8,128)(2,1)S(1)}, u32[]{:S(2)}, u32[]{:S(2)}) collective-permute-start(bf16[24,4096]{1,0:T(8,128)(2,1)} %get-tuple-element.35), channel_id=1, source_target_pairs={{12,0},{13,1},{6,2},{7,3},{0,4},{1,5},{10,6},{11,7},{4,8},{5,9},{1... | collective-permute-start | bytes 589832 | tf_op jit(solution)/shard_map/ppermute | solution.py:133
  10.2 20.8 %collective-permute-start.3 = (bf16[24,4096]{1,0:T(8,128)(2,1)}, bf16[24,4096]{1,0:T(8,128)(2,1)}, u32[]{:S(2)}, u32[]{:S(2)}) collective-permute-start(bf16[24,4096]{1,0:T(8,128)(2,1)} %get-tuple-element.36), channel_id=1, source_target_pairs={{10,0},{11,1},{8,2},{9,3},{14,4},{15,5},{12,6},{13,7},{2,8},{3,9},... | collective-permute-start | bytes 589832 | tf_op jit(solution)/shard_map/ppermute | solution.py:133
  25.2 23.2 %collective-permute-start.17 = (bf16[24,4096]{1,0:T(8,128)(2,1)S(1)}, bf16[24,4096]{1,0:T(8,128)(2,1)S(1)}, u32[]{:S(2)}, u32[]{:S(2)}) collective-permute-start(bf16[24,4096]{1,0:T(8,128)(2,1)S(1)} %copy-done.6), channel_id=1, source_target_pairs={{0,2},{1,3},{2,0},{3,1},{4,6},{5,7},{6,4},{7,5},{8,10},{9,11},{10,... | collective-permute-start | bytes 589832 | tf_op jit(solution)/shard_map/ppermute | solution.py:131
  28.0 20.3 %collective-permute-start.20 = (bf16[24,4096]{1,0:T(8,128)(2,1)S(1)}, bf16[24,4096]{1,0:T(8,128)(2,1)S(1)}, u32[]{:S(2)}, u32[]{:S(2)}) collective-permute-start(bf16[24,4096]{1,0:T(8,128)(2,1)S(1)} %copy-done.7), channel_id=1, source_target_pairs={{10,0},{11,1},{8,2},{9,3},{14,4},{15,5},{12,6},{13,7},{2,8},{3,9},... | collective-permute-start | bytes 589832 | tf_op jit(solution)/shard_map/ppermute | solution.py:133
  32.0 20.7 %collective-permute-start.4 = (bf16[72,4096]{1,0:T(8,128)(2,1)S(1)}, bf16[72,4096]{1,0:T(8,128)(2,1)S(1)}, u32[]{:S(2)}, u32[]{:S(2)}) collective-permute-start(bf16[72,4096]{1,0:T(8,128)(2,1)S(1)} %pad_maximum_fusion), channel_id=1, source_target_pairs={{0,2},{1,3},{2,0},{3,1},{4,6},{5,7},{6,4},{7,5},{8,10},{9,11},{10,... | collective-permute-start | bytes 1769480 | tf_op jit(solution)/shard_map/ppermute | solution.py:135
  48.3 23.0 %collective-permute-start.21 = (bf16[72,4096]{1,0:T(8,128)(2,1)S(1)}, bf16[72,4096]{1,0:T(8,128)(2,1)S(1)}, u32[]{:S(2)}, u32[]{:S(2)}) collective-permute-start(bf16[72,4096]{1,0:T(8,128)(2,1)S(1)} %pad_maximum_fusion.1), channel_id=1, source_target_pairs={{0,2},{1,3},{2,0},{3,1},{4,6},{5,7},{6,4},{7,5},{8,10},{9,11},{10,... | collective-permute-start | bytes 1769480 | tf_op jit(solution)/shard_map/ppermute | solution.py:135
  55.2 15.2 %collective-permute-start.6 = (f32[2,64]{1,0:T(2,128)S(1)}, f32[2,64]{1,0:T(2,128)S(1)}, u32[]{:S(2)}, u32[]{:S(2)}) collective-permute-start(f32[2,64]{1,0:T(2,128)S(1)} %copy-done.11), channel_id=1, source_target_pairs={{0,16},{16,32},{32,48},{48,64},{64,80},{80,96},{96,112},{112,128},... | collective-permute-start | bytes 1544 | tf_op jit(solution)/shard_map/ppermute | solution.py:227
  56.5 16.1 %collective-permute-start.15 = (f32[3,64]{1,0:T(4,128)S(1)}, f32[3,64]{1,0:T(4,128)S(1)}, u32[]{:S(2)}, u32[]{:S(2)}) collective-permute-start(f32[3,64]{1,0:T(4,128)S(1)} %copy-done.10), channel_id=1, source_target_pairs={{16,0},{32,16},{48,32},{64,48},{80,64},{96,80},{112,96},{128,112},... | collective-permute-start | bytes 2312 | tf_op jit(solution)/shard_map/ppermute | solution.py:228
  60.3 41.1 %collective-permute-start.5 = (bf16[64,4096]{1,0:T(8,128)(2,1)S(1)}, bf16[64,4096]{1,0:T(8,128)(2,1)S(1)}, u32[]{:S(2)}, u32[]{:S(2)}) collective-permute-start(bf16[64,4096]{1,0:T(8,128)(2,1)S(1)} %bitcast.125), channel_id=1, source_target_pairs={{0,16},{16,32},{32,48},{48,64},{64,80},{80,96},{96,112},{112,128},... | collective-permute-start | bytes 1572872 | tf_op jit(solution)/shard_map/ppermute | solution.py:229
  62.4 39.0 %collective-permute-start.16 = (bf16[64,4096]{1,0:T(8,128)(2,1)S(1)}, bf16[64,4096]{1,0:T(8,128)(2,1)S(1)}, u32[]{:S(2)}, u32[]{:S(2)}) collective-permute-start(bf16[64,4096]{1,0:T(8,128)(2,1)S(1)} %bitcast.127), channel_id=1, source_target_pairs={{16,0},{32,16},{48,32},{64,48},{80,64},{96,80},{112,96},{128,112},... | collective-permute-start | bytes 1572872 | tf_op jit(solution)/shard_map/ppermute | solution.py:230
  77.9 19.1 %collective-permute-start.9 = (bf16[24,4096]{1,0:T(8,128)(2,1)S(1)}, bf16[24,4096]{1,0:T(8,128)(2,1)S(1)}, u32[]{:S(2)}, u32[]{:S(2)}) collective-permute-start(bf16[24,4096]{1,0:T(8,128)(2,1)S(1)} %slice.97), channel_id=1, source_target_pairs={{0,2},{1,3},{2,0},{3,1},{4,6},{5,7},{6,4},{7,5},{8,10},{9,11},{10,... | collective-permute-start | bytes 589832 | tf_op jit(solution)/shard_map/ppermute | solution.py:148
  78.4 18.3 %collective-permute-start.10 = (bf16[72,4096]{1,0:T(8,128)(2,1)S(1)}, bf16[72,4096]{1,0:T(8,128)(2,1)S(1)}, u32[]{:S(2)}, u32[]{:S(2)}) collective-permute-start(bf16[72,4096]{1,0:T(8,128)(2,1)S(1)} %slice.99), channel_id=1, source_target_pairs={{0,2},{1,3},{2,0},{3,1},{4,6},{5,7},{6,4},{7,5},{8,10},{9,11},{10,... | collective-permute-start | bytes 1769480 | tf_op jit(solution)/shard_map/ppermute | solution.py:146
  84.5 13.4 %collective-permute-start.23 = (bf16[192,4096]{1,0:T(8,128)(2,1)S(1)}, bf16[192,4096]{1,0:T(8,128)(2,1)S(1)}, u32[]{:S(2)}, u32[]{:S(2)}) collective-permute-start(bf16[192,4096]{1,0:T(8,128)(2,1)S(1)} %fusion.1), channel_id=1, source_target_pairs={{0,1},{1,0},{2,3},{3,2},{4,5},{5,4},{6,7},{7,6},{8,9},{9,8},{10,11... | collective-permute-start | bytes 4718600 | tf_op jit(solution)/shard_map/ppermute | solution.py:140
  96.9 27.2 %collective-permute-start.12 = (bf16[24,4096]{1,0:T(8,128)(2,1)S(1)}, bf16[24,4096]{1,0:T(8,128)(2,1)S(1)}, u32[]{:S(2)}, u32[]{:S(2)}) collective-permute-start(bf16[24,4096]{1,0:T(8,128)(2,1)S(1)} %get-tuple-element.87), channel_id=1, source_target_pairs={{0,30},{1,31},{2,20},{3,21},{4,18},{5,19},{6,24},{7,25},{8,22},{9,... | collective-permute-start | bytes 589832 | tf_op jit(solution)/shard_map/ppermute | solution.py:152
  97.0 27.1 %collective-permute-start.14 = (bf16[24,4096]{1,0:T(8,128)(2,1)S(1)}, bf16[24,4096]{1,0:T(8,128)(2,1)S(1)}, u32[]{:S(2)}, u32[]{:S(2)}) collective-permute-start(bf16[24,4096]{1,0:T(8,128)(2,1)S(1)} %get-tuple-element.88), channel_id=1, source_target_pairs={{0,26},{1,27},{2,24},{3,25},{4,30},{5,31},{6,28},{7,29},{8,18},{9,... | collective-permute-start | bytes 589832 | tf_op jit(solution)/shard_map/ppermute | solution.py:152
  97.9 26.2 %collective-permute-start.13 = (bf16[24,4096]{1,0:T(8,128)(2,1)S(1)}, bf16[24,4096]{1,0:T(8,128)(2,1)S(1)}, u32[]{:S(2)}, u32[]{:S(2)}) collective-permute-start(bf16[24,4096]{1,0:T(8,128)(2,1)S(1)} %get-tuple-element.89), channel_id=1, source_target_pairs={{0,28},{1,29},{2,22},{3,23},{4,16},{5,17},{6,26},{7,27},{8,20},{9,... | collective-permute-start | bytes 589832 | tf_op jit(solution)/shard_map/ppermute | solution.py:152
  101.4 21.5 %collective-permute-start.25 = (bf16[72,4096]{1,0:T(8,128)(2,1)S(1)}, bf16[72,4096]{1,0:T(8,128)(2,1)S(1)}, u32[]{:S(2)}, u32[]{:S(2)}) collective-permute-start(bf16[72,4096]{1,0:T(8,128)(2,1)S(1)} %slice.110), channel_id=1, source_target_pairs={{0,2},{1,3},{2,0},{3,1},{4,6},{5,7},{6,4},{7,5},{8,10},{9,11},{10,... | collective-permute-start | bytes 1769480 | tf_op jit(solution)/shard_map/ppermute | solution.py:146
  101.5 22.5 %collective-permute-start.11 = (bf16[24,4096]{1,0:T(8,128)(2,1)S(1)}, bf16[24,4096]{1,0:T(8,128)(2,1)S(1)}, u32[]{:S(2)}, u32[]{:S(2)}) collective-permute-start(bf16[24,4096]{1,0:T(8,128)(2,1)S(1)} %fusion.45), channel_id=1, source_target_pairs={{0,16},{1,17},{2,18},{3,19},{4,20},{5,21},{6,22},{7,23},{8,24},{9,... | collective-permute-start | bytes 589832 | tf_op jit(solution)/shard_map/ppermute | solution.py:155
  122.9 13.2 %collective-permute-start.24 = (bf16[24,4096]{1,0:T(8,128)(2,1)S(1)}, bf16[24,4096]{1,0:T(8,128)(2,1)S(1)}, u32[]{:S(2)}, u32[]{:S(2)}) collective-permute-start(bf16[24,4096]{1,0:T(8,128)(2,1)S(1)} %slice.108), channel_id=1, source_target_pairs={{0,2},{1,3},{2,0},{3,1},{4,6},{5,7},{6,4},{7,5},{8,10},{9,11},{10,... | collective-permute-start | bytes 589832 | tf_op jit(solution)/shard_map/ppermute | solution.py:148
  124.1 25.3 %collective-permute-start.27 = (bf16[24,4096]{1,0:T(8,128)(2,1)S(1)}, bf16[24,4096]{1,0:T(8,128)(2,1)S(1)}, u32[]{:S(2)}, u32[]{:S(2)}) collective-permute-start(bf16[24,4096]{1,0:T(8,128)(2,1)S(1)} %get-tuple-element.64), channel_id=1, source_target_pairs={{0,254},{1,255},{2,244},{3,245},{4,242},{5,243},{6,248},{7,249},{8... | collective-permute-start | bytes 589832 | tf_op jit(solution)/shard_map/ppermute | solution.py:152
  128.4 21.0 %collective-permute-start.29 = (bf16[24,4096]{1,0:T(8,128)(2,1)S(1)}, bf16[24,4096]{1,0:T(8,128)(2,1)S(1)}, u32[]{:S(2)}, u32[]{:S(2)}) collective-permute-start(bf16[24,4096]{1,0:T(8,128)(2,1)S(1)} %get-tuple-element.65), channel_id=1, source_target_pairs={{0,250},{1,251},{2,248},{3,249},{4,254},{5,255},{6,252},{7,253},{8... | collective-permute-start | bytes 589832 | tf_op jit(solution)/shard_map/ppermute | solution.py:152
  133.4 16.0 %collective-permute-start.28 = (bf16[24,4096]{1,0:T(8,128)(2,1)S(1)}, bf16[24,4096]{1,0:T(8,128)(2,1)S(1)}, u32[]{:S(2)}, u32[]{:S(2)}) collective-permute-start(bf16[24,4096]{1,0:T(8,128)(2,1)S(1)} %get-tuple-element.66), channel_id=1, source_target_pairs={{0,252},{1,253},{2,246},{3,247},{4,240},{5,241},{6,250},{7,251},{8... | collective-permute-start | bytes 589832 | tf_op jit(solution)/shard_map/ppermute | solution.py:152
  136.1 13.3 %collective-permute-start.26 = (bf16[24,4096]{1,0:T(8,128)(2,1)S(1)}, bf16[24,4096]{1,0:T(8,128)(2,1)S(1)}, u32[]{:S(2)}, u32[]{:S(2)}) collective-permute-start(bf16[24,4096]{1,0:T(8,128)(2,1)S(1)} %fusion.44), channel_id=1, source_target_pairs={{0,240},{1,241},{2,242},{3,243},{4,244},{5,245},{6,246},{7,247},{8... | collective-permute-start | bytes 589832 | tf_op jit(solution)/shard_map/ppermute | solution.py:155
  (18 other events, 219.3 us)

commit v4 on v3

--- a/solution.py
+++ b/solution.py
@@ -8,6 +8,9 @@
 from jax.sharding import PartitionSpec as P
 
 REACH = 4
+EDGES = [['jB', 'own_d'], ['fwdB', 'rB'], ['relayB', 'jB1'], ['gF', 'rB'], ['heldF', 'closeB'], ['mF', 'gF'], ['distB', 'gF'], ['homeF', 'payB'], ['homeB', 'h2F'], ['homeB', 'h3F']]
+RELAY = 0
+MERGE = True
 
 
 def routes(devices, sections):
@@ -53,20 +56,34 @@
         )
         slot = jnp.sum(chosen * earlier, axis=0, keepdims=True).astype(jnp.int32)
         place = step * capacity + slot
-        for k, part in enumerate(parts):
+        for k, (part, start) in enumerate(parts):
             here = lax.broadcasted_iota(jnp.int32, (capacity, count), 0) + k * capacity == place
             here = jnp.where(here, keep, 0.0).astype(jnp.bfloat16)
-            part[...] = jnp.dot(here, rows, preferred_element_type=jnp.float32).astype(part.dtype)
+            made = jnp.dot(here, rows, preferred_element_type=jnp.float32)
+            part[start : start + capacity, :] = made.astype(part.dtype)
         return place.astype(jnp.float32)
 
     ids1, gates1, ids2, gates2, keep, rows1, rows2 = refs[:7]
-    outs = refs[7:]
+    own, near1, near2, told1, told2 = refs[7], refs[8:11], refs[11:14], refs[14], refs[15]
     kept = keep[...].astype(jnp.float32)
-    outs[8][0:1, :] = fill(ids1[...], rows1[...], jnp.ones_like(kept), outs[:REACH])
-    outs[8][1:2, :] = gates1[...]
-    outs[9][0:1, :] = fill(ids2[...], rows2[...], kept, outs[REACH : 2 * REACH])
-    outs[9][1:2, :] = gates2[...]
-    outs[9][2:3, :] = kept
+    parts1 = [(own, 0)] + [(part, 0) for part in near1]
+    parts2 = [(own, capacity)] + [(part, 0) for part in near2]
+    place1 = fill(ids1[...], rows1[...], jnp.ones_like(kept), parts1)
+    place2 = fill(ids2[...], rows2[...], kept, parts2)
+
+    def tell(told, place, gates):
+        high = gates.astype(jnp.bfloat16).astype(jnp.float32)
+        middle = (gates - high).astype(jnp.bfloat16).astype(jnp.float32)
+        low = gates - high - middle
+        row = lax.broadcasted_iota(jnp.int32, (8, count), 0)
+        lines = jnp.zeros((8, count), jnp.float32)
+        for k, line in enumerate((place, high, middle, low, kept)):
+            lines = jnp.where(row == k, line, lines)
+        told[...] = jnp.zeros_like(told)
+        told[:, 0:count] = lines.astype(told.dtype)
+
+    tell(told1, place1, gates1[...])
+    tell(told2, place2, gates2[...])
 
 
 def prepare(chip, pairs, capacity, ids1, gates1, ids2, gates2, keep, rows1, rows2):
@@ -75,19 +92,20 @@
     whole = pl.BlockSpec(memory_space=pltpu.VMEM)
     made = pl.pallas_call(
         functools.partial(prepare_kernel, pairs, capacity),
-        out_shape=[piece] * (2 * REACH)
+        out_shape=[jax.ShapeDtypeStruct((2 * capacity, width), jnp.bfloat16)]
+        + [piece] * (2 * REACH - 2)
         + [
-            jax.ShapeDtypeStruct((2, count), jnp.float32),
-            jax.ShapeDtypeStruct((3, count), jnp.float32),
+            jax.ShapeDtypeStruct((8, width), jnp.bfloat16),
+            jax.ShapeDtypeStruct((8, width), jnp.bfloat16),
         ],
         in_specs=[pl.BlockSpec(memory_space=pltpu.SMEM)] + [whole] * 7,
-        out_specs=[whole] * (2 * REACH + 2),
+        out_specs=[whole] * (2 * REACH + 1),
         cost_estimate=pl.CostEstimate(
             flops=4 * REACH * capacity * count * width, bytes_accessed=8 * count * width, transcendentals=0
         ),
         name="prepare",
     )(chip[None], ids1, gates1, ids2, gates2, keep, rows1, rows2)
-    return made[:REACH], made[REACH : 2 * REACH], made[8], made[9]
+    return made[0], made[1:REACH], made[REACH : 2 * REACH - 1], made[-2], made[-1]
 
 
 def placement(slot_at, slot_total):
@@ -127,33 +145,24 @@
     return total.astype(jnp.bfloat16)
 
 
-def dispatch(pieces, out, across):
-    own_distant = lax.ppermute(pieces[0], "expert", across)
-    near = jnp.concatenate(
-        [lax.ppermute(pieces[k], "expert", out(k)) for k in range(1, REACH)], axis=0
-    )
-    distant = lax.ppermute(near, "expert", across)
-    return jnp.concatenate([pieces[0], own_distant, near, distant], axis=0), own_distant
-
-
-def collect(mine, given, capacity, onward, sections, home, across, beside, earlier):
-    came = lax.ppermute(given, "expert", beside)
+def collect(mine, came, capacity, onward, home):
     summed = mine.astype(jnp.float32) + came.astype(jnp.float32)
-    own_near, own_far = summed[:capacity], summed[capacity : 2 * capacity]
-    width = (REACH - 1) * capacity
-    near, far = summed[2 * capacity : 2 * capacity + width], summed[2 * capacity + width :]
-    far = after(far.astype(jnp.bfloat16), *earlier[0])
-    near = near + lax.ppermute(far, "expert", across).astype(jnp.float32)
-    near = after(near.astype(jnp.bfloat16), *earlier[1])
-    own_came = lax.ppermute(own_far.astype(jnp.bfloat16), "expert", across)
-    pieces = [near[k * capacity : (k + 1) * capacity] for k in range(REACH - 1)]
-    own = (own_near + after(own_came, *pieces).astype(jnp.float32)).astype(jnp.bfloat16)
-    parts = [
-        lax.ppermute(piece, ("section", "expert"), home(k + 1, onward))
-        for k, piece in enumerate(pieces)
-    ]
-    parts.insert(0, lax.ppermute(own, ("section", "expert"), home(0, onward)))
-    return parts
+    width = 2 * capacity
+
+    def sent(k):
+        return summed[(REACH + k) * capacity :][:width].astype(jnp.bfloat16)
+
+    def kept(k, arrived):
+        total = summed[k * capacity :][:width] + arrived.astype(jnp.float32)
+        return total.astype(jnp.bfloat16)
+
+    def homeward(pieces, k):
+        return [
+            lax.ppermute(pieces[i * capacity :][:capacity], ("section", "expert"), home(k + i, onward))
+            for i in (1, 0)
+        ][::-1]
+
+    return sent, kept, homeward
 
 
 def combine(placed, back, gate_values):
@@ -188,7 +197,7 @@
     chip, core = me // 2, me % 2
     ahead = [(i, (i + 1) % sections) for i in range(sections)]
     behind = [((i + 1) % sections, i) for i in range(sections)]
-    first_pieces, second_pieces, first_told, second_told = prepare(
+    own_pieces, first_near, second_near, first_told, second_told = prepare(
         chip,
         pairs,
         capacity,
@@ -204,7 +213,7 @@
         [(here + jnp.where(here % 2 == 0, -step, step)) % chips for step in range(REACH)]
         for here in (chip, chip ^ 1)
     ]
-    origins = [origins[0][0], origins[1][0], *origins[0][1:], *origins[1][1:]]
+    origins = origins[0] + origins[1]
     stash_halves = [
         jnp.concatenate(
             [
@@ -218,53 +227,134 @@
     up_cols = up_weight[0]
     down_rows = down_weight[0]
 
-    held_first, own_distant = dispatch(first_pieces, out, across)
-    second_pieces = lax.optimization_barrier((*second_pieces, own_distant))[:REACH]
-    held_second, _ = dispatch(second_pieces, out, across)
-    tokens, grads, first_told, second_told, _ = lax.optimization_barrier(
-        (layer_input[0], cotangent[0], first_told, second_told, held_first)
-    )
-    first_told = lax.ppermute(first_told, "section", ahead)
-    second_told = lax.ppermute(second_told, "section", behind)
-    tokens = lax.ppermute(tokens, "section", ahead)
-    grads = lax.ppermute(grads, "section", behind)
+    V = {}
+
+    def gate(name, value):
+        for target, source in EDGES:
+            if target == name:
+                value = after(value, V[source])
+        return value
+
+    V["own_d"] = own_distant = lax.ppermute(own_pieces, "expert", across)
+    first_near = [
+        lax.ppermute(gate(f"jF{k + 1}", piece), "expert", out(k + 1)) for k, piece in enumerate(first_near)
+    ]
+    V["jF1"], V["jF2"], V["jF3"] = first_near
+    second_near = [gate(f"jB{k + 1}", gate("jB", piece)) for k, piece in enumerate(second_near)]
+    second_near = [
+        lax.ppermute(piece, "expert", out(k + 1)) for k, piece in enumerate(second_near)
+    ]
+    V["jB1"], V["jB2"], V["jB3"] = second_near
+    first_close = gate("fwdF", jnp.concatenate(first_near))
+    first_distant = lax.ppermute(first_close, "expert", across)
+    V["fwdF"] = first_distant
+    relay_done = False
+
+    bundles = [
+        jnp.concatenate((rows[0], told))
+        for rows, told in ((layer_input, first_told), (cotangent, second_told))
+    ]
+
+    def relay(first, second):
+        if not MERGE:
+            first = lax.ppermute(gate("relayF", first), "section", ahead)
+            V["rF"] = first
+        V["rB"] = second = lax.ppermute(gate("relayB", second), "section", behind)
+        return first, second
+
+    told = bundles
+    if RELAY == 0:
+        told = relay(*told)
+    V["closeB"] = second_close = gate("fwdB", jnp.concatenate(second_near))
+    second_distant = lax.ppermute(second_close, "expert", across)
+    V["fwdB"] = second_distant
+    if RELAY == 1:
+        told = relay(*told)
+    held_first = jnp.concatenate(
+        [own_pieces[:capacity], *first_near, own_distant[:capacity], first_distant]
+    )
+    V["heldF"] = held_first = gate("heldF", held_first)
+    if RELAY == 2:
+        told = relay(*told)
     beside_first = lax.ppermute(held_first, "expert", beside)
-    first_mine = hidden_forward(held_first, gate_cols, up_cols)
-    first_given = hidden_forward(beside_first, gate_cols, up_cols)
+    V["coreF"] = beside_first
+    first_mine = hidden_forward(gate("hmF", held_first), gate_cols, up_cols)
+    V["hmF"] = first_mine[0]
+    if RELAY == 3:
+        told = relay(*told)
+    first_given = hidden_forward(gate("hgF", beside_first), gate_cols, up_cols)
+    V["hgF"] = first_given[0]
     first_mine, first_given = lax.optimization_barrier((first_mine, first_given))
-    given_first = made_forward(first_given, down_rows)
-    made_first = lax.optimization_barrier(made_forward(first_mine, down_rows))
-    back_first = collect(
-        made_first, given_first, capacity, 1, sections, home, across, beside, ((), ())
-    )
-    held_second = after(held_second, made_first, given_first)
+    given_first = made_forward((gate("gF", first_given[0]),), down_rows)
+    V["gF"] = given_first
+    if RELAY == 4:
+        told = relay(*told)
+    came_first = lax.ppermute(given_first, "expert", beside)
+    V["cF"] = came_first
+    made_first = lax.optimization_barrier(made_forward((gate("mF", first_mine[0]),), down_rows))
+    V["mF"] = made_first
+
+    second_distant = gate("distB", second_distant)
+    held_second = jnp.concatenate(
+        [own_pieces[capacity:], *second_near, own_distant[capacity:], second_distant]
+    )
+    V["heldB"] = held_second = gate("heldB", held_second)
     beside_second = lax.ppermute(held_second, "expert", beside)
-    second_mine = hidden_backward(held_second, stash_halves[0], down_rows)
-    second_given = hidden_backward(beside_second, stash_halves[1], down_rows)
+    V["coreB"] = beside_second
+    second_mine = hidden_backward(gate("hmB", held_second), stash_halves[0], down_rows)
+    V["hmB"] = second_mine[0]
+    second_given = hidden_backward(gate("hgB", beside_second), stash_halves[1], down_rows)
     second_mine, second_given = lax.optimization_barrier((second_mine, second_given))
     given_second = made_backward(second_given, gate_cols, up_cols)
+    V["gB"] = given_second
+    came_second = lax.ppermute(given_second, "expert", beside)
+    V["cB"] = came_second
+    second_mine = (gate("mB", second_mine[0]), second_mine[1])
     made_second = lax.optimization_barrier(made_backward(second_mine, gate_cols, up_cols))
-    back_second = collect(
-        made_second,
-        given_second,
-        capacity,
-        -1,
-        sections,
-        home,
-        across,
-        beside,
-        ((tokens, grads, first_told, second_told), back_first),
-    )
-    first_branch = combine(
-        placement(first_told[0].astype(jnp.int32), slots), jnp.concatenate(back_first), first_told[1][:, None]
-    )
-    second_branch = combine(
-        placement(second_told[0].astype(jnp.int32), slots), jnp.concatenate(back_second), second_told[1][:, None]
-    )
-    mixed_out = (tokens.astype(jnp.float32) + first_branch).astype(jnp.bfloat16)
-    grad_out = (
-        second_told[2][:, None] * (grads.astype(jnp.float32) + second_branch)
-    ).astype(jnp.bfloat16)
+
+    sent, kept, homeward = collect(made_first, came_first, capacity, 1, home)
+    sent2, kept2, homeward2 = collect(made_second, came_second, capacity, -1, home)
+    far = lax.ppermute(gate("farF", sent(2)), "expert", across)
+    V["farF"] = far
+    if RELAY == 5:
+        told = relay(*told)
+    V["payB"] = far2 = gate("farB", sent2(2))
+    short = lax.ppermute(gate("shortF", sent(0)), "expert", across)
+    V["shortF"] = short
+    V["piecesF"] = pieces = gate("homeF", kept(2, far))
+    back_first = homeward(pieces, 2)
+    V["h2F"], V["h3F"] = back_first
+    far2 = lax.ppermute(far2, "expert", across)
+    V["farB"] = far2
+    last = gate("home0F", kept(0, after(short, pieces)))
+    if MERGE:
+        bundle = jnp.concatenate((last[:capacity], bundles[0]))
+        bundle = lax.ppermute(bundle, ("section", "expert"), home(0, 1))
+        one = lax.ppermute(last[capacity:], ("section", "expert"), home(1, 1))
+        back_first = [bundle[:capacity], one] + back_first
+        told = (bundle[capacity:], told[1])
+    else:
+        back_first = homeward(last, 0) + back_first
+    V["h0F"], V["h1F"] = back_first[:2]
+    short2 = lax.ppermute(gate("shortB", sent2(0)), "expert", across)
+    pieces = gate("homeB", kept2(2, far2))
+    back_second = homeward2(pieces, 2)
+    V["h2B"], V["h3B"] = back_second
+    pieces = gate("home0B", kept2(0, after(short2, pieces)))
+    back_second = homeward2(pieces, 0) + back_second
+    count = layer_input.shape[1]
+
+    def unpack(bundle, back):
+        lines = bundle[count:, :count].astype(jnp.float32)
+        gates = (lines[1] + lines[2]) + lines[3]
+        rows = jnp.concatenate(back)
+        branch = combine(placement(lines[0].astype(jnp.int32), slots), rows, gates[:, None])
+        return branch, bundle[:count].astype(jnp.float32), lines[4][:, None]
+
+    first_branch, tokens, _ = unpack(told[0], back_first)
+    second_branch, grads, keep = unpack(told[1], back_second)
+    mixed_out = (tokens + first_branch).astype(jnp.bfloat16)
+    grad_out = (keep * (grads + second_branch)).astype(jnp.bfloat16)
     return (mixed_out[None], grad_out[None])
 
 

time: 151 us -> 151 us (level)
  waiting for transfers between devices: 68.5 us -> 55.6 us
  starting transfers between devices: 53.5 us -> 63.9 us
  other arithmetic: 2.54 us -> 4.55 us
    ppermute x28 -> x24, waiting for transfers between devices: 66.9 us -> 54.6 us  [the longest x1 14.4 us: local(): far2 = lax.ppermute(far2, 'expert', across)]
    ppermute x28 -> x24, starting transfers between devices: 51 us -> 57.5 us  [the longest x6 30.7 us: homeward(): lax.ppermute(pieces[i * capacity:][:capacity], ('section', 'expert'), hom...]
    ppermute x1, starting transfers between devices: 2.4 us -> 5.55 us  [local(): beside_first = lax.ppermute(held_first, 'expert', beside)]
    concatenate x2 -> x4, other arithmetic: 1.01 us -> 3.01 us  [the longest x1 1.93 us: local(): jnp.concatenate((rows[0], told))]
    unnamed x47 -> x41, local copies, waits for them, and re-layouts: 3.87 us -> 4.78 us
  transfers between devices with their start and end apart: 30 -> 26, of which waited for: 9 -> 10; matrix products, arithmetic and copies ran while one was open for 15% -> 17% of each run, Pallas kernels for 0% -> 0%
where the time goes in v4:
time: 151 us
  starting transfers between devices  63.9 us (42%)
  waiting for transfers between devices  55.6 us (37%)
  matrix products  15.7 us (10%)
  local copies, waits for them, and re-layouts  6.69 us (4%)
  other arithmetic  4.55 us (3%)
  Pallas kernels  3.15 us (2%)
    ppermute x6, starting transfers between devices, homeward(): lax.ppermute(pieces[i * capacity:][:capacity], ('section', 'expert'), hom...  30.7 us
    ppermute x1, waiting for transfers between devices, local(): far2 = lax.ppermute(far2, 'expert', across)  14.4 us
    ppermute x3, waiting for transfers between devices, local(): lax.ppermute(piece, 'expert', out(k + 1))  9.14 us
    ppermute x3, starting transfers between devices, local(): lax.ppermute(gate(f'jF{k + 1}', piece), 'expert', out(k + 1))  8.68 us
    ppermute x3, waiting for transfers between devices, local(): lax.ppermute(gate(f'jF{k + 1}', piece), 'expert', out(k + 1))  7.85 us
    ppermute x1, waiting for transfers between devices, local(): second_distant = lax.ppermute(second_close, 'expert', across)  7.83 us
    ppermute x3, starting transfers between devices, local(): lax.ppermute(piece, 'expert', out(k + 1))  6.34 us
    ppermute x1, starting transfers between devices, local(): beside_first = lax.ppermute(held_first, 'expert', beside)  5.55 us
  transfers between devices with their start and end apart: 26, of which 10 were waited for; matrix products, arithmetic and copies ran while one was open for 17% of the time, Pallas kernels for 0%

profile of v4, /device:TPU:1, one launch (start us, length us, event | category | flops | bytes accessed | tf_op | source)
XLA Modules:
  0.0 150.9 jit_solution(1705474994986733496)
XLA Ops:
  0.7 3.1 %prepare.1 = (bf16[48,4096]{1,0:T(8,128)(2,1)}, bf16[24,4096]{1,0:T(8,128)(2,1)}, bf16[24,4096]{1,0:T(8,128)(2,1)}, bf16[24,4096]{1,0:T(8,128)(2,1)}, bf16[24,40...) custom-call(s32[1]{0:T(128)} %bitcast.chip_ref, ...), custom_call_target="tpu_custom_call" | custom-call | flops 100663296 | bytes 2097152 | tf_op jit(solution)/shard_map/prepare/pallas_call | solution.py:93
  3.8 2.5 %collective-permute-start.3 = (bf16[48,4096]{1,0:T(8,128)(2,1)}, bf16[48,4096]{1,0:T(8,128)(2,1)}, u32[]{:S(2)}, u32[]{:S(2)}) collective-permute-start(bf16[48,4096]{1,0:T(8,128)(2,1)} %get-tuple-element.31), channel_id=1, source_target_pairs={{0,2},{1,3},{2,0},{3,1},{4,6},{5,7},{6,4},{7,5},{8,10},{9,11},{10,... | collective-permute-start | bytes 1179656 | tf_op jit(solution)/shard_map/ppermute | solution.py:238
  6.3 4.7 %collective-permute-start = (bf16[24,4096]{1,0:T(8,128)(2,1)}, bf16[24,4096]{1,0:T(8,128)(2,1)S(1)}, u32[]{:S(2)}, u32[]{:S(2)}) collective-permute-start(bf16[24,4096]{1,0:T(8,128)(2,1)} %get-tuple-element.32), channel_id=1, source_target_pairs={{14,0},{15,1},{4,2},{5,3},{2,4},{3,5},{8,6},{9,7},{6,8},{7,9},{12,... | collective-permute-start | bytes 589832 | tf_op jit(solution)/shard_map/ppermute | solution.py:240
  10.9 4.0 %collective-permute-start.2 = (bf16[24,4096]{1,0:T(8,128)(2,1)}, bf16[24,4096]{1,0:T(8,128)(2,1)S(1)}, u32[]{:S(2)}, u32[]{:S(2)}) collective-permute-start(bf16[24,4096]{1,0:T(8,128)(2,1)} %get-tuple-element.34), channel_id=1, source_target_pairs={{10,0},{11,1},{8,2},{9,3},{14,4},{15,5},{12,6},{13,7},{2,8},{3,9},... | collective-permute-start | bytes 589832 | tf_op jit(solution)/shard_map/ppermute | solution.py:240
  15.0 1.8 %slice_dynamic-update-slice_fusion.2 = (bf16[192,4096]{1,0:T(8,128)(2,1)}, bf16[192,4096]{1,0:T(8,128)(2,1)}) fusion(bf16[48,4096]{1,0:T(8,128)(2,1)} %get-tuple-element.31), kind=kLoop, calls=%fused_computation.91 | loop fusion | bytes 786432
  16.8 1.9 %pad_maximum_fusion.3 = bf16[72,4096]{1,0:T(8,128)(2,1)} fusion(bf16[8,4096]{1,0:T(8,128)(2,1)} %get-tuple-element.41, bf16[64,4096]{1,0:T(8,128)(2,1)} %bitcast.129), kind=kLoop, calls=%fused_computation.60 | loop fusion | flops 1179648 | bytes 1179648 | tf_op jit(solution)/shard_map/concatenate | solution.py:254
  20.5 7.8 %collective-permute-done.1 = bf16[24,4096]{1,0:T(8,128)(2,1)} collective-permute-done((bf16[24,4096]{1,0:T(8,128)(2,1)}, bf16[24,4096]{1,0:T(8,128)(2,1)}, u32[]{:S(2)}, u32[]{:S(2)}) %collective-permute-start.1) | collective-permute-done | bytes 196640 | tf_op jit(solution)/shard_map/ppermute | solution.py:240
  30.4 1.7 %collective-permute-start.5 = (bf16[24,4096]{1,0:T(8,128)(2,1)}, bf16[24,4096]{1,0:T(8,128)(2,1)S(1)}, u32[]{:S(2)}, u32[]{:S(2)}) collective-permute-start(bf16[24,4096]{1,0:T(8,128)(2,1)} %get-tuple-element.36), channel_id=1, source_target_pairs={{14,0},{15,1},{4,2},{5,3},{2,4},{3,5},{8,6},{9,7},{6,8},{7,9},{12,... | collective-permute-start | bytes 589832 | tf_op jit(solution)/shard_map/ppermute | solution.py:245
  33.2 3.6 %collective-permute-start.7 = (bf16[24,4096]{1,0:T(8,128)(2,1)S(1)}, bf16[24,4096]{1,0:T(8,128)(2,1)S(1)}, u32[]{:S(2)}, u32[]{:S(2)}) collective-permute-start(bf16[24,4096]{1,0:T(8,128)(2,1)S(1)} %copy-done.8), channel_id=1, source_target_pairs={{10,0},{11,1},{8,2},{9,3},{14,4},{15,5},{12,6},{13,7},{2,8},{3,9},... | collective-permute-start | bytes 589832 | tf_op jit(solution)/shard_map/ppermute | solution.py:245
  36.8 5.2 %collective-permute-start.8 = (bf16[72,4096]{1,0:T(8,128)(2,1)S(1)}, bf16[72,4096]{1,0:T(8,128)(2,1)S(1)}, u32[]{:S(2)}, u32[]{:S(2)}) collective-permute-start(bf16[72,4096]{1,0:T(8,128)(2,1)S(1)} %copy-done.5), channel_id=1, source_target_pairs={{16,0},{32,16},{48,32},{64,48},{80,64},{96,80},{112,96},{128,112},... | collective-permute-start | bytes 1769480 | tf_op jit(solution)/shard_map/ppermute | solution.py:262
  42.0 9.1 %collective-permute-done.6 = bf16[24,4096]{1,0:T(8,128)(2,1)S(1)} collective-permute-done((bf16[24,4096]{1,0:T(8,128)(2,1)S(1)}, bf16[24,4096]{1,0:T(8,128)(2,1)S(1)}, u32[]{:S(2)}, u32[]{:S(2)}) %collective-permute-start.6) | collective-permute-done | bytes 196640 | tf_op jit(solution)/shard_map/ppermute | solution.py:245
  52.6 5.6 %collective-permute-start.9 = (bf16[192,4096]{1,0:T(8,128)(2,1)S(1)}, bf16[192,4096]{1,0:T(8,128)(2,1)S(1)}, u32[]{:S(2)}, u32[]{:S(2)}) collective-permute-start(bf16[192,4096]{1,0:T(8,128)(2,1)S(1)} %constant_dynamic-update-slice_fusion), channel_id=1, source_target_pairs={{0,1},{1,0},{2,3},{3,2},{4,5},{5,4},{6,7},{7,6},{8,9},{9,8},{10,11... | collective-permute-start | bytes 4718600 | tf_op jit(solution)/shard_map/ppermute | solution.py:279
  65.6 7.8 %collective-permute-done.13 = bf16[72,4096]{1,0:T(8,128)(2,1)S(1)} collective-permute-done((bf16[72,4096]{1,0:T(8,128)(2,1)S(1)}, bf16[72,4096]{1,0:T(8,128)(2,1)S(1)}, u32[]{:S(2)}, u32[]{:S(2)}) %collective-permute-start.13) | collective-permute-done | bytes 589856 | tf_op jit(solution)/shard_map/ppermute | solution.py:269
  84.8 2.3 %collective-permute-done.12 = bf16[48,4096]{1,0:T(8,128)(2,1)S(1)} collective-permute-done((bf16[48,4096]{1,0:T(8,128)(2,1)S(1)}, bf16[48,4096]{1,0:T(8,128)(2,1)S(1)}, u32[]{:S(2)}, u32[]{:S(2)}) %collective-permute-start.12) | collective-permute-done | bytes 393248 | tf_op jit(solution)/shard_map/ppermute | solution.py:317
  88.0 2.7 %collective-permute-start.19 = (bf16[24,4096]{1,0:T(8,128)(2,1)S(1)}, bf16[24,4096]{1,0:T(8,128)(2,1)S(1)}, u32[]{:S(2)}, u32[]{:S(2)}) collective-permute-start(bf16[24,4096]{1,0:T(8,128)(2,1)S(1)} %get-tuple-element.95), channel_id=1, source_target_pairs={{0,26},{1,27},{2,24},{3,25},{4,30},{5,31},{6,28},{7,29},{8,18},{9,... | collective-permute-start | bytes 589832 | tf_op jit(solution)/shard_map/ppermute | solution.py:161
  90.8 1.9 %collective-permute-start.18 = (bf16[24,4096]{1,0:T(8,128)(2,1)S(1)}, bf16[24,4096]{1,0:T(8,128)(2,1)S(1)}, u32[]{:S(2)}, u32[]{:S(2)}) collective-permute-start(bf16[24,4096]{1,0:T(8,128)(2,1)S(1)} %get-tuple-element.94), channel_id=1, source_target_pairs={{0,28},{1,29},{2,22},{3,23},{4,16},{5,17},{6,26},{7,27},{8,20},{9,... | collective-permute-start | bytes 589832 | tf_op jit(solution)/shard_map/ppermute | solution.py:161
  92.6 3.4 %collective-permute-done.11 = bf16[48,4096]{1,0:T(8,128)(2,1)S(1)} collective-permute-done((bf16[48,4096]{1,0:T(8,128)(2,1)S(1)}, bf16[48,4096]{1,0:T(8,128)(2,1)S(1)}, u32[]{:S(2)}, u32[]{:S(2)}) %collective-permute-start.11) | collective-permute-done | bytes 393248 | tf_op jit(solution)/shard_map/ppermute | solution.py:322
  96.4 1.7 %collective-permute-start.20 = (bf16[48,4096]{1,0:T(8,128)(2,1)S(1)}, bf16[48,4096]{1,0:T(8,128)(2,1)S(1)}, u32[]{:S(2)}, u32[]{:S(2)}) collective-permute-start(bf16[48,4096]{1,0:T(8,128)(2,1)S(1)} %get-tuple-element.64), channel_id=1, source_target_pairs={{0,2},{1,3},{2,0},{3,1},{4,6},{5,7},{6,4},{7,5},{8,10},{9,11},{10,... | collective-permute-start | bytes 1179656 | tf_op jit(solution)/shard_map/ppermute | solution.py:339
  98.1 14.4 %collective-permute-done.21 = bf16[48,4096]{1,0:T(8,128)(2,1)S(1)} collective-permute-done((bf16[48,4096]{1,0:T(8,128)(2,1)S(1)}, bf16[48,4096]{1,0:T(8,128)(2,1)S(1)}, u32[]{:S(2)}, u32[]{:S(2)}) %collective-permute-start.21) | collective-permute-done | bytes 393248 | tf_op jit(solution)/shard_map/ppermute | solution.py:327
  112.6 8.1 %collective-permute-start.25 = (bf16[24,4096]{1,0:T(8,128)(2,1)S(1)}, bf16[24,4096]{1,0:T(8,128)(2,1)S(1)}, u32[]{:S(2)}, u32[]{:S(2)}) collective-permute-start(bf16[24,4096]{1,0:T(8,128)(2,1)S(1)} %get-tuple-element.91), channel_id=1, source_target_pairs={{0,250},{1,251},{2,248},{3,249},{4,254},{5,255},{6,252},{7,253},{8... | collective-permute-start | bytes 589832 | tf_op jit(solution)/shard_map/ppermute | solution.py:161
  121.6 17.2 %collective-permute-start.23 = (bf16[24,4096]{1,0:T(8,128)(2,1)S(1)}, bf16[24,4096]{1,0:T(8,128)(2,1)S(1)}, u32[]{:S(2)}, u32[]{:S(2)}) collective-permute-start(bf16[24,4096]{1,0:T(8,128)(2,1)S(1)} %get-tuple-element.89), channel_id=1, source_target_pairs={{0,254},{1,255},{2,244},{3,245},{4,242},{5,243},{6,248},{7,249},{8... | collective-permute-start | bytes 589832 | tf_op jit(solution)/shard_map/ppermute | solution.py:161
  138.9 3.4 %collective-permute-done.23 = bf16[24,4096]{1,0:T(8,128)(2,1)S(1)} collective-permute-done((bf16[24,4096]{1,0:T(8,128)(2,1)S(1)}, bf16[24,4096]{1,0:T(8,128)(2,1)S(1)}, u32[]{:S(2)}, u32[]{:S(2)}) %collective-permute-start.23) | collective-permute-done | bytes 196640 | tf_op jit(solution)/shard_map/ppermute | solution.py:161
  142.4 1.8 %collective-permute-done.22 = bf16[24,4096]{1,0:T(8,128)(2,1)S(1)} collective-permute-done((bf16[24,4096]{1,0:T(8,128)(2,1)S(1)}, bf16[24,4096]{1,0:T(8,128)(2,1)S(1)}, u32[]{:S(2)}, u32[]{:S(2)}) %collective-permute-start.22) | collective-permute-done | bytes 196640 | tf_op jit(solution)/shard_map/ppermute | solution.py:161
  145.4 4.3 %collective-permute-done.17 = bf16[24,4096]{1,0:T(8,128)(2,1)S(1)} collective-permute-done((bf16[24,4096]{1,0:T(8,128)(2,1)S(1)}, bf16[24,4096]{1,0:T(8,128)(2,1)S(1)}, u32[]{:S(2)}, u32[]{:S(2)}) %collective-permute-start.17) | collective-permute-done | bytes 196640 | tf_op jit(solution)/shard_map/ppermute | solution.py:333
  (110 shorter events, 29.5 us)
Async XLA Ops:
  3.8 26.6 %collective-permute-start.3 = (bf16[48,4096]{1,0:T(8,128)(2,1)}, bf16[48,4096]{1,0:T(8,128)(2,1)}, u32[]{:S(2)}, u32[]{:S(2)}) collective-permute-start(bf16[48,4096]{1,0:T(8,128)(2,1)} %get-tuple-element.31), channel_id=1, source_target_pairs={{0,2},{1,3},{2,0},{3,1},{4,6},{5,7},{6,4},{7,5},{8,10},{9,11},{10,... | collective-permute-start | bytes 1179656 | tf_op jit(solution)/shard_map/ppermute | solution.py:238
  6.3 14.2 %collective-permute-start = (bf16[24,4096]{1,0:T(8,128)(2,1)}, bf16[24,4096]{1,0:T(8,128)(2,1)S(1)}, u32[]{:S(2)}, u32[]{:S(2)}) collective-permute-start(bf16[24,4096]{1,0:T(8,128)(2,1)} %get-tuple-element.32), channel_id=1, source_target_pairs={{14,0},{15,1},{4,2},{5,3},{2,4},{3,5},{8,6},{9,7},{6,8},{7,9},{12,... | collective-permute-start | bytes 589832 | tf_op jit(solution)/shard_map/ppermute | solution.py:240
  10.9 17.4 %collective-permute-start.1 = (bf16[24,4096]{1,0:T(8,128)(2,1)}, bf16[24,4096]{1,0:T(8,128)(2,1)}, u32[]{:S(2)}, u32[]{:S(2)}) collective-permute-start(bf16[24,4096]{1,0:T(8,128)(2,1)} %get-tuple-element.33), channel_id=1, source_target_pairs={{12,0},{13,1},{6,2},{7,3},{0,4},{1,5},{10,6},{11,7},{4,8},{5,9},{1... | collective-permute-start | bytes 589832 | tf_op jit(solution)/shard_map/ppermute | solution.py:240
  10.9 17.4 %collective-permute-start.2 = (bf16[24,4096]{1,0:T(8,128)(2,1)}, bf16[24,4096]{1,0:T(8,128)(2,1)S(1)}, u32[]{:S(2)}, u32[]{:S(2)}) collective-permute-start(bf16[24,4096]{1,0:T(8,128)(2,1)} %get-tuple-element.34), channel_id=1, source_target_pairs={{10,0},{11,1},{8,2},{9,3},{14,4},{15,5},{12,6},{13,7},{2,8},{3,9},... | collective-permute-start | bytes 589832 | tf_op jit(solution)/shard_map/ppermute | solution.py:240
  29.3 23.2 %collective-permute-start.4 = (bf16[72,4096]{1,0:T(8,128)(2,1)S(1)}, bf16[72,4096]{1,0:T(8,128)(2,1)S(1)}, u32[]{:S(2)}, u32[]{:S(2)}) collective-permute-start(bf16[72,4096]{1,0:T(8,128)(2,1)S(1)} %pad_maximum_fusion.1), channel_id=1, source_target_pairs={{0,2},{1,3},{2,0},{3,1},{4,6},{5,7},{6,4},{7,5},{8,10},{9,11},{10,... | collective-permute-start | bytes 1769480 | tf_op jit(solution)/shard_map/ppermute | solution.py:249
  30.4 6.4 %collective-permute-start.5 = (bf16[24,4096]{1,0:T(8,128)(2,1)}, bf16[24,4096]{1,0:T(8,128)(2,1)S(1)}, u32[]{:S(2)}, u32[]{:S(2)}) collective-permute-start(bf16[24,4096]{1,0:T(8,128)(2,1)} %get-tuple-element.36), channel_id=1, source_target_pairs={{14,0},{15,1},{4,2},{5,3},{2,4},{3,5},{8,6},{9,7},{6,8},{7,9},{12,... | collective-permute-start | bytes 589832 | tf_op jit(solution)/shard_map/ppermute | solution.py:245
  32.1 19.1 %collective-permute-start.6 = (bf16[24,4096]{1,0:T(8,128)(2,1)S(1)}, bf16[24,4096]{1,0:T(8,128)(2,1)S(1)}, u32[]{:S(2)}, u32[]{:S(2)}) collective-permute-start(bf16[24,4096]{1,0:T(8,128)(2,1)S(1)} %copy-done.9), channel_id=1, source_target_pairs={{12,0},{13,1},{6,2},{7,3},{0,4},{1,5},{10,6},{11,7},{4,8},{5,9},{1... | collective-permute-start | bytes 589832 | tf_op jit(solution)/shard_map/ppermute | solution.py:245
  33.2 18.0 %collective-permute-start.7 = (bf16[24,4096]{1,0:T(8,128)(2,1)S(1)}, bf16[24,4096]{1,0:T(8,128)(2,1)S(1)}, u32[]{:S(2)}, u32[]{:S(2)}) collective-permute-start(bf16[24,4096]{1,0:T(8,128)(2,1)S(1)} %copy-done.8), channel_id=1, source_target_pairs={{10,0},{11,1},{8,2},{9,3},{14,4},{15,5},{12,6},{13,7},{2,8},{3,9},... | collective-permute-start | bytes 589832 | tf_op jit(solution)/shard_map/ppermute | solution.py:245
  36.8 15.8 %collective-permute-start.8 = (bf16[72,4096]{1,0:T(8,128)(2,1)S(1)}, bf16[72,4096]{1,0:T(8,128)(2,1)S(1)}, u32[]{:S(2)}, u32[]{:S(2)}) collective-permute-start(bf16[72,4096]{1,0:T(8,128)(2,1)S(1)} %copy-done.5), channel_id=1, source_target_pairs={{16,0},{32,16},{48,32},{64,48},{80,64},{96,80},{112,96},{128,112},... | collective-permute-start | bytes 1769480 | tf_op jit(solution)/shard_map/ppermute | solution.py:262
  52.6 8.6 %collective-permute-start.9 = (bf16[192,4096]{1,0:T(8,128)(2,1)S(1)}, bf16[192,4096]{1,0:T(8,128)(2,1)S(1)}, u32[]{:S(2)}, u32[]{:S(2)}) collective-permute-start(bf16[192,4096]{1,0:T(8,128)(2,1)S(1)} %constant_dynamic-update-slice_fusion), channel_id=1, source_target_pairs={{0,1},{1,0},{2,3},{3,2},{4,5},{5,4},{6,7},{7,6},{8,9},{9,8},{10,11... | collective-permute-start | bytes 4718600 | tf_op jit(solution)/shard_map/ppermute | solution.py:279
  58.2 15.2 %collective-permute-start.13 = (bf16[72,4096]{1,0:T(8,128)(2,1)S(1)}, bf16[72,4096]{1,0:T(8,128)(2,1)S(1)}, u32[]{:S(2)}, u32[]{:S(2)}) collective-permute-start(bf16[72,4096]{1,0:T(8,128)(2,1)S(1)} %pad_maximum_fusion.2), channel_id=1, source_target_pairs={{0,2},{1,3},{2,0},{3,1},{4,6},{5,7},{6,4},{7,5},{8,10},{9,11},{10,... | collective-permute-start | bytes 1769480 | tf_op jit(solution)/shard_map/ppermute | solution.py:269
  64.1 11.5 %collective-permute-start.10 = (bf16[192,4096]{1,0:T(8,128)(2,1)S(1)}, bf16[192,4096]{1,0:T(8,128)(2,1)S(1)}, u32[]{:S(2)}, u32[]{:S(2)}) collective-permute-start(bf16[192,4096]{1,0:T(8,128)(2,1)S(1)} %convolution_convert_fusion.1), channel_id=1, source_target_pairs={{0,1},{1,0},{2,3},{3,2},{4,5},{5,4},{6,7},{7,6},{8,9},{9,8},{10,11... | collective-permute-start | bytes 4718600 | tf_op jit(solution)/shard_map/ppermute | solution.py:292
  76.3 10.8 %collective-permute-start.12 = (bf16[48,4096]{1,0:T(8,128)(2,1)S(1)}, bf16[48,4096]{1,0:T(8,128)(2,1)S(1)}, u32[]{:S(2)}, u32[]{:S(2)}) collective-permute-start(bf16[48,4096]{1,0:T(8,128)(2,1)S(1)} %get-tuple-element.67), channel_id=1, source_target_pairs={{0,2},{1,3},{2,0},{3,1},{4,6},{5,7},{6,4},{7,5},{8,10},{9,11},{10,... | collective-permute-start | bytes 1179656 | tf_op jit(solution)/shard_map/ppermute | solution.py:317
  81.1 6.0 %collective-permute-start.15 = (bf16[192,4096]{1,0:T(8,128)(2,1)S(1)}, bf16[192,4096]{1,0:T(8,128)(2,1)S(1)}, u32[]{:S(2)}, u32[]{:S(2)}) collective-permute-start(bf16[192,4096]{1,0:T(8,128)(2,1)S(1)} %fusion.1), channel_id=1, source_target_pairs={{0,1},{1,0},{2,3},{3,2},{4,5},{5,4},{6,7},{7,6},{8,9},{9,8},{10,11... | collective-permute-start | bytes 4718600 | tf_op jit(solution)/shard_map/ppermute | solution.py:310
  84.3 11.8 %collective-permute-start.11 = (bf16[48,4096]{1,0:T(8,128)(2,1)S(1)}, bf16[48,4096]{1,0:T(8,128)(2,1)S(1)}, u32[]{:S(2)}, u32[]{:S(2)}) collective-permute-start(bf16[48,4096]{1,0:T(8,128)(2,1)S(1)} %get-tuple-element.66), channel_id=1, source_target_pairs={{0,2},{1,3},{2,0},{3,1},{4,6},{5,7},{6,4},{7,5},{8,10},{9,11},{10,... | collective-permute-start | bytes 1179656 | tf_op jit(solution)/shard_map/ppermute | solution.py:322
  87.9 24.6 %collective-permute-start.21 = (bf16[48,4096]{1,0:T(8,128)(2,1)S(1)}, bf16[48,4096]{1,0:T(8,128)(2,1)S(1)}, u32[]{:S(2)}, u32[]{:S(2)}) collective-permute-start(bf16[48,4096]{1,0:T(8,128)(2,1)S(1)} %get-tuple-element.65), channel_id=1, source_target_pairs={{0,2},{1,3},{2,0},{3,1},{4,6},{5,7},{6,4},{7,5},{8,10},{9,11},{10,... | collective-permute-start | bytes 1179656 | tf_op jit(solution)/shard_map/ppermute | solution.py:327
  88.0 24.5 %collective-permute-start.19 = (bf16[24,4096]{1,0:T(8,128)(2,1)S(1)}, bf16[24,4096]{1,0:T(8,128)(2,1)S(1)}, u32[]{:S(2)}, u32[]{:S(2)}) collective-permute-start(bf16[24,4096]{1,0:T(8,128)(2,1)S(1)} %get-tuple-element.95), channel_id=1, source_target_pairs={{0,26},{1,27},{2,24},{3,25},{4,30},{5,31},{6,28},{7,29},{8,18},{9,... | collective-permute-start | bytes 589832 | tf_op jit(solution)/shard_map/ppermute | solution.py:161
  90.8 21.8 %collective-permute-start.18 = (bf16[24,4096]{1,0:T(8,128)(2,1)S(1)}, bf16[24,4096]{1,0:T(8,128)(2,1)S(1)}, u32[]{:S(2)}, u32[]{:S(2)}) collective-permute-start(bf16[24,4096]{1,0:T(8,128)(2,1)S(1)} %get-tuple-element.94), channel_id=1, source_target_pairs={{0,28},{1,29},{2,22},{3,23},{4,16},{5,17},{6,26},{7,27},{8,20},{9,... | collective-permute-start | bytes 589832 | tf_op jit(solution)/shard_map/ppermute | solution.py:161
  96.3 49.1 %collective-permute-start.16 = (bf16[96,4096]{1,0:T(8,128)(2,1)S(1)}, bf16[96,4096]{1,0:T(8,128)(2,1)S(1)}, u32[]{:S(2)}, u32[]{:S(2)}) collective-permute-start(bf16[96,4096]{1,0:T(8,128)(2,1)S(1)} %pad_maximum_fusion), channel_id=1, source_target_pairs={{0,16},{1,17},{2,18},{3,19},{4,20},{5,21},{6,22},{7,23},{8,24},{9,... | collective-permute-start | bytes 2359304 | tf_op jit(solution)/shard_map/ppermute | solution.py:332
  96.4 25.1 %collective-permute-start.20 = (bf16[48,4096]{1,0:T(8,128)(2,1)S(1)}, bf16[48,4096]{1,0:T(8,128)(2,1)S(1)}, u32[]{:S(2)}, u32[]{:S(2)}) collective-permute-start(bf16[48,4096]{1,0:T(8,128)(2,1)S(1)} %get-tuple-element.64), channel_id=1, source_target_pairs={{0,2},{1,3},{2,0},{3,1},{4,6},{5,7},{6,4},{7,5},{8,10},{9,11},{10,... | collective-permute-start | bytes 1179656 | tf_op jit(solution)/shard_map/ppermute | solution.py:339
  112.6 26.2 %collective-permute-start.25 = (bf16[24,4096]{1,0:T(8,128)(2,1)S(1)}, bf16[24,4096]{1,0:T(8,128)(2,1)S(1)}, u32[]{:S(2)}, u32[]{:S(2)}) collective-permute-start(bf16[24,4096]{1,0:T(8,128)(2,1)S(1)} %get-tuple-element.91), channel_id=1, source_target_pairs={{0,250},{1,251},{2,248},{3,249},{4,254},{5,255},{6,252},{7,253},{8... | collective-permute-start | bytes 589832 | tf_op jit(solution)/shard_map/ppermute | solution.py:161
  120.7 18.3 %collective-permute-start.24 = (bf16[24,4096]{1,0:T(8,128)(2,1)S(1)}, bf16[24,4096]{1,0:T(8,128)(2,1)S(1)}, u32[]{:S(2)}, u32[]{:S(2)}) collective-permute-start(bf16[24,4096]{1,0:T(8,128)(2,1)S(1)} %get-tuple-element.90), channel_id=1, source_target_pairs={{0,252},{1,253},{2,246},{3,247},{4,240},{5,241},{6,250},{7,251},{8... | collective-permute-start | bytes 589832 | tf_op jit(solution)/shard_map/ppermute | solution.py:161
  121.6 20.7 %collective-permute-start.23 = (bf16[24,4096]{1,0:T(8,128)(2,1)S(1)}, bf16[24,4096]{1,0:T(8,128)(2,1)S(1)}, u32[]{:S(2)}, u32[]{:S(2)}) collective-permute-start(bf16[24,4096]{1,0:T(8,128)(2,1)S(1)} %get-tuple-element.89), channel_id=1, source_target_pairs={{0,254},{1,255},{2,244},{3,245},{4,242},{5,243},{6,248},{7,249},{8... | collective-permute-start | bytes 589832 | tf_op jit(solution)/shard_map/ppermute | solution.py:161
  138.8 10.9 %collective-permute-start.17 = (bf16[24,4096]{1,0:T(8,128)(2,1)S(1)}, bf16[24,4096]{1,0:T(8,128)(2,1)S(1)}, u32[]{:S(2)}, u32[]{:S(2)}) collective-permute-start(bf16[24,4096]{1,0:T(8,128)(2,1)S(1)} %get-tuple-element.93), channel_id=1, source_target_pairs={{0,30},{1,31},{2,20},{3,21},{4,18},{5,19},{6,24},{7,25},{8,22},{9,... | collective-permute-start | bytes 589832 | tf_op jit(solution)/shard_map/ppermute | solution.py:333
  (12 other events, 171.4 us)

commit v5 on v4

--- a/solution.py
+++ b/solution.py
@@ -8,9 +8,10 @@
 from jax.sharding import PartitionSpec as P
 
 REACH = 4
-EDGES = [['jB', 'own_d'], ['fwdB', 'rB'], ['relayB', 'jB1'], ['gF', 'rB'], ['heldF', 'closeB'], ['mF', 'gF'], ['distB', 'gF'], ['homeF', 'payB'], ['homeB', 'h2F'], ['homeB', 'h3F']]
-RELAY = 0
-MERGE = True
+EDGES = [['jB', 'own_d'], ['heldB', 'rB'], ['heldB', 'rF'], ['heldF', 'closeB'], ['mF', 'gF'], ['distB', 'gF'], ['homeF', 'payB'], ['shortB', 'h3F'], ['home0B', 'h0F'], ['home0B', 'h1F'], ['home0F', 'payB'], ['ownB', 'own_d']]
+RELAY = 3
+MERGE = False
+OWN = 1
 
 
 def routes(devices, sections):
@@ -37,75 +38,54 @@
     return out, home, across, beside
 
 
-def prepare_kernel(pairs, capacity, chip_ref, *refs):
-    count = refs[0].shape[1]
+def prepare_kernel(pairs, capacity, masked, chip_ref, ids_ref, gates_ref, keep_ref, rows_ref, *outs):
+    count, rows = ids_ref.shape[1], rows_ref[...]
     chip = chip_ref[0]
-    odd = lax.rem(chip, 2)
+    kept = keep_ref[...].astype(jnp.float32)
     before = lax.broadcasted_iota(jnp.int32, (count, count), 0)
     before = (before < lax.broadcasted_iota(jnp.int32, (count, count), 1)).astype(jnp.bfloat16)
-
-    def fill(ids, rows, keep, parts):
-        ahead = ids - lax.div(chip, 2)
-        ahead = jnp.where(ahead < 0, ahead + pairs, ahead)
-        near = jnp.where(odd == 1, 1, pairs - 1)
-        step = jnp.where(ahead == 0, 0, jnp.where(ahead == 2, 3, jnp.where(ahead == near, 1, 2)))
-        chosen = lax.broadcasted_iota(jnp.int32, (8, count), 0) == step
-        chosen = jnp.where(chosen, 1.0, 0.0)
-        earlier = jnp.dot(
-            chosen.astype(jnp.bfloat16), before, preferred_element_type=jnp.float32
-        )
-        slot = jnp.sum(chosen * earlier, axis=0, keepdims=True).astype(jnp.int32)
-        place = step * capacity + slot
-        for k, (part, start) in enumerate(parts):
-            here = lax.broadcasted_iota(jnp.int32, (capacity, count), 0) + k * capacity == place
-            here = jnp.where(here, keep, 0.0).astype(jnp.bfloat16)
-            made = jnp.dot(here, rows, preferred_element_type=jnp.float32)
-            part[start : start + capacity, :] = made.astype(part.dtype)
-        return place.astype(jnp.float32)
-
-    ids1, gates1, ids2, gates2, keep, rows1, rows2 = refs[:7]
-    own, near1, near2, told1, told2 = refs[7], refs[8:11], refs[11:14], refs[14], refs[15]
-    kept = keep[...].astype(jnp.float32)
-    parts1 = [(own, 0)] + [(part, 0) for part in near1]
-    parts2 = [(own, capacity)] + [(part, 0) for part in near2]
-    place1 = fill(ids1[...], rows1[...], jnp.ones_like(kept), parts1)
-    place2 = fill(ids2[...], rows2[...], kept, parts2)
-
-    def tell(told, place, gates):
-        high = gates.astype(jnp.bfloat16).astype(jnp.float32)
-        middle = (gates - high).astype(jnp.bfloat16).astype(jnp.float32)
-        low = gates - high - middle
-        row = lax.broadcasted_iota(jnp.int32, (8, count), 0)
-        lines = jnp.zeros((8, count), jnp.float32)
-        for k, line in enumerate((place, high, middle, low, kept)):
-            lines = jnp.where(row == k, line, lines)
-        told[...] = jnp.zeros_like(told)
-        told[:, 0:count] = lines.astype(told.dtype)
-
-    tell(told1, place1, gates1[...])
-    tell(told2, place2, gates2[...])
-
-
-def prepare(chip, pairs, capacity, ids1, gates1, ids2, gates2, keep, rows1, rows2):
-    count, width = rows1.shape
-    piece = jax.ShapeDtypeStruct((capacity, width), jnp.bfloat16)
+    ahead = ids_ref[...] - lax.div(chip, 2)
+    ahead = jnp.where(ahead < 0, ahead + pairs, ahead)
+    near = jnp.where(lax.rem(chip, 2) == 1, 1, pairs - 1)
+    step = jnp.where(ahead == 0, 0, jnp.where(ahead == 2, 3, jnp.where(ahead == near, 1, 2)))
+    chosen = jnp.where(lax.broadcasted_iota(jnp.int32, (8, count), 0) == step, 1.0, 0.0)
+    earlier = jnp.dot(chosen.astype(jnp.bfloat16), before, preferred_element_type=jnp.float32)
+    slot = jnp.sum(chosen * earlier, axis=0, keepdims=True).astype(jnp.int32)
+    place = step * capacity + slot
+    for k in range(REACH):
+        here = lax.broadcasted_iota(jnp.int32, (capacity, count), 0) + k * capacity == place
+        here = jnp.where(here, kept if masked else 1.0, 0.0).astype(jnp.bfloat16)
+        made = jnp.dot(here, rows, preferred_element_type=jnp.float32)
+        outs[k][...] = made.astype(jnp.bfloat16)
+    gates = gates_ref[...]
+    high = gates.astype(jnp.bfloat16).astype(jnp.float32)
+    middle = (gates - high).astype(jnp.bfloat16).astype(jnp.float32)
+    row = lax.broadcasted_iota(jnp.int32, (8, count), 0)
+    lines = jnp.zeros((8, count), jnp.float32)
+    for k, line in enumerate((place.astype(jnp.float32), high, middle, gates - high - middle, kept)):
+        lines = jnp.where(row == k, line, lines)
+    told = outs[REACH]
+    told[...] = jnp.zeros_like(told)
+    told[:, 0:count] = lines.astype(told.dtype)
+
+
+def prepare(masked, chip, pairs, capacity, ids, gates, keep, rows):
+    count, width = rows.shape
     whole = pl.BlockSpec(memory_space=pltpu.VMEM)
     made = pl.pallas_call(
-        functools.partial(prepare_kernel, pairs, capacity),
-        out_shape=[jax.ShapeDtypeStruct((2 * capacity, width), jnp.bfloat16)]
-        + [piece] * (2 * REACH - 2)
-        + [
-            jax.ShapeDtypeStruct((8, width), jnp.bfloat16),
-            jax.ShapeDtypeStruct((8, width), jnp.bfloat16),
-        ],
-        in_specs=[pl.BlockSpec(memory_space=pltpu.SMEM)] + [whole] * 7,
-        out_specs=[whole] * (2 * REACH + 1),
+        functools.partial(prepare_kernel, pairs, capacity, masked),
+        out_shape=[jax.ShapeDtypeStruct((capacity, width), jnp.bfloat16)] * REACH
+        + [jax.ShapeDtypeStruct((8, width), jnp.bfloat16)],
+        in_specs=[pl.BlockSpec(memory_space=pltpu.SMEM)] + [whole] * 4,
+        out_specs=[whole] * (REACH + 1),
         cost_estimate=pl.CostEstimate(
-            flops=4 * REACH * capacity * count * width, bytes_accessed=8 * count * width, transcendentals=0
+            flops=2 * REACH * capacity * count * width,
+            bytes_accessed=4 * count * width,
+            transcendentals=0,
         ),
-        name="prepare",
-    )(chip[None], ids1, gates1, ids2, gates2, keep, rows1, rows2)
-    return made[0], made[1:REACH], made[REACH : 2 * REACH - 1], made[-2], made[-1]
+        name="prepare_second" if masked else "prepare_first",
+    )(chip[None], ids, gates, keep, rows)
+    return made[:REACH], made[REACH]
 
 
 def placement(slot_at, slot_total):
@@ -197,18 +177,13 @@
     chip, core = me // 2, me % 2
     ahead = [(i, (i + 1) % sections) for i in range(sections)]
     behind = [((i + 1) % sections, i) for i in range(sections)]
-    own_pieces, first_near, second_near, first_told, second_told = prepare(
-        chip,
-        pairs,
-        capacity,
-        first_ids[..., 0],
-        first_gates[..., 0],
-        second_ids[..., 0],
-        second_gates[..., 0],
-        keep_mask,
-        layer_input[0],
-        cotangent[0],
-    )
+    first_pieces, first_told = prepare(
+        False, chip, pairs, capacity, first_ids[..., 0], first_gates[..., 0], keep_mask, layer_input[0]
+    )
+    second_pieces, second_told = prepare(
+        True, chip, pairs, capacity, second_ids[..., 0], second_gates[..., 0], keep_mask, cotangent[0]
+    )
+    first_near, second_near = first_pieces[1:], second_pieces[1:]
     origins = [
         [(here + jnp.where(here % 2 == 0, -step, step)) % chips for step in range(REACH)]
         for here in (chip, chip ^ 1)
@@ -235,11 +210,19 @@
                 value = after(value, V[source])
         return value
 
-    V["own_d"] = own_distant = lax.ppermute(own_pieces, "expert", across)
+    if OWN == 0:
+        own_pieces = jnp.concatenate((first_pieces[0], second_pieces[0]))
+        V["own_d"] = own_distant = lax.ppermute(own_pieces, "expert", across)
+        own_distants = own_distant[:capacity], own_distant[capacity:]
+    else:
+        V["own_d"] = lax.ppermute(first_pieces[0], "expert", across)
     first_near = [
         lax.ppermute(gate(f"jF{k + 1}", piece), "expert", out(k + 1)) for k, piece in enumerate(first_near)
     ]
     V["jF1"], V["jF2"], V["jF3"] = first_near
+    if OWN == 1:
+        own_distants = V["own_d"], lax.ppermute(gate("ownB", second_pieces[0]), "expert", across)
+        V["own_dB"] = own_distants[1]
     second_near = [gate(f"jB{k + 1}", gate("jB", piece)) for k, piece in enumerate(second_near)]
     second_near = [
         lax.ppermute(piece, "expert", out(k + 1)) for k, piece in enumerate(second_near)
@@ -271,7 +254,7 @@
     if RELAY == 1:
         told = relay(*told)
     held_first = jnp.concatenate(
-        [own_pieces[:capacity], *first_near, own_distant[:capacity], first_distant]
+        [first_pieces[0], *first_near, own_distants[0], first_distant]
     )
     V["heldF"] = held_first = gate("heldF", held_first)
     if RELAY == 2:
@@ -294,9 +277,11 @@
     made_first = lax.optimization_barrier(made_forward((gate("mF", first_mine[0]),), down_rows))
     V["mF"] = made_first
 
+    sent, kept, homeward = collect(made_first, came_first, capacity, 1, home)
+    V["payF"] = far = gate("farF", sent(2))
     second_distant = gate("distB", second_distant)
     held_second = jnp.concatenate(
-        [own_pieces[capacity:], *second_near, own_distant[capacity:], second_distant]
+        [second_pieces[0], *second_near, own_distants[1], second_distant]
     )
     V["heldB"] = held_second = gate("heldB", held_second)
     beside_second = lax.ppermute(held_second, "expert", beside)
@@ -312,9 +297,8 @@
     second_mine = (gate("mB", second_mine[0]), second_mine[1])
     made_second = lax.optimization_barrier(made_backward(second_mine, gate_cols, up_cols))
 
-    sent, kept, homeward = collect(made_first, came_first, capacity, 1, home)
     sent2, kept2, homeward2 = collect(made_second, came_second, capacity, -1, home)
-    far = lax.ppermute(gate("farF", sent(2)), "expert", across)
+    far = lax.ppermute(far, "expert", across)
     V["farF"] = far
     if RELAY == 5:
         told = relay(*told)

time: 151 us -> 144 us (0.954)
  waiting for transfers between devices: 55.6 us -> 37.9 us
  starting transfers between devices: 63.9 us -> 68.5 us
  Pallas kernels: 3.15 us -> 4.87 us
  other arithmetic: 4.55 us -> 6.22 us
    ppermute x3, waiting for transfers between devices: 7.85 us -> 0.01 us  [local(): lax.ppermute(gate(f'jF{k + 1}', piece), 'expert', out(k + 1))]
    ppermute x1, waiting for transfers between devices: 7.83 us -> 0.01 us  [local(): second_distant = lax.ppermute(second_close, 'expert', across)]
    ppermute x1, waiting for transfers between devices: 14.4 us -> 7.32 us  [local(): far2 = lax.ppermute(far2, 'expert', across)]
    ppermute x3, waiting for transfers between devices: 9.14 us -> 15.4 us  [local(): lax.ppermute(piece, 'expert', out(k + 1))]
    ppermute x6 -> x8, waiting for transfers between devices: 5.28 us -> 10.8 us  [homeward(): lax.ppermute(pieces[i * capacity:][:capacity], ('section', 'expert'), hom...]
    ppermute x4, waiting for transfers between devices: 6.65 us -> 1.47 us  [the longest x1 1.46 us: local(): far = lax.ppermute(far, 'expert', across)]
    ppermute x1, starting transfers between devices: 0.47 us -> 4.89 us  [local(): came_first = lax.ppermute(given_first, 'expert', beside)]
    ppermute x3, starting transfers between devices: 6.34 us -> 1.99 us  [local(): lax.ppermute(piece, 'expert', out(k + 1))]
  transfers between devices with their start and end apart: 26 -> 28, of which waited for: 10 -> 10; matrix products, arithmetic and copies ran while one was open for 17% -> 20% of each run, Pallas kernels for 0% -> 2%
where the time goes in v5:
time: 144 us
  starting transfers between devices  68.5 us (48%)
  waiting for transfers between devices  37.9 us (26%)
  matrix products  16.8 us (12%)
  local copies, waits for them, and re-layouts  8.16 us (6%)
  other arithmetic  6.22 us (4%)
  Pallas kernels  4.87 us (3%)
    ppermute x8, starting transfers between devices, homeward(): lax.ppermute(pieces[i * capacity:][:capacity], ('section', 'expert'), hom...  31.8 us
    ppermute x3, waiting for transfers between devices, local(): lax.ppermute(piece, 'expert', out(k + 1))  15.4 us
    ppermute x8, waiting for transfers between devices, homeward(): lax.ppermute(pieces[i * capacity:][:capacity], ('section', 'expert'), hom...  10.8 us
    ppermute x3, starting transfers between devices, local(): lax.ppermute(gate(f'jF{k + 1}', piece), 'expert', out(k + 1))  10.4 us
    ppermute x1, waiting for transfers between devices, local(): far2 = lax.ppermute(far2, 'expert', across)  7.32 us
    unnamed x43, local copies, waits for them, and re-layouts  6.32 us
    ppermute x1, starting transfers between devices, relay(): V['rB'] = second = lax.ppermute(gate('relayB', second), 'section', behind)  4.92 us
    ppermute x1, starting transfers between devices, local(): came_first = lax.ppermute(given_first, 'expert', beside)  4.89 us
  transfers between devices with their start and end apart: 28, of which 10 were waited for; matrix products, arithmetic and copies ran while one was open for 20% of the time, Pallas kernels for 2%

profile of v5, /device:TPU:1, one launch (start us, length us, event | category | flops | bytes accessed | tf_op | source)
XLA Modules:
  0.0 143.6 jit_solution(12095044584856181004)
XLA Ops:
  0.7 2.5 %prepare_first.1 = (bf16[24,4096]{1,0:T(8,128)(2,1)}, bf16[24,4096]{1,0:T(8,128)(2,1)}, bf16[24,4096]{1,0:T(8,128)(2,1)}, bf16[24,4096]{1,0:T(8,128)(2,1)}, bf16[8,4096]{1,0:T(8,128)(2,1)}) custom-call(s32[1]{0:T(128)} %bitcast.1.chip_ref, s32[1,64]{1,0:T(1,128)} %bitcast.130, f32[1,64]{1,0:T(1,128)} %bitcast.131, s32[1,64]{1,0:T(1,128)} %keep_ref.3, ...), custom_call_target="tpu_custom_call" | custom-call | flops 50331648 | bytes 1048576 | tf_op jit(solution)/shard_map/prepare_first/pallas_call | solution.py:75
  3.2 6.4 %collective-permute-start.1 = (bf16[24,4096]{1,0:T(8,128)(2,1)}, bf16[24,4096]{1,0:T(8,128)(2,1)S(1)}, u32[]{:S(2)}, u32[]{:S(2)}) collective-permute-start(bf16[24,4096]{1,0:T(8,128)(2,1)} %get-tuple-element.36), channel_id=1, source_target_pairs={{14,0},{15,1},{4,2},{5,3},{2,4},{3,5},{8,6},{9,7},{6,8},{7,9},{12,... | collective-permute-start | bytes 589832 | tf_op jit(solution)/shard_map/ppermute | solution.py:220
  9.6 4.0 %collective-permute-start.3 = (bf16[24,4096]{1,0:T(8,128)(2,1)}, bf16[24,4096]{1,0:T(8,128)(2,1)}, u32[]{:S(2)}, u32[]{:S(2)}) collective-permute-start(bf16[24,4096]{1,0:T(8,128)(2,1)} %get-tuple-element.38), channel_id=1, source_target_pairs={{10,0},{11,1},{8,2},{9,3},{14,4},{15,5},{12,6},{13,7},{2,8},{3,9},... | collective-permute-start | bytes 589832 | tf_op jit(solution)/shard_map/ppermute | solution.py:220
  13.6 2.4 %prepare_second.1 = (bf16[24,4096]{1,0:T(8,128)(2,1)}, bf16[24,4096]{1,0:T(8,128)(2,1)}, bf16[24,4096]{1,0:T(8,128)(2,1)}, bf16[24,4096]{1,0:T(8,128)(2,1)}, bf16[8,4096]{1,0:T(8,128)(2,1)}) custom-call(s32[1]{0:T(128)} %bitcast.1.chip_ref, s32[1,64]{1,0:T(1,128)} %bitcast.132, f32[1,64]{1,0:T(1,128)} %bitcast.133, s32[1,64]{1,0:T(1,128)} %keep_ref.3, ...), custom_call_target="tpu_custom_call" | custom-call | flops 50331648 | bytes 1048576 | tf_op jit(solution)/shard_map/prepare_second/pallas_call | solution.py:75
  15.9 1.9 %pad_maximum_fusion.2 = bf16[72,4096]{1,0:T(8,128)(2,1)} fusion(bf16[8,4096]{1,0:T(8,128)(2,1)} %get-tuple-element.52, bf16[64,4096]{1,0:T(8,128)(2,1)} %bitcast.127), kind=kLoop, calls=%fused_computation.59 | loop fusion | flops 1179648 | bytes 1179648 | tf_op jit(solution)/shard_map/concatenate | solution.py:237
  17.9 4.9 %collective-permute-start.15 = (bf16[72,4096]{1,0:T(8,128)(2,1)}, bf16[72,4096]{1,0:T(8,128)(2,1)}, u32[]{:S(2)}, u32[]{:S(2)}) collective-permute-start(bf16[72,4096]{1,0:T(8,128)(2,1)} %pad_maximum_fusion.2), channel_id=1, source_target_pairs={{16,0},{32,16},{48,32},{64,48},{80,64},{96,80},{112,96},{128,112},... | collective-permute-start | bytes 1769480 | tf_op jit(solution)/shard_map/ppermute | solution.py:245
  24.4 1.6 %constant_dynamic-update-slice_fusion.14 = bf16[192,4096]{1,0:T(8,128)(2,1)} fusion(bf16[24,4096]{1,0:T(8,128)(2,1)} %get-tuple-element.50), kind=kLoop, calls=%fused_computation.106 | loop fusion | bytes 393216
  34.9 2.8 %collective-permute-done.6 = bf16[24,4096]{1,0:T(8,128)(2,1)S(1)} collective-permute-done((bf16[24,4096]{1,0:T(8,128)(2,1)S(1)}, bf16[24,4096]{1,0:T(8,128)(2,1)S(1)}, u32[]{:S(2)}, u32[]{:S(2)}) %collective-permute-start.6) | collective-permute-done | bytes 196640 | tf_op jit(solution)/shard_map/ppermute | solution.py:228
  38.4 12.6 %collective-permute-done.7 = bf16[24,4096]{1,0:T(8,128)(2,1)S(1)} collective-permute-done((bf16[24,4096]{1,0:T(8,128)(2,1)S(1)}, bf16[24,4096]{1,0:T(8,128)(2,1)S(1)}, u32[]{:S(2)}, u32[]{:S(2)}) %collective-permute-start.7) | collective-permute-done | bytes 196640 | tf_op jit(solution)/shard_map/ppermute | solution.py:228
  51.1 1.6 %collective-permute-start.13 = (bf16[24,4096]{1,0:T(8,128)(2,1)S(1)}, bf16[24,4096]{1,0:T(8,128)(2,1)S(1)}, u32[]{:S(2)}, u32[]{:S(2)}) collective-permute-start(bf16[24,4096]{1,0:T(8,128)(2,1)S(1)} %copy-done.5), channel_id=1, source_target_pairs={{0,2},{1,3},{2,0},{3,1},{4,6},{5,7},{6,4},{7,5},{8,10},{9,11},{10,... | collective-permute-start | bytes 589832 | tf_op jit(solution)/shard_map/ppermute | solution.py:224
  52.9 4.7 %collective-permute-start.9 = (bf16[192,4096]{1,0:T(8,128)(2,1)S(1)}, bf16[192,4096]{1,0:T(8,128)(2,1)S(1)}, u32[]{:S(2)}, u32[]{:S(2)}) collective-permute-start(bf16[192,4096]{1,0:T(8,128)(2,1)S(1)} %constant_dynamic-update-slice_fusion), channel_id=1, source_target_pairs={{0,1},{1,0},{2,3},{3,2},{4,5},{5,4},{6,7},{7,6},{8,9},{9,8},{10,11... | collective-permute-start | bytes 4718600 | tf_op jit(solution)/shard_map/ppermute | solution.py:262
  64.3 4.9 %collective-permute-start.10 = (bf16[192,4096]{1,0:T(8,128)(2,1)S(1)}, bf16[192,4096]{1,0:T(8,128)(2,1)S(1)}, u32[]{:S(2)}, u32[]{:S(2)}) collective-permute-start(bf16[192,4096]{1,0:T(8,128)(2,1)S(1)} %convolution_convert_fusion.1), channel_id=1, source_target_pairs={{0,1},{1,0},{2,3},{3,2},{4,5},{5,4},{6,7},{7,6},{8,9},{9,8},{10,11... | collective-permute-start | bytes 4718600 | tf_op jit(solution)/shard_map/ppermute | solution.py:275
  73.3 2.1 %collective-permute-start.12 = (bf16[48,4096]{1,0:T(8,128)(2,1)S(1)}, bf16[48,4096]{1,0:T(8,128)(2,1)S(1)}, u32[]{:S(2)}, u32[]{:S(2)}) collective-permute-start(bf16[48,4096]{1,0:T(8,128)(2,1)S(1)} %get-tuple-element.73), channel_id=1, source_target_pairs={{0,2},{1,3},{2,0},{3,1},{4,6},{5,7},{6,4},{7,5},{8,10},{9,11},{10,... | collective-permute-start | bytes 1179656 | tf_op jit(solution)/shard_map/ppermute | solution.py:301
  87.0 3.2 %collective-permute-start.21 = (bf16[24,4096]{1,0:T(8,128)(2,1)S(1)}, bf16[24,4096]{1,0:T(8,128)(2,1)S(1)}, u32[]{:S(2)}, u32[]{:S(2)}) collective-permute-start(bf16[24,4096]{1,0:T(8,128)(2,1)S(1)} %get-tuple-element.101), channel_id=1, source_target_pairs={{0,26},{1,27},{2,24},{3,25},{4,30},{5,31},{6,28},{7,29},{8,18},{9,... | collective-permute-start | bytes 589832 | tf_op jit(solution)/shard_map/ppermute | solution.py:141
  90.2 2.5 %collective-permute-start.20 = (bf16[24,4096]{1,0:T(8,128)(2,1)S(1)}, bf16[24,4096]{1,0:T(8,128)(2,1)S(1)}, u32[]{:S(2)}, u32[]{:S(2)}) collective-permute-start(bf16[24,4096]{1,0:T(8,128)(2,1)S(1)} %get-tuple-element.100), channel_id=1, source_target_pairs={{0,28},{1,29},{2,22},{3,23},{4,16},{5,17},{6,26},{7,27},{8,20},{9,... | collective-permute-start | bytes 589832 | tf_op jit(solution)/shard_map/ppermute | solution.py:141
  92.7 2.4 %collective-permute-done.11 = bf16[48,4096]{1,0:T(8,128)(2,1)S(1)} collective-permute-done((bf16[48,4096]{1,0:T(8,128)(2,1)S(1)}, bf16[48,4096]{1,0:T(8,128)(2,1)S(1)}, u32[]{:S(2)}, u32[]{:S(2)}) %collective-permute-start.11) | collective-permute-done | bytes 393248 | tf_op jit(solution)/shard_map/ppermute | solution.py:306
  95.2 5.0 %collective-permute-start.19 = (bf16[24,4096]{1,0:T(8,128)(2,1)S(1)}, bf16[24,4096]{1,0:T(8,128)(2,1)S(1)}, u32[]{:S(2)}, u32[]{:S(2)}) collective-permute-start(bf16[24,4096]{1,0:T(8,128)(2,1)S(1)} %get-tuple-element.99), channel_id=1, source_target_pairs={{0,30},{1,31},{2,20},{3,21},{4,18},{5,19},{6,24},{7,25},{8,22},{9,... | collective-permute-start | bytes 589832 | tf_op jit(solution)/shard_map/ppermute | solution.py:141
  100.6 1.9 %collective-permute-done.21 = bf16[24,4096]{1,0:T(8,128)(2,1)S(1)} collective-permute-done((bf16[24,4096]{1,0:T(8,128)(2,1)S(1)}, bf16[24,4096]{1,0:T(8,128)(2,1)S(1)}, u32[]{:S(2)}, u32[]{:S(2)}) %collective-permute-start.21) | collective-permute-done | bytes 196640 | tf_op jit(solution)/shard_map/ppermute | solution.py:141
  102.5 7.3 %collective-permute-done.23 = bf16[48,4096]{1,0:T(8,128)(2,1)S(1)} collective-permute-done((bf16[48,4096]{1,0:T(8,128)(2,1)S(1)}, bf16[48,4096]{1,0:T(8,128)(2,1)S(1)}, u32[]{:S(2)}, u32[]{:S(2)}) %collective-permute-start.23) | collective-permute-done | bytes 393248 | tf_op jit(solution)/shard_map/ppermute | solution.py:311
  109.9 7.8 %collective-permute-start.27 = (bf16[24,4096]{1,0:T(8,128)(2,1)S(1)}, bf16[24,4096]{1,0:T(8,128)(2,1)S(1)}, u32[]{:S(2)}, u32[]{:S(2)}) collective-permute-start(bf16[24,4096]{1,0:T(8,128)(2,1)S(1)} %get-tuple-element.97), channel_id=1, source_target_pairs={{0,250},{1,251},{2,248},{3,249},{4,254},{5,255},{6,252},{7,253},{8... | collective-permute-start | bytes 589832 | tf_op jit(solution)/shard_map/ppermute | solution.py:141
  118.2 11.5 %collective-permute-start.26 = (bf16[24,4096]{1,0:T(8,128)(2,1)S(1)}, bf16[24,4096]{1,0:T(8,128)(2,1)S(1)}, u32[]{:S(2)}, u32[]{:S(2)}) collective-permute-start(bf16[24,4096]{1,0:T(8,128)(2,1)S(1)} %get-tuple-element.96), channel_id=1, source_target_pairs={{0,252},{1,253},{2,246},{3,247},{4,240},{5,241},{6,250},{7,251},{8... | collective-permute-start | bytes 589832 | tf_op jit(solution)/shard_map/ppermute | solution.py:141
  133.1 4.3 %collective-permute-done.25 = bf16[24,4096]{1,0:T(8,128)(2,1)S(1)} collective-permute-done((bf16[24,4096]{1,0:T(8,128)(2,1)S(1)}, bf16[24,4096]{1,0:T(8,128)(2,1)S(1)}, u32[]{:S(2)}, u32[]{:S(2)}) %collective-permute-start.25) | collective-permute-done | bytes 196640 | tf_op jit(solution)/shard_map/ppermute | solution.py:141
  137.4 4.0 %collective-permute-done.24 = bf16[24,4096]{1,0:T(8,128)(2,1)S(1)} collective-permute-done((bf16[24,4096]{1,0:T(8,128)(2,1)S(1)}, bf16[24,4096]{1,0:T(8,128)(2,1)S(1)}, u32[]{:S(2)}, u32[]{:S(2)}) %collective-permute-start.24) | collective-permute-done | bytes 196640 | tf_op jit(solution)/shard_map/ppermute | solution.py:141
  141.4 2.2 %fusion.51 = bf16[1,64,4096]{2,1,0:T(8,128)(2,1)} fusion(bf16[72,4096]{1,0:T(8,128)(2,1)} %collective-permute-done.15, f32[64]{0:T(128)S(1)} %get-tuple-element.110, f32[64]{0:T(128)S(1)} %get-tuple-element.109, bf16[24,4096]{1,0:T(8,128)(2,1)S(1)} %collective-permute-done.27, bf16[24,4096]{1,0:T(8,128)(2,1)S(1)} %collective-permute-done.26, ...), kind=kOutput, calls=%fused_computation.60 | convolution fusion | flops 54794240 | bytes 1835776 | tf_op jit(solution)/shard_map/dot_general | solution.py:149
  (115 shorter events, 37.9 us)
Async XLA Ops:
  3.2 25.8 %collective-permute-start.1 = (bf16[24,4096]{1,0:T(8,128)(2,1)}, bf16[24,4096]{1,0:T(8,128)(2,1)S(1)}, u32[]{:S(2)}, u32[]{:S(2)}) collective-permute-start(bf16[24,4096]{1,0:T(8,128)(2,1)} %get-tuple-element.36), channel_id=1, source_target_pairs={{14,0},{15,1},{4,2},{5,3},{2,4},{3,5},{8,6},{9,7},{6,8},{7,9},{12,... | collective-permute-start | bytes 589832 | tf_op jit(solution)/shard_map/ppermute | solution.py:220
  9.6 19.5 %collective-permute-start.2 = (bf16[24,4096]{1,0:T(8,128)(2,1)}, bf16[24,4096]{1,0:T(8,128)(2,1)S(1)}, u32[]{:S(2)}, u32[]{:S(2)}) collective-permute-start(bf16[24,4096]{1,0:T(8,128)(2,1)} %get-tuple-element.37), channel_id=1, source_target_pairs={{12,0},{13,1},{6,2},{7,3},{0,4},{1,5},{10,6},{11,7},{4,8},{5,9},{1... | collective-permute-start | bytes 589832 | tf_op jit(solution)/shard_map/ppermute | solution.py:220
  9.6 19.5 %collective-permute-start.3 = (bf16[24,4096]{1,0:T(8,128)(2,1)}, bf16[24,4096]{1,0:T(8,128)(2,1)}, u32[]{:S(2)}, u32[]{:S(2)}) collective-permute-start(bf16[24,4096]{1,0:T(8,128)(2,1)} %get-tuple-element.38), channel_id=1, source_target_pairs={{10,0},{11,1},{8,2},{9,3},{14,4},{15,5},{12,6},{13,7},{2,8},{3,9},... | collective-permute-start | bytes 589832 | tf_op jit(solution)/shard_map/ppermute | solution.py:220
  13.6 18.1 %collective-permute-start.4 = (bf16[24,4096]{1,0:T(8,128)(2,1)}, bf16[24,4096]{1,0:T(8,128)(2,1)}, u32[]{:S(2)}, u32[]{:S(2)}) collective-permute-start(bf16[24,4096]{1,0:T(8,128)(2,1)} %get-tuple-element.35), channel_id=1, source_target_pairs={{0,2},{1,3},{2,0},{3,1},{4,6},{5,7},{6,4},{7,5},{8,10},{9,11},{10,... | collective-permute-start | bytes 589832 | tf_op jit(solution)/shard_map/ppermute | solution.py:218
  17.9 39.8 %collective-permute-start.15 = (bf16[72,4096]{1,0:T(8,128)(2,1)}, bf16[72,4096]{1,0:T(8,128)(2,1)}, u32[]{:S(2)}, u32[]{:S(2)}) collective-permute-start(bf16[72,4096]{1,0:T(8,128)(2,1)} %pad_maximum_fusion.2), channel_id=1, source_target_pairs={{16,0},{32,16},{48,32},{64,48},{80,64},{96,80},{112,96},{128,112},... | collective-permute-start | bytes 1769480 | tf_op jit(solution)/shard_map/ppermute | solution.py:245
  28.9 28.8 %collective-permute-start = (bf16[72,4096]{1,0:T(8,128)(2,1)S(1)}, bf16[72,4096]{1,0:T(8,128)(2,1)S(1)}, u32[]{:S(2)}, u32[]{:S(2)}) collective-permute-start(bf16[72,4096]{1,0:T(8,128)(2,1)S(1)} %pad_maximum_fusion), channel_id=1, source_target_pairs={{0,16},{16,32},{32,48},{48,64},{64,80},{80,96},{96,112},{112,128},... | collective-permute-start | bytes 1769480 | tf_op jit(solution)/shard_map/ppermute | solution.py:243
  30.1 22.8 %collective-permute-start.5 = (bf16[72,4096]{1,0:T(8,128)(2,1)S(1)}, bf16[72,4096]{1,0:T(8,128)(2,1)S(1)}, u32[]{:S(2)}, u32[]{:S(2)}) collective-permute-start(bf16[72,4096]{1,0:T(8,128)(2,1)S(1)} %pad_maximum_fusion.1), channel_id=1, source_target_pairs={{0,2},{1,3},{2,0},{3,1},{4,6},{5,7},{6,4},{7,5},{8,10},{9,11},{10,... | collective-permute-start | bytes 1769480 | tf_op jit(solution)/shard_map/ppermute | solution.py:232
  32.3 18.8 %collective-permute-start.7 = (bf16[24,4096]{1,0:T(8,128)(2,1)S(1)}, bf16[24,4096]{1,0:T(8,128)(2,1)S(1)}, u32[]{:S(2)}, u32[]{:S(2)}) collective-permute-start(bf16[24,4096]{1,0:T(8,128)(2,1)S(1)} %copy-done.8), channel_id=1, source_target_pairs={{12,0},{13,1},{6,2},{7,3},{0,4},{1,5},{10,6},{11,7},{4,8},{5,9},{1... | collective-permute-start | bytes 589832 | tf_op jit(solution)/shard_map/ppermute | solution.py:228
  37.7 15.0 %collective-permute-start.8 = (bf16[24,4096]{1,0:T(8,128)(2,1)S(1)}, bf16[24,4096]{1,0:T(8,128)(2,1)S(1)}, u32[]{:S(2)}, u32[]{:S(2)}) collective-permute-start(bf16[24,4096]{1,0:T(8,128)(2,1)S(1)} %copy-done.7), channel_id=1, source_target_pairs={{10,0},{11,1},{8,2},{9,3},{14,4},{15,5},{12,6},{13,7},{2,8},{3,9},... | collective-permute-start | bytes 589832 | tf_op jit(solution)/shard_map/ppermute | solution.py:228
  52.8 17.4 %collective-permute-start.14 = (bf16[72,4096]{1,0:T(8,128)(2,1)S(1)}, bf16[72,4096]{1,0:T(8,128)(2,1)S(1)}, u32[]{:S(2)}, u32[]{:S(2)}) collective-permute-start(bf16[72,4096]{1,0:T(8,128)(2,1)S(1)} %get-tuple-element.103), channel_id=1, source_target_pairs={{0,2},{1,3},{2,0},{3,1},{4,6},{5,7},{6,4},{7,5},{8,10},{9,11},{10,... | collective-permute-start | bytes 1769480 | tf_op jit(solution)/shard_map/ppermute | solution.py:252
  52.9 8.4 %collective-permute-start.9 = (bf16[192,4096]{1,0:T(8,128)(2,1)S(1)}, bf16[192,4096]{1,0:T(8,128)(2,1)S(1)}, u32[]{:S(2)}, u32[]{:S(2)}) collective-permute-start(bf16[192,4096]{1,0:T(8,128)(2,1)S(1)} %constant_dynamic-update-slice_fusion), channel_id=1, source_target_pairs={{0,1},{1,0},{2,3},{3,2},{4,5},{5,4},{6,7},{7,6},{8,9},{9,8},{10,11... | collective-permute-start | bytes 4718600 | tf_op jit(solution)/shard_map/ppermute | solution.py:262
  64.3 8.3 %collective-permute-start.10 = (bf16[192,4096]{1,0:T(8,128)(2,1)S(1)}, bf16[192,4096]{1,0:T(8,128)(2,1)S(1)}, u32[]{:S(2)}, u32[]{:S(2)}) collective-permute-start(bf16[192,4096]{1,0:T(8,128)(2,1)S(1)} %convolution_convert_fusion.1), channel_id=1, source_target_pairs={{0,1},{1,0},{2,3},{3,2},{4,5},{5,4},{6,7},{7,6},{8,9},{9,8},{10,11... | collective-permute-start | bytes 4718600 | tf_op jit(solution)/shard_map/ppermute | solution.py:275
  73.3 11.6 %collective-permute-start.12 = (bf16[48,4096]{1,0:T(8,128)(2,1)S(1)}, bf16[48,4096]{1,0:T(8,128)(2,1)S(1)}, u32[]{:S(2)}, u32[]{:S(2)}) collective-permute-start(bf16[48,4096]{1,0:T(8,128)(2,1)S(1)} %get-tuple-element.73), channel_id=1, source_target_pairs={{0,2},{1,3},{2,0},{3,1},{4,6},{5,7},{6,4},{7,5},{8,10},{9,11},{10,... | collective-permute-start | bytes 1179656 | tf_op jit(solution)/shard_map/ppermute | solution.py:301
  82.2 12.8 %collective-permute-start.11 = (bf16[48,4096]{1,0:T(8,128)(2,1)S(1)}, bf16[48,4096]{1,0:T(8,128)(2,1)S(1)}, u32[]{:S(2)}, u32[]{:S(2)}) collective-permute-start(bf16[48,4096]{1,0:T(8,128)(2,1)S(1)} %get-tuple-element.72), channel_id=1, source_target_pairs={{0,2},{1,3},{2,0},{3,1},{4,6},{5,7},{6,4},{7,5},{8,10},{9,11},{10,... | collective-permute-start | bytes 1179656 | tf_op jit(solution)/shard_map/ppermute | solution.py:306
  85.6 24.2 %collective-permute-start.23 = (bf16[48,4096]{1,0:T(8,128)(2,1)S(1)}, bf16[48,4096]{1,0:T(8,128)(2,1)S(1)}, u32[]{:S(2)}, u32[]{:S(2)}) collective-permute-start(bf16[48,4096]{1,0:T(8,128)(2,1)S(1)} %get-tuple-element.71), channel_id=1, source_target_pairs={{0,2},{1,3},{2,0},{3,1},{4,6},{5,7},{6,4},{7,5},{8,10},{9,11},{10,... | collective-permute-start | bytes 1179656 | tf_op jit(solution)/shard_map/ppermute | solution.py:311
  87.0 15.4 %collective-permute-start.21 = (bf16[24,4096]{1,0:T(8,128)(2,1)S(1)}, bf16[24,4096]{1,0:T(8,128)(2,1)S(1)}, u32[]{:S(2)}, u32[]{:S(2)}) collective-permute-start(bf16[24,4096]{1,0:T(8,128)(2,1)S(1)} %get-tuple-element.101), channel_id=1, source_target_pairs={{0,26},{1,27},{2,24},{3,25},{4,30},{5,31},{6,28},{7,29},{8,18},{9,... | collective-permute-start | bytes 589832 | tf_op jit(solution)/shard_map/ppermute | solution.py:141
  90.2 41.2 %collective-permute-start.20 = (bf16[24,4096]{1,0:T(8,128)(2,1)S(1)}, bf16[24,4096]{1,0:T(8,128)(2,1)S(1)}, u32[]{:S(2)}, u32[]{:S(2)}) collective-permute-start(bf16[24,4096]{1,0:T(8,128)(2,1)S(1)} %get-tuple-element.100), channel_id=1, source_target_pairs={{0,28},{1,29},{2,22},{3,23},{4,16},{5,17},{6,26},{7,27},{8,20},{9,... | collective-permute-start | bytes 589832 | tf_op jit(solution)/shard_map/ppermute | solution.py:141
  95.2 34.7 %collective-permute-start.19 = (bf16[24,4096]{1,0:T(8,128)(2,1)S(1)}, bf16[24,4096]{1,0:T(8,128)(2,1)S(1)}, u32[]{:S(2)}, u32[]{:S(2)}) collective-permute-start(bf16[24,4096]{1,0:T(8,128)(2,1)S(1)} %get-tuple-element.99), channel_id=1, source_target_pairs={{0,30},{1,31},{2,20},{3,21},{4,18},{5,19},{6,24},{7,25},{8,22},{9,... | collective-permute-start | bytes 589832 | tf_op jit(solution)/shard_map/ppermute | solution.py:141
  100.1 29.7 %collective-permute-start.18 = (bf16[24,4096]{1,0:T(8,128)(2,1)S(1)}, bf16[24,4096]{1,0:T(8,128)(2,1)S(1)}, u32[]{:S(2)}, u32[]{:S(2)}) collective-permute-start(bf16[24,4096]{1,0:T(8,128)(2,1)S(1)} %get-tuple-element.98), channel_id=1, source_target_pairs={{0,16},{1,17},{2,18},{3,19},{4,20},{5,21},{6,22},{7,23},{8,24},{9,... | collective-permute-start | bytes 589832 | tf_op jit(solution)/shard_map/ppermute | solution.py:141
  102.4 15.8 %collective-permute-start.22 = (bf16[48,4096]{1,0:T(8,128)(2,1)S(1)}, bf16[48,4096]{1,0:T(8,128)(2,1)S(1)}, u32[]{:S(2)}, u32[]{:S(2)}) collective-permute-start(bf16[48,4096]{1,0:T(8,128)(2,1)S(1)} %get-tuple-element.62), channel_id=1, source_target_pairs={{0,2},{1,3},{2,0},{3,1},{4,6},{5,7},{6,4},{7,5},{8,10},{9,11},{10,... | collective-permute-start | bytes 1179656 | tf_op jit(solution)/shard_map/ppermute | solution.py:323
  109.9 22.6 %collective-permute-start.27 = (bf16[24,4096]{1,0:T(8,128)(2,1)S(1)}, bf16[24,4096]{1,0:T(8,128)(2,1)S(1)}, u32[]{:S(2)}, u32[]{:S(2)}) collective-permute-start(bf16[24,4096]{1,0:T(8,128)(2,1)S(1)} %get-tuple-element.97), channel_id=1, source_target_pairs={{0,250},{1,251},{2,248},{3,249},{4,254},{5,255},{6,252},{7,253},{8... | collective-permute-start | bytes 589832 | tf_op jit(solution)/shard_map/ppermute | solution.py:141
  118.2 14.9 %collective-permute-start.26 = (bf16[24,4096]{1,0:T(8,128)(2,1)S(1)}, bf16[24,4096]{1,0:T(8,128)(2,1)S(1)}, u32[]{:S(2)}, u32[]{:S(2)}) collective-permute-start(bf16[24,4096]{1,0:T(8,128)(2,1)S(1)} %get-tuple-element.96), channel_id=1, source_target_pairs={{0,252},{1,253},{2,246},{3,247},{4,240},{5,241},{6,250},{7,251},{8... | collective-permute-start | bytes 589832 | tf_op jit(solution)/shard_map/ppermute | solution.py:141
  129.9 7.6 %collective-permute-start.25 = (bf16[24,4096]{1,0:T(8,128)(2,1)S(1)}, bf16[24,4096]{1,0:T(8,128)(2,1)S(1)}, u32[]{:S(2)}, u32[]{:S(2)}) collective-permute-start(bf16[24,4096]{1,0:T(8,128)(2,1)S(1)} %get-tuple-element.95), channel_id=1, source_target_pairs={{0,254},{1,255},{2,244},{3,245},{4,242},{5,243},{6,248},{7,249},{8... | collective-permute-start | bytes 589832 | tf_op jit(solution)/shard_map/ppermute | solution.py:141
  131.2 10.1 %collective-permute-start.24 = (bf16[24,4096]{1,0:T(8,128)(2,1)S(1)}, bf16[24,4096]{1,0:T(8,128)(2,1)S(1)}, u32[]{:S(2)}, u32[]{:S(2)}) collective-permute-start(bf16[24,4096]{1,0:T(8,128)(2,1)S(1)} %get-tuple-element.94), channel_id=1, source_target_pairs={{0,240},{1,241},{2,242},{3,243},{4,244},{5,245},{6,246},{7,247},{8... | collective-permute-start | bytes 589832 | tf_op jit(solution)/shard_map/ppermute | solution.py:141
  (14 other events, 168.0 us)

commit v6 on v5

--- a/solution.py
+++ b/solution.py
@@ -8,10 +8,24 @@
 from jax.sharding import PartitionSpec as P
 
 REACH = 4
-EDGES = [['jB', 'own_d'], ['heldB', 'rB'], ['heldB', 'rF'], ['heldF', 'closeB'], ['mF', 'gF'], ['distB', 'gF'], ['homeF', 'payB'], ['shortB', 'h3F'], ['home0B', 'h0F'], ['home0B', 'h1F'], ['home0F', 'payB'], ['ownB', 'own_d']]
-RELAY = 3
-MERGE = False
-OWN = 1
+WAITS = (
+    ("jB3", "own_d"),
+    ("fwdF", "jB1"),
+    ("relayB", "own_dB"),
+    ("relayF", "own_dB"),
+    ("heldB", "rB"),
+    ("heldB", "rF"),
+    ("heldF", "closeB"),
+    ("mF", "gF"),
+    ("distB", "gF"),
+    ("homeF", "payB"),
+    ("shortB", "h3F"),
+    ("homeB", "h2F"),
+    ("homeB", "h3F"),
+    ("home0B", "h0F"),
+    ("home0B", "h1F"),
+    ("home0F", "payB"),
+)
 
 
 def routes(devices, sections):
@@ -205,24 +219,18 @@
     V = {}
 
     def gate(name, value):
-        for target, source in EDGES:
+        for target, source in WAITS:
             if target == name:
                 value = after(value, V[source])
         return value
 
-    if OWN == 0:
-        own_pieces = jnp.concatenate((first_pieces[0], second_pieces[0]))
-        V["own_d"] = own_distant = lax.ppermute(own_pieces, "expert", across)
-        own_distants = own_distant[:capacity], own_distant[capacity:]
-    else:
-        V["own_d"] = lax.ppermute(first_pieces[0], "expert", across)
+    V["own_d"] = lax.ppermute(first_pieces[0], "expert", across)
     first_near = [
         lax.ppermute(gate(f"jF{k + 1}", piece), "expert", out(k + 1)) for k, piece in enumerate(first_near)
     ]
     V["jF1"], V["jF2"], V["jF3"] = first_near
-    if OWN == 1:
-        own_distants = V["own_d"], lax.ppermute(gate("ownB", second_pieces[0]), "expert", across)
-        V["own_dB"] = own_distants[1]
+    V["own_dB"] = lax.ppermute(gate("ownB", second_pieces[0]), "expert", across)
+    own_distants = V["own_d"], V["own_dB"]
     second_near = [gate(f"jB{k + 1}", gate("jB", piece)) for k, piece in enumerate(second_near)]
     second_near = [
         lax.ppermute(piece, "expert", out(k + 1)) for k, piece in enumerate(second_near)
@@ -231,7 +239,6 @@
     first_close = gate("fwdF", jnp.concatenate(first_near))
     first_distant = lax.ppermute(first_close, "expert", across)
     V["fwdF"] = first_distant
-    relay_done = False
 
     bundles = [
         jnp.concatenate((rows[0], told))
@@ -239,39 +246,27 @@
     ]
 
     def relay(first, second):
-        if not MERGE:
-            first = lax.ppermute(gate("relayF", first), "section", ahead)
-            V["rF"] = first
+        V["rF"] = first = lax.ppermute(gate("relayF", first), "section", ahead)
         V["rB"] = second = lax.ppermute(gate("relayB", second), "section", behind)
         return first, second
 
-    told = bundles
-    if RELAY == 0:
-        told = relay(*told)
     V["closeB"] = second_close = gate("fwdB", jnp.concatenate(second_near))
     second_distant = lax.ppermute(second_close, "expert", across)
     V["fwdB"] = second_distant
-    if RELAY == 1:
-        told = relay(*told)
+    told = relay(*bundles)
     held_first = jnp.concatenate(
         [first_pieces[0], *first_near, own_distants[0], first_distant]
     )
     V["heldF"] = held_first = gate("heldF", held_first)
-    if RELAY == 2:
-        told = relay(*told)
     beside_first = lax.ppermute(held_first, "expert", beside)
     V["coreF"] = beside_first
     first_mine = hidden_forward(gate("hmF", held_first), gate_cols, up_cols)
     V["hmF"] = first_mine[0]
-    if RELAY == 3:
-        told = relay(*told)
     first_given = hidden_forward(gate("hgF", beside_first), gate_cols, up_cols)
     V["hgF"] = first_given[0]
     first_mine, first_given = lax.optimization_barrier((first_mine, first_given))
     given_first = made_forward((gate("gF", first_given[0]),), down_rows)
     V["gF"] = given_first
-    if RELAY == 4:
-        told = relay(*told)
     came_first = lax.ppermute(given_first, "expert", beside)
     V["cF"] = came_first
     made_first = lax.optimization_barrier(made_forward((gate("mF", first_mine[0]),), down_rows))
@@ -300,8 +295,6 @@
     sent2, kept2, homeward2 = collect(made_second, came_second, capacity, -1, home)
     far = lax.ppermute(far, "expert", across)
     V["farF"] = far
-    if RELAY == 5:
-        told = relay(*told)
     V["payB"] = far2 = gate("farB", sent2(2))
     short = lax.ppermute(gate("shortF", sent(0)), "expert", across)
     V["shortF"] = short
@@ -311,14 +304,7 @@
     far2 = lax.ppermute(far2, "expert", across)
     V["farB"] = far2
     last = gate("home0F", kept(0, after(short, pieces)))
-    if MERGE:
-        bundle = jnp.concatenate((last[:capacity], bundles[0]))
-        bundle = lax.ppermute(bundle, ("section", "expert"), home(0, 1))
-        one = lax.ppermute(last[capacity:], ("section", "expert"), home(1, 1))
-        back_first = [bundle[:capacity], one] + back_first
-        told = (bundle[capacity:], told[1])
-    else:
-        back_first = homeward(last, 0) + back_first
+    back_first = homeward(last, 0) + back_first
     V["h0F"], V["h1F"] = back_first[:2]
     short2 = lax.ppermute(gate("shortB", sent2(0)), "expert", across)
     pieces = gate("homeB", kept2(2, far2))

time: 144 us -> 139 us (0.965)
  starting transfers between devices: 68.5 us -> 58.6 us
  waiting for transfers between devices: 37.9 us -> 45.2 us
  other arithmetic: 6.22 us -> 3.47 us
    ppermute x8, starting transfers between devices: 31.8 us -> 21.6 us  [homeward(): lax.ppermute(pieces[i * capacity:][:capacity], ('section', 'expert'), hom...]
    ppermute x3, waiting for transfers between devices: 15.4 us -> 7.26 us  [local(): lax.ppermute(piece, 'expert', out(k + 1))]
    ppermute x1, waiting for transfers between devices: 2.39 us -> 8.51 us  [local(): short = lax.ppermute(gate('shortF', sent(0)), 'expert', across)]
    ppermute x1, waiting for transfers between devices: 0.51 us -> 6.1 us  [local(): short2 = lax.ppermute(gate('shortB', sent2(0)), 'expert', across)]
    ppermute x8, waiting for transfers between devices: 10.8 us -> 6.08 us  [homeward(): lax.ppermute(pieces[i * capacity:][:capacity], ('section', 'expert'), hom...]
    ppermute x1, waiting for transfers between devices: 0.01 us -> 4.19 us  [local(): first_distant = lax.ppermute(first_close, 'expert', across)]
    ppermute x3, starting transfers between devices: 1.99 us -> 4.82 us  [local(): lax.ppermute(piece, 'expert', out(k + 1))]
    concatenate x2, other arithmetic: 2.94 us -> 0.97 us  [local(): jnp.concatenate((rows[0], told))]
  transfers between devices with their start and end apart: 28 -> 28, of which waited for: 10 -> 13; matrix products, arithmetic and copies ran while one was open for 20% -> 19% of each run, Pallas kernels for 2% -> 2%
where the time goes in v6:
time: 139 us; the launch traced here: 138 us
  starting transfers between devices  58.6 us (42%)
  waiting for transfers between devices  45.2 us (33%)
  matrix products  15.7 us (11%)
  local copies, waits for them, and re-layouts  9.27 us (7%)
  Pallas kernels  4.85 us (3%)
  other arithmetic  3.47 us (2%)
    ppermute x8, starting transfers between devices, homeward(): lax.ppermute(pieces[i * capacity:][:capacity], ('section', 'expert'), hom...  21.6 us
    ppermute x3, starting transfers between devices, local(): lax.ppermute(gate(f'jF{k + 1}', piece), 'expert', out(k + 1))  10.4 us
    ppermute x1, waiting for transfers between devices, local(): short = lax.ppermute(gate('shortF', sent(0)), 'expert', across)  8.51 us
    unnamed x45, local copies, waits for them, and re-layouts  7.4 us
    ppermute x3, waiting for transfers between devices, local(): lax.ppermute(piece, 'expert', out(k + 1))  7.26 us
    ppermute x1, waiting for transfers between devices, local(): far2 = lax.ppermute(far2, 'expert', across)  7.04 us
    ppermute x1, waiting for transfers between devices, local(): short2 = lax.ppermute(gate('shortB', sent2(0)), 'expert', across)  6.1 us
    ppermute x8, waiting for transfers between devices, homeward(): lax.ppermute(pieces[i * capacity:][:capacity], ('section', 'expert'), hom...  6.08 us
  transfers between devices with their start and end apart: 28, of which 13 were waited for; matrix products, arithmetic and copies ran while one was open for 19% of the time, Pallas kernels for 2%

profile of v6, /device:TPU:1, one launch (start us, length us, event | category | flops | bytes accessed | tf_op | source)
XLA Modules:
  0.0 138.3 jit_solution(17486523212253722936)
XLA Ops:
  0.7 2.5 %prepare_first.1 = (bf16[24,4096]{1,0:T(8,128)(2,1)}, bf16[24,4096]{1,0:T(8,128)(2,1)}, bf16[24,4096]{1,0:T(8,128)(2,1)}, bf16[24,4096]{1,0:T(8,128)(2,1)}, bf16[8,4096]{1,0:T(8,128)(2,1)}) custom-call(s32[1]{0:T(128)} %bitcast.1.chip_ref, s32[1,64]{1,0:T(1,128)} %bitcast.130, f32[1,64]{1,0:T(1,128)} %bitcast.131, s32[1,64]{1,0:T(1,128)} %keep_ref.3, ...), custom_call_target="tpu_custom_call" | custom-call | flops 50331648 | bytes 1048576 | tf_op jit(solution)/shard_map/prepare_first/pallas_call | solution.py:89
  3.1 6.4 %collective-permute-start.2 = (bf16[24,4096]{1,0:T(8,128)(2,1)}, bf16[24,4096]{1,0:T(8,128)(2,1)S(1)}, u32[]{:S(2)}, u32[]{:S(2)}) collective-permute-start(bf16[24,4096]{1,0:T(8,128)(2,1)} %get-tuple-element.40), channel_id=1, source_target_pairs={{14,0},{15,1},{4,2},{5,3},{2,4},{3,5},{8,6},{9,7},{6,8},{7,9},{12,... | collective-permute-start | bytes 589832 | tf_op jit(solution)/shard_map/ppermute | solution.py:229
  9.6 4.0 %collective-permute-start.4 = (bf16[24,4096]{1,0:T(8,128)(2,1)}, bf16[24,4096]{1,0:T(8,128)(2,1)S(1)}, u32[]{:S(2)}, u32[]{:S(2)}) collective-permute-start(bf16[24,4096]{1,0:T(8,128)(2,1)} %get-tuple-element.42), channel_id=1, source_target_pairs={{10,0},{11,1},{8,2},{9,3},{14,4},{15,5},{12,6},{13,7},{2,8},{3,9},... | collective-permute-start | bytes 589832 | tf_op jit(solution)/shard_map/ppermute | solution.py:229
  13.6 2.4 %prepare_second.1 = (bf16[24,4096]{1,0:T(8,128)(2,1)}, bf16[24,4096]{1,0:T(8,128)(2,1)}, bf16[24,4096]{1,0:T(8,128)(2,1)}, bf16[24,4096]{1,0:T(8,128)(2,1)}, bf16[8,4096]{1,0:T(8,128)(2,1)}) custom-call(s32[1]{0:T(128)} %bitcast.1.chip_ref, s32[1,64]{1,0:T(1,128)} %bitcast.132, f32[1,64]{1,0:T(1,128)} %bitcast.133, s32[1,64]{1,0:T(1,128)} %keep_ref.3, ...), custom_call_target="tpu_custom_call" | custom-call | flops 50331648 | bytes 1048576 | tf_op jit(solution)/shard_map/prepare_second/pallas_call | solution.py:89
  17.4 1.6 %constant_dynamic-update-slice_fusion.5 = bf16[192,4096]{1,0:T(8,128)(2,1)} fusion(bf16[24,4096]{1,0:T(8,128)(2,1)} %get-tuple-element.39), kind=kLoop, calls=%fused_computation.97 | loop fusion | bytes 393216
  19.0 1.6 %constant_dynamic-update-slice_fusion.14 = bf16[192,4096]{1,0:T(8,128)(2,1)} fusion(bf16[24,4096]{1,0:T(8,128)(2,1)} %get-tuple-element.37), kind=kLoop, calls=%fused_computation.106 | loop fusion | bytes 393216
  23.5 1.8 %collective-permute-start.6 = (bf16[24,4096]{1,0:T(8,128)(2,1)S(1)}, bf16[24,4096]{1,0:T(8,128)(2,1)S(1)}, u32[]{:S(2)}, u32[]{:S(2)}) collective-permute-start(bf16[24,4096]{1,0:T(8,128)(2,1)S(1)} %copy-done.10), channel_id=1, source_target_pairs={{14,0},{15,1},{4,2},{5,3},{2,4},{3,5},{8,6},{9,7},{6,8},{7,9},{12,... | collective-permute-start | bytes 589832 | tf_op jit(solution)/shard_map/ppermute | solution.py:236
  27.2 7.3 %collective-permute-done.6 = bf16[24,4096]{1,0:T(8,128)(2,1)S(1)} collective-permute-done((bf16[24,4096]{1,0:T(8,128)(2,1)S(1)}, bf16[24,4096]{1,0:T(8,128)(2,1)S(1)}, u32[]{:S(2)}, u32[]{:S(2)}) %collective-permute-start.6) | collective-permute-done | bytes 196640 | tf_op jit(solution)/shard_map/ppermute | solution.py:236
  34.4 1.9 %collective-permute-start.7 = (bf16[72,4096]{1,0:T(8,128)(2,1)S(1)}, bf16[72,4096]{1,0:T(8,128)(2,1)S(1)}, u32[]{:S(2)}, u32[]{:S(2)}) collective-permute-start(bf16[72,4096]{1,0:T(8,128)(2,1)S(1)} %pad_maximum_fusion.1), channel_id=1, source_target_pairs={{0,2},{1,3},{2,0},{3,1},{4,6},{5,7},{6,4},{7,5},{8,10},{9,11},{10,... | collective-permute-start | bytes 1769480 | tf_op jit(solution)/shard_map/ppermute | solution.py:240
  36.4 3.0 %collective-permute-start.9 = (bf16[24,4096]{1,0:T(8,128)(2,1)S(1)}, bf16[24,4096]{1,0:T(8,128)(2,1)S(1)}, u32[]{:S(2)}, u32[]{:S(2)}) collective-permute-start(bf16[24,4096]{1,0:T(8,128)(2,1)S(1)} %copy-done.8), channel_id=1, source_target_pairs={{10,0},{11,1},{8,2},{9,3},{14,4},{15,5},{12,6},{13,7},{2,8},{3,9},... | collective-permute-start | bytes 589832 | tf_op jit(solution)/shard_map/ppermute | solution.py:236
  39.4 4.9 %collective-permute-start.15 = (bf16[72,4096]{1,0:T(8,128)(2,1)S(1)}, bf16[72,4096]{1,0:T(8,128)(2,1)S(1)}, u32[]{:S(2)}, u32[]{:S(2)}) collective-permute-start(bf16[72,4096]{1,0:T(8,128)(2,1)S(1)} %pad_maximum_fusion.2), channel_id=1, source_target_pairs={{16,0},{32,16},{48,32},{64,48},{80,64},{96,80},{112,96},{128,112},... | collective-permute-start | bytes 1769480 | tf_op jit(solution)/shard_map/ppermute | solution.py:250
  47.8 4.2 %collective-permute-done.7 = bf16[72,4096]{1,0:T(8,128)(2,1)S(1)} collective-permute-done((bf16[72,4096]{1,0:T(8,128)(2,1)S(1)}, bf16[72,4096]{1,0:T(8,128)(2,1)S(1)}, u32[]{:S(2)}, u32[]{:S(2)}) %collective-permute-start.7) | collective-permute-done | bytes 589856 | tf_op jit(solution)/shard_map/ppermute | solution.py:240
  52.1 5.5 %collective-permute-start.10 = (bf16[192,4096]{1,0:T(8,128)(2,1)S(1)}, bf16[192,4096]{1,0:T(8,128)(2,1)S(1)}, u32[]{:S(2)}, u32[]{:S(2)}) collective-permute-start(bf16[192,4096]{1,0:T(8,128)(2,1)S(1)} %constant_dynamic-update-slice_fusion), channel_id=1, source_target_pairs={{0,1},{1,0},{2,3},{3,2},{4,5},{5,4},{6,7},{7,6},{8,9},{9,8},{10,11... | collective-permute-start | bytes 4718600 | tf_op jit(solution)/shard_map/ppermute | solution.py:261
  66.0 3.4 %collective-permute-start.11 = (bf16[192,4096]{1,0:T(8,128)(2,1)S(1)}, bf16[192,4096]{1,0:T(8,128)(2,1)S(1)}, u32[]{:S(2)}, u32[]{:S(2)}) collective-permute-start(bf16[192,4096]{1,0:T(8,128)(2,1)S(1)} %convolution_convert_fusion.1), channel_id=1, source_target_pairs={{0,1},{1,0},{2,3},{3,2},{4,5},{5,4},{6,7},{7,6},{8,9},{9,8},{10,11... | collective-permute-start | bytes 4718600 | tf_op jit(solution)/shard_map/ppermute | solution.py:270
  84.6 2.2 %collective-permute-start.21 = (bf16[24,4096]{1,0:T(8,128)(2,1)S(1)}, bf16[24,4096]{1,0:T(8,128)(2,1)S(1)}, u32[]{:S(2)}, u32[]{:S(2)}) collective-permute-start(bf16[24,4096]{1,0:T(8,128)(2,1)S(1)} %get-tuple-element.105), channel_id=1, source_target_pairs={{0,26},{1,27},{2,24},{3,25},{4,30},{5,31},{6,28},{7,29},{8,18},{9,... | collective-permute-start | bytes 589832 | tf_op jit(solution)/shard_map/ppermute | solution.py:155
  86.7 1.9 %collective-permute-start.20 = (bf16[24,4096]{1,0:T(8,128)(2,1)S(1)}, bf16[24,4096]{1,0:T(8,128)(2,1)S(1)}, u32[]{:S(2)}, u32[]{:S(2)}) collective-permute-start(bf16[24,4096]{1,0:T(8,128)(2,1)S(1)} %get-tuple-element.104), channel_id=1, source_target_pairs={{0,28},{1,29},{2,22},{3,23},{4,16},{5,17},{6,26},{7,27},{8,20},{9,... | collective-permute-start | bytes 589832 | tf_op jit(solution)/shard_map/ppermute | solution.py:155
  88.7 8.5 %collective-permute-done.12 = bf16[48,4096]{1,0:T(8,128)(2,1)S(1)} collective-permute-done((bf16[48,4096]{1,0:T(8,128)(2,1)S(1)}, bf16[48,4096]{1,0:T(8,128)(2,1)S(1)}, u32[]{:S(2)}, u32[]{:S(2)}) %collective-permute-start.12) | collective-permute-done | bytes 393248 | tf_op jit(solution)/shard_map/ppermute | solution.py:299
  97.4 2.1 %collective-permute-start.18 = (bf16[24,4096]{1,0:T(8,128)(2,1)S(1)}, bf16[24,4096]{1,0:T(8,128)(2,1)S(1)}, u32[]{:S(2)}, u32[]{:S(2)}) collective-permute-start(bf16[24,4096]{1,0:T(8,128)(2,1)S(1)} %get-tuple-element.102), channel_id=1, source_target_pairs={{0,16},{1,17},{2,18},{3,19},{4,20},{5,21},{6,22},{7,23},{8,24},{9,... | collective-permute-start | bytes 589832 | tf_op jit(solution)/shard_map/ppermute | solution.py:155
  102.1 7.0 %collective-permute-done.23 = bf16[48,4096]{1,0:T(8,128)(2,1)S(1)} collective-permute-done((bf16[48,4096]{1,0:T(8,128)(2,1)S(1)}, bf16[48,4096]{1,0:T(8,128)(2,1)S(1)}, u32[]{:S(2)}, u32[]{:S(2)}) %collective-permute-start.23) | collective-permute-done | bytes 393248 | tf_op jit(solution)/shard_map/ppermute | solution.py:304
  109.3 4.4 %collective-permute-start.27 = (bf16[24,4096]{1,0:T(8,128)(2,1)S(1)}, bf16[24,4096]{1,0:T(8,128)(2,1)S(1)}, u32[]{:S(2)}, u32[]{:S(2)}) collective-permute-start(bf16[24,4096]{1,0:T(8,128)(2,1)S(1)} %get-tuple-element.101), channel_id=1, source_target_pairs={{0,250},{1,251},{2,248},{3,249},{4,254},{5,255},{6,252},{7,253},{8... | collective-permute-start | bytes 589832 | tf_op jit(solution)/shard_map/ppermute | solution.py:155
  114.6 6.1 %collective-permute-done.22 = bf16[48,4096]{1,0:T(8,128)(2,1)S(1)} collective-permute-done((bf16[48,4096]{1,0:T(8,128)(2,1)S(1)}, bf16[48,4096]{1,0:T(8,128)(2,1)S(1)}, u32[]{:S(2)}, u32[]{:S(2)}) %collective-permute-start.22) | collective-permute-done | bytes 393248 | tf_op jit(solution)/shard_map/ppermute | solution.py:309
  120.9 9.4 %collective-permute-start.25 = (bf16[24,4096]{1,0:T(8,128)(2,1)S(1)}, bf16[24,4096]{1,0:T(8,128)(2,1)S(1)}, u32[]{:S(2)}, u32[]{:S(2)}) collective-permute-start(bf16[24,4096]{1,0:T(8,128)(2,1)S(1)} %get-tuple-element.99), channel_id=1, source_target_pairs={{0,254},{1,255},{2,244},{3,245},{4,242},{5,243},{6,248},{7,249},{8... | collective-permute-start | bytes 589832 | tf_op jit(solution)/shard_map/ppermute | solution.py:155
  132.0 1.8 %collective-permute-done.25 = bf16[24,4096]{1,0:T(8,128)(2,1)S(1)} collective-permute-done((bf16[24,4096]{1,0:T(8,128)(2,1)S(1)}, bf16[24,4096]{1,0:T(8,128)(2,1)S(1)}, u32[]{:S(2)}, u32[]{:S(2)}) %collective-permute-start.25) | collective-permute-done | bytes 196640 | tf_op jit(solution)/shard_map/ppermute | solution.py:155
  133.8 3.3 %collective-permute-done.24 = bf16[24,4096]{1,0:T(8,128)(2,1)S(1)} collective-permute-done((bf16[24,4096]{1,0:T(8,128)(2,1)S(1)}, bf16[24,4096]{1,0:T(8,128)(2,1)S(1)}, u32[]{:S(2)}, u32[]{:S(2)}) %collective-permute-start.24) | collective-permute-done | bytes 196640 | tf_op jit(solution)/shard_map/ppermute | solution.py:155
  (117 shorter events, 39.8 us)
Async XLA Ops:
  3.1 20.4 %collective-permute-start.2 = (bf16[24,4096]{1,0:T(8,128)(2,1)}, bf16[24,4096]{1,0:T(8,128)(2,1)S(1)}, u32[]{:S(2)}, u32[]{:S(2)}) collective-permute-start(bf16[24,4096]{1,0:T(8,128)(2,1)} %get-tuple-element.40), channel_id=1, source_target_pairs={{14,0},{15,1},{4,2},{5,3},{2,4},{3,5},{8,6},{9,7},{6,8},{7,9},{12,... | collective-permute-start | bytes 589832 | tf_op jit(solution)/shard_map/ppermute | solution.py:229
  9.6 15.8 %collective-permute-start.3 = (bf16[24,4096]{1,0:T(8,128)(2,1)}, bf16[24,4096]{1,0:T(8,128)(2,1)}, u32[]{:S(2)}, u32[]{:S(2)}) collective-permute-start(bf16[24,4096]{1,0:T(8,128)(2,1)} %get-tuple-element.41), channel_id=1, source_target_pairs={{12,0},{13,1},{6,2},{7,3},{0,4},{1,5},{10,6},{11,7},{4,8},{5,9},{1... | collective-permute-start | bytes 589832 | tf_op jit(solution)/shard_map/ppermute | solution.py:229
  9.6 16.7 %collective-permute-start.4 = (bf16[24,4096]{1,0:T(8,128)(2,1)}, bf16[24,4096]{1,0:T(8,128)(2,1)S(1)}, u32[]{:S(2)}, u32[]{:S(2)}) collective-permute-start(bf16[24,4096]{1,0:T(8,128)(2,1)} %get-tuple-element.42), channel_id=1, source_target_pairs={{10,0},{11,1},{8,2},{9,3},{14,4},{15,5},{12,6},{13,7},{2,8},{3,9},... | collective-permute-start | bytes 589832 | tf_op jit(solution)/shard_map/ppermute | solution.py:229
  13.6 22.8 %collective-permute-start.5 = (bf16[24,4096]{1,0:T(8,128)(2,1)}, bf16[24,4096]{1,0:T(8,128)(2,1)}, u32[]{:S(2)}, u32[]{:S(2)}) collective-permute-start(bf16[24,4096]{1,0:T(8,128)(2,1)} %get-tuple-element.39), channel_id=1, source_target_pairs={{0,2},{1,3},{2,0},{3,1},{4,6},{5,7},{6,4},{7,5},{8,10},{9,11},{10,... | collective-permute-start | bytes 589832 | tf_op jit(solution)/shard_map/ppermute | solution.py:227
  15.9 23.5 %collective-permute-start = (bf16[24,4096]{1,0:T(8,128)(2,1)}, bf16[24,4096]{1,0:T(8,128)(2,1)}, u32[]{:S(2)}, u32[]{:S(2)}) collective-permute-start(bf16[24,4096]{1,0:T(8,128)(2,1)} %get-tuple-element.37), channel_id=1, source_target_pairs={{0,2},{1,3},{2,0},{3,1},{4,6},{5,7},{6,4},{7,5},{8,10},{9,11},{10,... | collective-permute-start | bytes 589832 | tf_op jit(solution)/shard_map/ppermute | solution.py:232
  23.5 10.9 %collective-permute-start.6 = (bf16[24,4096]{1,0:T(8,128)(2,1)S(1)}, bf16[24,4096]{1,0:T(8,128)(2,1)S(1)}, u32[]{:S(2)}, u32[]{:S(2)}) collective-permute-start(bf16[24,4096]{1,0:T(8,128)(2,1)S(1)} %copy-done.10), channel_id=1, source_target_pairs={{14,0},{15,1},{4,2},{5,3},{2,4},{3,5},{8,6},{9,7},{6,8},{7,9},{12,... | collective-permute-start | bytes 589832 | tf_op jit(solution)/shard_map/ppermute | solution.py:236
  25.3 20.1 %collective-permute-start.8 = (bf16[24,4096]{1,0:T(8,128)(2,1)S(1)}, bf16[24,4096]{1,0:T(8,128)(2,1)S(1)}, u32[]{:S(2)}, u32[]{:S(2)}) collective-permute-start(bf16[24,4096]{1,0:T(8,128)(2,1)S(1)} %copy-done.9), channel_id=1, source_target_pairs={{12,0},{13,1},{6,2},{7,3},{0,4},{1,5},{10,6},{11,7},{4,8},{5,9},{1... | collective-permute-start | bytes 589832 | tf_op jit(solution)/shard_map/ppermute | solution.py:236
  34.4 17.6 %collective-permute-start.7 = (bf16[72,4096]{1,0:T(8,128)(2,1)S(1)}, bf16[72,4096]{1,0:T(8,128)(2,1)S(1)}, u32[]{:S(2)}, u32[]{:S(2)}) collective-permute-start(bf16[72,4096]{1,0:T(8,128)(2,1)S(1)} %pad_maximum_fusion.1), channel_id=1, source_target_pairs={{0,2},{1,3},{2,0},{3,1},{4,6},{5,7},{6,4},{7,5},{8,10},{9,11},{10,... | collective-permute-start | bytes 1769480 | tf_op jit(solution)/shard_map/ppermute | solution.py:240
  36.4 10.2 %collective-permute-start.9 = (bf16[24,4096]{1,0:T(8,128)(2,1)S(1)}, bf16[24,4096]{1,0:T(8,128)(2,1)S(1)}, u32[]{:S(2)}, u32[]{:S(2)}) collective-permute-start(bf16[24,4096]{1,0:T(8,128)(2,1)S(1)} %copy-done.8), channel_id=1, source_target_pairs={{10,0},{11,1},{8,2},{9,3},{14,4},{15,5},{12,6},{13,7},{2,8},{3,9},... | collective-permute-start | bytes 589832 | tf_op jit(solution)/shard_map/ppermute | solution.py:236
  39.4 20.7 %collective-permute-start.15 = (bf16[72,4096]{1,0:T(8,128)(2,1)S(1)}, bf16[72,4096]{1,0:T(8,128)(2,1)S(1)}, u32[]{:S(2)}, u32[]{:S(2)}) collective-permute-start(bf16[72,4096]{1,0:T(8,128)(2,1)S(1)} %pad_maximum_fusion.2), channel_id=1, source_target_pairs={{16,0},{32,16},{48,32},{64,48},{80,64},{96,80},{112,96},{128,112},... | collective-permute-start | bytes 1769480 | tf_op jit(solution)/shard_map/ppermute | solution.py:250
  44.3 15.7 %collective-permute-start.1 = (bf16[72,4096]{1,0:T(8,128)(2,1)S(1)}, bf16[72,4096]{1,0:T(8,128)(2,1)S(1)}, u32[]{:S(2)}, u32[]{:S(2)}) collective-permute-start(bf16[72,4096]{1,0:T(8,128)(2,1)S(1)} %pad_maximum_fusion), channel_id=1, source_target_pairs={{0,16},{16,32},{32,48},{48,64},{64,80},{80,96},{96,112},{112,128},... | collective-permute-start | bytes 1769480 | tf_op jit(solution)/shard_map/ppermute | solution.py:249
  46.6 23.9 %collective-permute-start.14 = (bf16[72,4096]{1,0:T(8,128)(2,1)S(1)}, bf16[72,4096]{1,0:T(8,128)(2,1)S(1)}, u32[]{:S(2)}, u32[]{:S(2)}) collective-permute-start(bf16[72,4096]{1,0:T(8,128)(2,1)S(1)} %get-tuple-element.107), channel_id=1, source_target_pairs={{0,2},{1,3},{2,0},{3,1},{4,6},{5,7},{6,4},{7,5},{8,10},{9,11},{10,... | collective-permute-start | bytes 1769480 | tf_op jit(solution)/shard_map/ppermute | solution.py:254
  52.1 10.9 %collective-permute-start.10 = (bf16[192,4096]{1,0:T(8,128)(2,1)S(1)}, bf16[192,4096]{1,0:T(8,128)(2,1)S(1)}, u32[]{:S(2)}, u32[]{:S(2)}) collective-permute-start(bf16[192,4096]{1,0:T(8,128)(2,1)S(1)} %constant_dynamic-update-slice_fusion), channel_id=1, source_target_pairs={{0,1},{1,0},{2,3},{3,2},{4,5},{5,4},{6,7},{7,6},{8,9},{9,8},{10,11... | collective-permute-start | bytes 4718600 | tf_op jit(solution)/shard_map/ppermute | solution.py:261
  73.1 10.4 %collective-permute-start.13 = (bf16[48,4096]{1,0:T(8,128)(2,1)S(1)}, bf16[48,4096]{1,0:T(8,128)(2,1)S(1)}, u32[]{:S(2)}, u32[]{:S(2)}) collective-permute-start(bf16[48,4096]{1,0:T(8,128)(2,1)S(1)} %get-tuple-element.77), channel_id=1, source_target_pairs={{0,2},{1,3},{2,0},{3,1},{4,6},{5,7},{6,4},{7,5},{8,10},{9,11},{10,... | collective-permute-start | bytes 1179656 | tf_op jit(solution)/shard_map/ppermute | solution.py:296
  81.6 15.6 %collective-permute-start.12 = (bf16[48,4096]{1,0:T(8,128)(2,1)S(1)}, bf16[48,4096]{1,0:T(8,128)(2,1)S(1)}, u32[]{:S(2)}, u32[]{:S(2)}) collective-permute-start(bf16[48,4096]{1,0:T(8,128)(2,1)S(1)} %get-tuple-element.76), channel_id=1, source_target_pairs={{0,2},{1,3},{2,0},{3,1},{4,6},{5,7},{6,4},{7,5},{8,10},{9,11},{10,... | collective-permute-start | bytes 1179656 | tf_op jit(solution)/shard_map/ppermute | solution.py:299
  84.3 24.8 %collective-permute-start.23 = (bf16[48,4096]{1,0:T(8,128)(2,1)S(1)}, bf16[48,4096]{1,0:T(8,128)(2,1)S(1)}, u32[]{:S(2)}, u32[]{:S(2)}) collective-permute-start(bf16[48,4096]{1,0:T(8,128)(2,1)S(1)} %get-tuple-element.75), channel_id=1, source_target_pairs={{0,2},{1,3},{2,0},{3,1},{4,6},{5,7},{6,4},{7,5},{8,10},{9,11},{10,... | collective-permute-start | bytes 1179656 | tf_op jit(solution)/shard_map/ppermute | solution.py:304
  84.6 15.9 %collective-permute-start.21 = (bf16[24,4096]{1,0:T(8,128)(2,1)S(1)}, bf16[24,4096]{1,0:T(8,128)(2,1)S(1)}, u32[]{:S(2)}, u32[]{:S(2)}) collective-permute-start(bf16[24,4096]{1,0:T(8,128)(2,1)S(1)} %get-tuple-element.105), channel_id=1, source_target_pairs={{0,26},{1,27},{2,24},{3,25},{4,30},{5,31},{6,28},{7,29},{8,18},{9,... | collective-permute-start | bytes 589832 | tf_op jit(solution)/shard_map/ppermute | solution.py:155
  86.7 22.5 %collective-permute-start.20 = (bf16[24,4096]{1,0:T(8,128)(2,1)S(1)}, bf16[24,4096]{1,0:T(8,128)(2,1)S(1)}, u32[]{:S(2)}, u32[]{:S(2)}) collective-permute-start(bf16[24,4096]{1,0:T(8,128)(2,1)S(1)} %get-tuple-element.104), channel_id=1, source_target_pairs={{0,28},{1,29},{2,22},{3,23},{4,16},{5,17},{6,26},{7,27},{8,20},{9,... | collective-permute-start | bytes 589832 | tf_op jit(solution)/shard_map/ppermute | solution.py:155
  97.3 23.5 %collective-permute-start.19 = (bf16[24,4096]{1,0:T(8,128)(2,1)S(1)}, bf16[24,4096]{1,0:T(8,128)(2,1)S(1)}, u32[]{:S(2)}, u32[]{:S(2)}) collective-permute-start(bf16[24,4096]{1,0:T(8,128)(2,1)S(1)} %get-tuple-element.103), channel_id=1, source_target_pairs={{0,30},{1,31},{2,20},{3,21},{4,18},{5,19},{6,24},{7,25},{8,22},{9,... | collective-permute-start | bytes 589832 | tf_op jit(solution)/shard_map/ppermute | solution.py:155
  97.4 23.4 %collective-permute-start.18 = (bf16[24,4096]{1,0:T(8,128)(2,1)S(1)}, bf16[24,4096]{1,0:T(8,128)(2,1)S(1)}, u32[]{:S(2)}, u32[]{:S(2)}) collective-permute-start(bf16[24,4096]{1,0:T(8,128)(2,1)S(1)} %get-tuple-element.102), channel_id=1, source_target_pairs={{0,16},{1,17},{2,18},{3,19},{4,20},{5,21},{6,22},{7,23},{8,24},{9,... | collective-permute-start | bytes 589832 | tf_op jit(solution)/shard_map/ppermute | solution.py:155
  100.5 20.2 %collective-permute-start.22 = (bf16[48,4096]{1,0:T(8,128)(2,1)S(1)}, bf16[48,4096]{1,0:T(8,128)(2,1)S(1)}, u32[]{:S(2)}, u32[]{:S(2)}) collective-permute-start(bf16[48,4096]{1,0:T(8,128)(2,1)S(1)} %get-tuple-element.64), channel_id=1, source_target_pairs={{0,2},{1,3},{2,0},{3,1},{4,6},{5,7},{6,4},{7,5},{8,10},{9,11},{10,... | collective-permute-start | bytes 1179656 | tf_op jit(solution)/shard_map/ppermute | solution.py:309
  109.3 22.8 %collective-permute-start.27 = (bf16[24,4096]{1,0:T(8,128)(2,1)S(1)}, bf16[24,4096]{1,0:T(8,128)(2,1)S(1)}, u32[]{:S(2)}, u32[]{:S(2)}) collective-permute-start(bf16[24,4096]{1,0:T(8,128)(2,1)S(1)} %get-tuple-element.101), channel_id=1, source_target_pairs={{0,250},{1,251},{2,248},{3,249},{4,254},{5,255},{6,252},{7,253},{8... | collective-permute-start | bytes 589832 | tf_op jit(solution)/shard_map/ppermute | solution.py:155
  113.6 18.4 %collective-permute-start.26 = (bf16[24,4096]{1,0:T(8,128)(2,1)S(1)}, bf16[24,4096]{1,0:T(8,128)(2,1)S(1)}, u32[]{:S(2)}, u32[]{:S(2)}) collective-permute-start(bf16[24,4096]{1,0:T(8,128)(2,1)S(1)} %get-tuple-element.100), channel_id=1, source_target_pairs={{0,252},{1,253},{2,246},{3,247},{4,240},{5,241},{6,250},{7,251},{8... | collective-permute-start | bytes 589832 | tf_op jit(solution)/shard_map/ppermute | solution.py:155
  120.9 12.9 %collective-permute-start.25 = (bf16[24,4096]{1,0:T(8,128)(2,1)S(1)}, bf16[24,4096]{1,0:T(8,128)(2,1)S(1)}, u32[]{:S(2)}, u32[]{:S(2)}) collective-permute-start(bf16[24,4096]{1,0:T(8,128)(2,1)S(1)} %get-tuple-element.99), channel_id=1, source_target_pairs={{0,254},{1,255},{2,244},{3,245},{4,242},{5,243},{6,248},{7,249},{8... | collective-permute-start | bytes 589832 | tf_op jit(solution)/shard_map/ppermute | solution.py:155
  (15 other events, 171.0 us)

commit v7 on v6

--- a/solution.py
+++ b/solution.py
@@ -66,11 +66,11 @@
     earlier = jnp.dot(chosen.astype(jnp.bfloat16), before, preferred_element_type=jnp.float32)
     slot = jnp.sum(chosen * earlier, axis=0, keepdims=True).astype(jnp.int32)
     place = step * capacity + slot
+    here = lax.broadcasted_iota(jnp.int32, (REACH * capacity, count), 0) == place
+    here = jnp.where(here, kept if masked else 1.0, 0.0).astype(jnp.bfloat16)
+    made = jnp.dot(here, rows, preferred_element_type=jnp.float32)
     for k in range(REACH):
-        here = lax.broadcasted_iota(jnp.int32, (capacity, count), 0) + k * capacity == place
-        here = jnp.where(here, kept if masked else 1.0, 0.0).astype(jnp.bfloat16)
-        made = jnp.dot(here, rows, preferred_element_type=jnp.float32)
-        outs[k][...] = made.astype(jnp.bfloat16)
+        outs[k][...] = made[k * capacity : (k + 1) * capacity].astype(jnp.bfloat16)
     gates = gates_ref[...]
     high = gates.astype(jnp.bfloat16).astype(jnp.float32)
     middle = (gates - high).astype(jnp.bfloat16).astype(jnp.float32)

time: 139 us -> 139 us (level)
    ppermute x8, waiting for transfers between devices: 6.08 us -> 8.17 us  [homeward(): lax.ppermute(pieces[i * capacity:][:capacity], ('section', 'expert'), hom...]
    ppermute x8, starting transfers between devices: 21.6 us -> 19.8 us  [homeward(): lax.ppermute(pieces[i * capacity:][:capacity], ('section', 'expert'), hom...]
where the time goes in v7:
time: 139 us; the launch traced here: 138 us
  starting transfers between devices  57.3 us (41%)
  waiting for transfers between devices  46.5 us (33%)
  matrix products  15.7 us (11%)
  local copies, waits for them, and re-layouts  9.26 us (7%)
  Pallas kernels  5.04 us (4%)
  other arithmetic  3.47 us (2%)
    ppermute x8, starting transfers between devices, homeward(): lax.ppermute(pieces[i * capacity:][:capacity], ('section', 'expert'), hom...  19.8 us
    ppermute x3, starting transfers between devices, local(): lax.ppermute(gate(f'jF{k + 1}', piece), 'expert', out(k + 1))  10.4 us
    ppermute x1, waiting for transfers between devices, local(): short = lax.ppermute(gate('shortF', sent(0)), 'expert', across)  8.27 us
    ppermute x8, waiting for transfers between devices, homeward(): lax.ppermute(pieces[i * capacity:][:capacity], ('section', 'expert'), hom...  8.17 us
    unnamed x45, local copies, waits for them, and re-layouts  7.39 us
    ppermute x3, waiting for transfers between devices, local(): lax.ppermute(piece, 'expert', out(k + 1))  7.26 us
    ppermute x1, waiting for transfers between devices, local(): far2 = lax.ppermute(far2, 'expert', across)  6.74 us
    ppermute x1, waiting for transfers between devices, local(): short2 = lax.ppermute(gate('shortB', sent2(0)), 'expert', across)  6.05 us
  transfers between devices with their start and end apart: 28, of which 13 were waited for; matrix products, arithmetic and copies ran while one was open for 19% of the time, Pallas kernels for 2%

profile of v7, /device:TPU:1, one launch (start us, length us, event | category | flops | bytes accessed | tf_op | source)
XLA Modules:
  0.0 138.5 jit_solution(13630430901087069542)
XLA Ops:
  0.7 2.6 %prepare_first.1 = (bf16[24,4096]{1,0:T(8,128)(2,1)}, bf16[24,4096]{1,0:T(8,128)(2,1)}, bf16[24,4096]{1,0:T(8,128)(2,1)}, bf16[24,4096]{1,0:T(8,128)(2,1)}, bf16[8,4096]{1,0:T(8,128)(2,1)}) custom-call(s32[1]{0:T(128)} %bitcast.1.chip_ref, s32[1,64]{1,0:T(1,128)} %bitcast.130, f32[1,64]{1,0:T(1,128)} %bitcast.131, s32[1,64]{1,0:T(1,128)} %keep_ref.3, ...), custom_call_target="tpu_custom_call" | custom-call | flops 50331648 | bytes 1048576 | tf_op jit(solution)/shard_map/prepare_first/pallas_call | solution.py:89
  3.2 6.4 %collective-permute-start.2 = (bf16[24,4096]{1,0:T(8,128)(2,1)}, bf16[24,4096]{1,0:T(8,128)(2,1)S(1)}, u32[]{:S(2)}, u32[]{:S(2)}) collective-permute-start(bf16[24,4096]{1,0:T(8,128)(2,1)} %get-tuple-element.40), channel_id=1, source_target_pairs={{14,0},{15,1},{4,2},{5,3},{2,4},{3,5},{8,6},{9,7},{6,8},{7,9},{12,... | collective-permute-start | bytes 589832 | tf_op jit(solution)/shard_map/ppermute | solution.py:229
  9.6 4.0 %collective-permute-start.4 = (bf16[24,4096]{1,0:T(8,128)(2,1)}, bf16[24,4096]{1,0:T(8,128)(2,1)S(1)}, u32[]{:S(2)}, u32[]{:S(2)}) collective-permute-start(bf16[24,4096]{1,0:T(8,128)(2,1)} %get-tuple-element.42), channel_id=1, source_target_pairs={{10,0},{11,1},{8,2},{9,3},{14,4},{15,5},{12,6},{13,7},{2,8},{3,9},... | collective-permute-start | bytes 589832 | tf_op jit(solution)/shard_map/ppermute | solution.py:229
  13.6 2.5 %prepare_second.1 = (bf16[24,4096]{1,0:T(8,128)(2,1)}, bf16[24,4096]{1,0:T(8,128)(2,1)}, bf16[24,4096]{1,0:T(8,128)(2,1)}, bf16[24,4096]{1,0:T(8,128)(2,1)}, bf16[8,4096]{1,0:T(8,128)(2,1)}) custom-call(s32[1]{0:T(128)} %bitcast.1.chip_ref, s32[1,64]{1,0:T(1,128)} %bitcast.132, f32[1,64]{1,0:T(1,128)} %bitcast.133, s32[1,64]{1,0:T(1,128)} %keep_ref.3, ...), custom_call_target="tpu_custom_call" | custom-call | flops 50331648 | bytes 1048576 | tf_op jit(solution)/shard_map/prepare_second/pallas_call | solution.py:89
  19.2 1.6 %constant_dynamic-update-slice_fusion.14 = bf16[192,4096]{1,0:T(8,128)(2,1)} fusion(bf16[24,4096]{1,0:T(8,128)(2,1)} %get-tuple-element.37), kind=kLoop, calls=%fused_computation.106 | loop fusion | bytes 393216
  23.7 1.7 %collective-permute-start.6 = (bf16[24,4096]{1,0:T(8,128)(2,1)S(1)}, bf16[24,4096]{1,0:T(8,128)(2,1)S(1)}, u32[]{:S(2)}, u32[]{:S(2)}) collective-permute-start(bf16[24,4096]{1,0:T(8,128)(2,1)S(1)} %copy-done.10), channel_id=1, source_target_pairs={{14,0},{15,1},{4,2},{5,3},{2,4},{3,5},{8,6},{9,7},{6,8},{7,9},{12,... | collective-permute-start | bytes 589832 | tf_op jit(solution)/shard_map/ppermute | solution.py:236
  27.3 7.3 %collective-permute-done.6 = bf16[24,4096]{1,0:T(8,128)(2,1)S(1)} collective-permute-done((bf16[24,4096]{1,0:T(8,128)(2,1)S(1)}, bf16[24,4096]{1,0:T(8,128)(2,1)S(1)}, u32[]{:S(2)}, u32[]{:S(2)}) %collective-permute-start.6) | collective-permute-done | bytes 196640 | tf_op jit(solution)/shard_map/ppermute | solution.py:236
  34.5 2.1 %collective-permute-start.7 = (bf16[72,4096]{1,0:T(8,128)(2,1)S(1)}, bf16[72,4096]{1,0:T(8,128)(2,1)S(1)}, u32[]{:S(2)}, u32[]{:S(2)}) collective-permute-start(bf16[72,4096]{1,0:T(8,128)(2,1)S(1)} %pad_maximum_fusion.1), channel_id=1, source_target_pairs={{0,2},{1,3},{2,0},{3,1},{4,6},{5,7},{6,4},{7,5},{8,10},{9,11},{10,... | collective-permute-start | bytes 1769480 | tf_op jit(solution)/shard_map/ppermute | solution.py:240
  36.6 2.9 %collective-permute-start.9 = (bf16[24,4096]{1,0:T(8,128)(2,1)S(1)}, bf16[24,4096]{1,0:T(8,128)(2,1)S(1)}, u32[]{:S(2)}, u32[]{:S(2)}) collective-permute-start(bf16[24,4096]{1,0:T(8,128)(2,1)S(1)} %copy-done.8), channel_id=1, source_target_pairs={{10,0},{11,1},{8,2},{9,3},{14,4},{15,5},{12,6},{13,7},{2,8},{3,9},... | collective-permute-start | bytes 589832 | tf_op jit(solution)/shard_map/ppermute | solution.py:236
  39.5 4.9 %collective-permute-start.15 = (bf16[72,4096]{1,0:T(8,128)(2,1)S(1)}, bf16[72,4096]{1,0:T(8,128)(2,1)S(1)}, u32[]{:S(2)}, u32[]{:S(2)}) collective-permute-start(bf16[72,4096]{1,0:T(8,128)(2,1)S(1)} %pad_maximum_fusion.2), channel_id=1, source_target_pairs={{16,0},{32,16},{48,32},{64,48},{80,64},{96,80},{112,96},{128,112},... | collective-permute-start | bytes 1769480 | tf_op jit(solution)/shard_map/ppermute | solution.py:250
  48.1 4.3 %collective-permute-done.7 = bf16[72,4096]{1,0:T(8,128)(2,1)S(1)} collective-permute-done((bf16[72,4096]{1,0:T(8,128)(2,1)S(1)}, bf16[72,4096]{1,0:T(8,128)(2,1)S(1)}, u32[]{:S(2)}, u32[]{:S(2)}) %collective-permute-start.7) | collective-permute-done | bytes 589856 | tf_op jit(solution)/shard_map/ppermute | solution.py:240
  52.4 5.3 %collective-permute-start.10 = (bf16[192,4096]{1,0:T(8,128)(2,1)S(1)}, bf16[192,4096]{1,0:T(8,128)(2,1)S(1)}, u32[]{:S(2)}, u32[]{:S(2)}) collective-permute-start(bf16[192,4096]{1,0:T(8,128)(2,1)S(1)} %constant_dynamic-update-slice_fusion), channel_id=1, source_target_pairs={{0,1},{1,0},{2,3},{3,2},{4,5},{5,4},{6,7},{7,6},{8,9},{9,8},{10,11... | collective-permute-start | bytes 4718600 | tf_op jit(solution)/shard_map/ppermute | solution.py:261
  66.1 3.4 %collective-permute-start.11 = (bf16[192,4096]{1,0:T(8,128)(2,1)S(1)}, bf16[192,4096]{1,0:T(8,128)(2,1)S(1)}, u32[]{:S(2)}, u32[]{:S(2)}) collective-permute-start(bf16[192,4096]{1,0:T(8,128)(2,1)S(1)} %convolution_convert_fusion.1), channel_id=1, source_target_pairs={{0,1},{1,0},{2,3},{3,2},{4,5},{5,4},{6,7},{7,6},{8,9},{9,8},{10,11... | collective-permute-start | bytes 4718600 | tf_op jit(solution)/shard_map/ppermute | solution.py:270
  84.8 2.0 %collective-permute-start.21 = (bf16[24,4096]{1,0:T(8,128)(2,1)S(1)}, bf16[24,4096]{1,0:T(8,128)(2,1)S(1)}, u32[]{:S(2)}, u32[]{:S(2)}) collective-permute-start(bf16[24,4096]{1,0:T(8,128)(2,1)S(1)} %get-tuple-element.105), channel_id=1, source_target_pairs={{0,26},{1,27},{2,24},{3,25},{4,30},{5,31},{6,28},{7,29},{8,18},{9,... | collective-permute-start | bytes 589832 | tf_op jit(solution)/shard_map/ppermute | solution.py:155
  86.8 2.1 %collective-permute-start.20 = (bf16[24,4096]{1,0:T(8,128)(2,1)S(1)}, bf16[24,4096]{1,0:T(8,128)(2,1)S(1)}, u32[]{:S(2)}, u32[]{:S(2)}) collective-permute-start(bf16[24,4096]{1,0:T(8,128)(2,1)S(1)} %get-tuple-element.104), channel_id=1, source_target_pairs={{0,28},{1,29},{2,22},{3,23},{4,16},{5,17},{6,26},{7,27},{8,20},{9,... | collective-permute-start | bytes 589832 | tf_op jit(solution)/shard_map/ppermute | solution.py:155
  89.0 8.3 %collective-permute-done.12 = bf16[48,4096]{1,0:T(8,128)(2,1)S(1)} collective-permute-done((bf16[48,4096]{1,0:T(8,128)(2,1)S(1)}, bf16[48,4096]{1,0:T(8,128)(2,1)S(1)}, u32[]{:S(2)}, u32[]{:S(2)}) %collective-permute-start.12) | collective-permute-done | bytes 393248 | tf_op jit(solution)/shard_map/ppermute | solution.py:299
  97.5 3.0 %collective-permute-done.21 = bf16[24,4096]{1,0:T(8,128)(2,1)S(1)} collective-permute-done((bf16[24,4096]{1,0:T(8,128)(2,1)S(1)}, bf16[24,4096]{1,0:T(8,128)(2,1)S(1)}, u32[]{:S(2)}, u32[]{:S(2)}) %collective-permute-start.21) | collective-permute-done | bytes 196640 | tf_op jit(solution)/shard_map/ppermute | solution.py:155
  100.6 1.9 %collective-permute-start.22 = (bf16[48,4096]{1,0:T(8,128)(2,1)S(1)}, bf16[48,4096]{1,0:T(8,128)(2,1)S(1)}, u32[]{:S(2)}, u32[]{:S(2)}) collective-permute-start(bf16[48,4096]{1,0:T(8,128)(2,1)S(1)} %get-tuple-element.64), channel_id=1, source_target_pairs={{0,2},{1,3},{2,0},{3,1},{4,6},{5,7},{6,4},{7,5},{8,10},{9,11},{10,... | collective-permute-start | bytes 1179656 | tf_op jit(solution)/shard_map/ppermute | solution.py:309
  102.5 6.7 %collective-permute-done.23 = bf16[48,4096]{1,0:T(8,128)(2,1)S(1)} collective-permute-done((bf16[48,4096]{1,0:T(8,128)(2,1)S(1)}, bf16[48,4096]{1,0:T(8,128)(2,1)S(1)}, u32[]{:S(2)}, u32[]{:S(2)}) %collective-permute-start.23) | collective-permute-done | bytes 393248 | tf_op jit(solution)/shard_map/ppermute | solution.py:304
  109.3 4.7 %collective-permute-start.27 = (bf16[24,4096]{1,0:T(8,128)(2,1)S(1)}, bf16[24,4096]{1,0:T(8,128)(2,1)S(1)}, u32[]{:S(2)}, u32[]{:S(2)}) collective-permute-start(bf16[24,4096]{1,0:T(8,128)(2,1)S(1)} %get-tuple-element.101), channel_id=1, source_target_pairs={{0,250},{1,251},{2,248},{3,249},{4,254},{5,255},{6,252},{7,253},{8... | collective-permute-start | bytes 589832 | tf_op jit(solution)/shard_map/ppermute | solution.py:155
  114.9 6.0 %collective-permute-done.22 = bf16[48,4096]{1,0:T(8,128)(2,1)S(1)} collective-permute-done((bf16[48,4096]{1,0:T(8,128)(2,1)S(1)}, bf16[48,4096]{1,0:T(8,128)(2,1)S(1)}, u32[]{:S(2)}, u32[]{:S(2)}) %collective-permute-start.22) | collective-permute-done | bytes 393248 | tf_op jit(solution)/shard_map/ppermute | solution.py:309
  121.1 9.3 %collective-permute-start.25 = (bf16[24,4096]{1,0:T(8,128)(2,1)S(1)}, bf16[24,4096]{1,0:T(8,128)(2,1)S(1)}, u32[]{:S(2)}, u32[]{:S(2)}) collective-permute-start(bf16[24,4096]{1,0:T(8,128)(2,1)S(1)} %get-tuple-element.99), channel_id=1, source_target_pairs={{0,254},{1,255},{2,244},{3,245},{4,242},{5,243},{6,248},{7,249},{8... | collective-permute-start | bytes 589832 | tf_op jit(solution)/shard_map/ppermute | solution.py:155
  132.2 1.7 %collective-permute-done.25 = bf16[24,4096]{1,0:T(8,128)(2,1)S(1)} collective-permute-done((bf16[24,4096]{1,0:T(8,128)(2,1)S(1)}, bf16[24,4096]{1,0:T(8,128)(2,1)S(1)}, u32[]{:S(2)}, u32[]{:S(2)}) %collective-permute-start.25) | collective-permute-done | bytes 196640 | tf_op jit(solution)/shard_map/ppermute | solution.py:155
  133.9 3.4 %collective-permute-done.24 = bf16[24,4096]{1,0:T(8,128)(2,1)S(1)} collective-permute-done((bf16[24,4096]{1,0:T(8,128)(2,1)S(1)}, bf16[24,4096]{1,0:T(8,128)(2,1)S(1)}, u32[]{:S(2)}, u32[]{:S(2)}) %collective-permute-start.24) | collective-permute-done | bytes 196640 | tf_op jit(solution)/shard_map/ppermute | solution.py:155
  (117 shorter events, 39.1 us)
Async XLA Ops:
  3.2 20.5 %collective-permute-start.2 = (bf16[24,4096]{1,0:T(8,128)(2,1)}, bf16[24,4096]{1,0:T(8,128)(2,1)S(1)}, u32[]{:S(2)}, u32[]{:S(2)}) collective-permute-start(bf16[24,4096]{1,0:T(8,128)(2,1)} %get-tuple-element.40), channel_id=1, source_target_pairs={{14,0},{15,1},{4,2},{5,3},{2,4},{3,5},{8,6},{9,7},{6,8},{7,9},{12,... | collective-permute-start | bytes 589832 | tf_op jit(solution)/shard_map/ppermute | solution.py:229
  9.6 15.8 %collective-permute-start.3 = (bf16[24,4096]{1,0:T(8,128)(2,1)}, bf16[24,4096]{1,0:T(8,128)(2,1)}, u32[]{:S(2)}, u32[]{:S(2)}) collective-permute-start(bf16[24,4096]{1,0:T(8,128)(2,1)} %get-tuple-element.41), channel_id=1, source_target_pairs={{12,0},{13,1},{6,2},{7,3},{0,4},{1,5},{10,6},{11,7},{4,8},{5,9},{1... | collective-permute-start | bytes 589832 | tf_op jit(solution)/shard_map/ppermute | solution.py:229
  9.6 16.7 %collective-permute-start.4 = (bf16[24,4096]{1,0:T(8,128)(2,1)}, bf16[24,4096]{1,0:T(8,128)(2,1)S(1)}, u32[]{:S(2)}, u32[]{:S(2)}) collective-permute-start(bf16[24,4096]{1,0:T(8,128)(2,1)} %get-tuple-element.42), channel_id=1, source_target_pairs={{10,0},{11,1},{8,2},{9,3},{14,4},{15,5},{12,6},{13,7},{2,8},{3,9},... | collective-permute-start | bytes 589832 | tf_op jit(solution)/shard_map/ppermute | solution.py:229
  13.6 23.0 %collective-permute-start.5 = (bf16[24,4096]{1,0:T(8,128)(2,1)}, bf16[24,4096]{1,0:T(8,128)(2,1)}, u32[]{:S(2)}, u32[]{:S(2)}) collective-permute-start(bf16[24,4096]{1,0:T(8,128)(2,1)} %get-tuple-element.39), channel_id=1, source_target_pairs={{0,2},{1,3},{2,0},{3,1},{4,6},{5,7},{6,4},{7,5},{8,10},{9,11},{10,... | collective-permute-start | bytes 589832 | tf_op jit(solution)/shard_map/ppermute | solution.py:227
  16.1 23.4 %collective-permute-start = (bf16[24,4096]{1,0:T(8,128)(2,1)}, bf16[24,4096]{1,0:T(8,128)(2,1)}, u32[]{:S(2)}, u32[]{:S(2)}) collective-permute-start(bf16[24,4096]{1,0:T(8,128)(2,1)} %get-tuple-element.37), channel_id=1, source_target_pairs={{0,2},{1,3},{2,0},{3,1},{4,6},{5,7},{6,4},{7,5},{8,10},{9,11},{10,... | collective-permute-start | bytes 589832 | tf_op jit(solution)/shard_map/ppermute | solution.py:232
  23.7 10.8 %collective-permute-start.6 = (bf16[24,4096]{1,0:T(8,128)(2,1)S(1)}, bf16[24,4096]{1,0:T(8,128)(2,1)S(1)}, u32[]{:S(2)}, u32[]{:S(2)}) collective-permute-start(bf16[24,4096]{1,0:T(8,128)(2,1)S(1)} %copy-done.10), channel_id=1, source_target_pairs={{14,0},{15,1},{4,2},{5,3},{2,4},{3,5},{8,6},{9,7},{6,8},{7,9},{12,... | collective-permute-start | bytes 589832 | tf_op jit(solution)/shard_map/ppermute | solution.py:236
  25.4 20.1 %collective-permute-start.8 = (bf16[24,4096]{1,0:T(8,128)(2,1)S(1)}, bf16[24,4096]{1,0:T(8,128)(2,1)S(1)}, u32[]{:S(2)}, u32[]{:S(2)}) collective-permute-start(bf16[24,4096]{1,0:T(8,128)(2,1)S(1)} %copy-done.9), channel_id=1, source_target_pairs={{12,0},{13,1},{6,2},{7,3},{0,4},{1,5},{10,6},{11,7},{4,8},{5,9},{1... | collective-permute-start | bytes 589832 | tf_op jit(solution)/shard_map/ppermute | solution.py:236
  34.5 17.9 %collective-permute-start.7 = (bf16[72,4096]{1,0:T(8,128)(2,1)S(1)}, bf16[72,4096]{1,0:T(8,128)(2,1)S(1)}, u32[]{:S(2)}, u32[]{:S(2)}) collective-permute-start(bf16[72,4096]{1,0:T(8,128)(2,1)S(1)} %pad_maximum_fusion.1), channel_id=1, source_target_pairs={{0,2},{1,3},{2,0},{3,1},{4,6},{5,7},{6,4},{7,5},{8,10},{9,11},{10,... | collective-permute-start | bytes 1769480 | tf_op jit(solution)/shard_map/ppermute | solution.py:240
  36.6 10.0 %collective-permute-start.9 = (bf16[24,4096]{1,0:T(8,128)(2,1)S(1)}, bf16[24,4096]{1,0:T(8,128)(2,1)S(1)}, u32[]{:S(2)}, u32[]{:S(2)}) collective-permute-start(bf16[24,4096]{1,0:T(8,128)(2,1)S(1)} %copy-done.8), channel_id=1, source_target_pairs={{10,0},{11,1},{8,2},{9,3},{14,4},{15,5},{12,6},{13,7},{2,8},{3,9},... | collective-permute-start | bytes 589832 | tf_op jit(solution)/shard_map/ppermute | solution.py:236
  39.5 20.7 %collective-permute-start.15 = (bf16[72,4096]{1,0:T(8,128)(2,1)S(1)}, bf16[72,4096]{1,0:T(8,128)(2,1)S(1)}, u32[]{:S(2)}, u32[]{:S(2)}) collective-permute-start(bf16[72,4096]{1,0:T(8,128)(2,1)S(1)} %pad_maximum_fusion.2), channel_id=1, source_target_pairs={{16,0},{32,16},{48,32},{64,48},{80,64},{96,80},{112,96},{128,112},... | collective-permute-start | bytes 1769480 | tf_op jit(solution)/shard_map/ppermute | solution.py:250
  44.4 15.7 %collective-permute-start.1 = (bf16[72,4096]{1,0:T(8,128)(2,1)S(1)}, bf16[72,4096]{1,0:T(8,128)(2,1)S(1)}, u32[]{:S(2)}, u32[]{:S(2)}) collective-permute-start(bf16[72,4096]{1,0:T(8,128)(2,1)S(1)} %pad_maximum_fusion), channel_id=1, source_target_pairs={{0,16},{16,32},{32,48},{48,64},{64,80},{80,96},{96,112},{112,128},... | collective-permute-start | bytes 1769480 | tf_op jit(solution)/shard_map/ppermute | solution.py:249
  46.7 23.9 %collective-permute-start.14 = (bf16[72,4096]{1,0:T(8,128)(2,1)S(1)}, bf16[72,4096]{1,0:T(8,128)(2,1)S(1)}, u32[]{:S(2)}, u32[]{:S(2)}) collective-permute-start(bf16[72,4096]{1,0:T(8,128)(2,1)S(1)} %get-tuple-element.107), channel_id=1, source_target_pairs={{0,2},{1,3},{2,0},{3,1},{4,6},{5,7},{6,4},{7,5},{8,10},{9,11},{10,... | collective-permute-start | bytes 1769480 | tf_op jit(solution)/shard_map/ppermute | solution.py:254
  52.4 10.7 %collective-permute-start.10 = (bf16[192,4096]{1,0:T(8,128)(2,1)S(1)}, bf16[192,4096]{1,0:T(8,128)(2,1)S(1)}, u32[]{:S(2)}, u32[]{:S(2)}) collective-permute-start(bf16[192,4096]{1,0:T(8,128)(2,1)S(1)} %constant_dynamic-update-slice_fusion), channel_id=1, source_target_pairs={{0,1},{1,0},{2,3},{3,2},{4,5},{5,4},{6,7},{7,6},{8,9},{9,8},{10,11... | collective-permute-start | bytes 4718600 | tf_op jit(solution)/shard_map/ppermute | solution.py:261
  73.2 10.4 %collective-permute-start.13 = (bf16[48,4096]{1,0:T(8,128)(2,1)S(1)}, bf16[48,4096]{1,0:T(8,128)(2,1)S(1)}, u32[]{:S(2)}, u32[]{:S(2)}) collective-permute-start(bf16[48,4096]{1,0:T(8,128)(2,1)S(1)} %get-tuple-element.77), channel_id=1, source_target_pairs={{0,2},{1,3},{2,0},{3,1},{4,6},{5,7},{6,4},{7,5},{8,10},{9,11},{10,... | collective-permute-start | bytes 1179656 | tf_op jit(solution)/shard_map/ppermute | solution.py:296
  81.7 15.5 %collective-permute-start.12 = (bf16[48,4096]{1,0:T(8,128)(2,1)S(1)}, bf16[48,4096]{1,0:T(8,128)(2,1)S(1)}, u32[]{:S(2)}, u32[]{:S(2)}) collective-permute-start(bf16[48,4096]{1,0:T(8,128)(2,1)S(1)} %get-tuple-element.76), channel_id=1, source_target_pairs={{0,2},{1,3},{2,0},{3,1},{4,6},{5,7},{6,4},{7,5},{8,10},{9,11},{10,... | collective-permute-start | bytes 1179656 | tf_op jit(solution)/shard_map/ppermute | solution.py:299
  84.4 24.8 %collective-permute-start.23 = (bf16[48,4096]{1,0:T(8,128)(2,1)S(1)}, bf16[48,4096]{1,0:T(8,128)(2,1)S(1)}, u32[]{:S(2)}, u32[]{:S(2)}) collective-permute-start(bf16[48,4096]{1,0:T(8,128)(2,1)S(1)} %get-tuple-element.75), channel_id=1, source_target_pairs={{0,2},{1,3},{2,0},{3,1},{4,6},{5,7},{6,4},{7,5},{8,10},{9,11},{10,... | collective-permute-start | bytes 1179656 | tf_op jit(solution)/shard_map/ppermute | solution.py:304
  84.8 15.8 %collective-permute-start.21 = (bf16[24,4096]{1,0:T(8,128)(2,1)S(1)}, bf16[24,4096]{1,0:T(8,128)(2,1)S(1)}, u32[]{:S(2)}, u32[]{:S(2)}) collective-permute-start(bf16[24,4096]{1,0:T(8,128)(2,1)S(1)} %get-tuple-element.105), channel_id=1, source_target_pairs={{0,26},{1,27},{2,24},{3,25},{4,30},{5,31},{6,28},{7,29},{8,18},{9,... | collective-permute-start | bytes 589832 | tf_op jit(solution)/shard_map/ppermute | solution.py:155
  86.8 22.5 %collective-permute-start.20 = (bf16[24,4096]{1,0:T(8,128)(2,1)S(1)}, bf16[24,4096]{1,0:T(8,128)(2,1)S(1)}, u32[]{:S(2)}, u32[]{:S(2)}) collective-permute-start(bf16[24,4096]{1,0:T(8,128)(2,1)S(1)} %get-tuple-element.104), channel_id=1, source_target_pairs={{0,28},{1,29},{2,22},{3,23},{4,16},{5,17},{6,26},{7,27},{8,20},{9,... | collective-permute-start | bytes 589832 | tf_op jit(solution)/shard_map/ppermute | solution.py:155
  97.4 23.7 %collective-permute-start.19 = (bf16[24,4096]{1,0:T(8,128)(2,1)S(1)}, bf16[24,4096]{1,0:T(8,128)(2,1)S(1)}, u32[]{:S(2)}, u32[]{:S(2)}) collective-permute-start(bf16[24,4096]{1,0:T(8,128)(2,1)S(1)} %get-tuple-element.103), channel_id=1, source_target_pairs={{0,30},{1,31},{2,20},{3,21},{4,18},{5,19},{6,24},{7,25},{8,22},{9,... | collective-permute-start | bytes 589832 | tf_op jit(solution)/shard_map/ppermute | solution.py:155
  97.5 23.6 %collective-permute-start.18 = (bf16[24,4096]{1,0:T(8,128)(2,1)S(1)}, bf16[24,4096]{1,0:T(8,128)(2,1)S(1)}, u32[]{:S(2)}, u32[]{:S(2)}) collective-permute-start(bf16[24,4096]{1,0:T(8,128)(2,1)S(1)} %get-tuple-element.102), channel_id=1, source_target_pairs={{0,16},{1,17},{2,18},{3,19},{4,20},{5,21},{6,22},{7,23},{8,24},{9,... | collective-permute-start | bytes 589832 | tf_op jit(solution)/shard_map/ppermute | solution.py:155
  100.6 20.4 %collective-permute-start.22 = (bf16[48,4096]{1,0:T(8,128)(2,1)S(1)}, bf16[48,4096]{1,0:T(8,128)(2,1)S(1)}, u32[]{:S(2)}, u32[]{:S(2)}) collective-permute-start(bf16[48,4096]{1,0:T(8,128)(2,1)S(1)} %get-tuple-element.64), channel_id=1, source_target_pairs={{0,2},{1,3},{2,0},{3,1},{4,6},{5,7},{6,4},{7,5},{8,10},{9,11},{10,... | collective-permute-start | bytes 1179656 | tf_op jit(solution)/shard_map/ppermute | solution.py:309
  109.3 22.9 %collective-permute-start.27 = (bf16[24,4096]{1,0:T(8,128)(2,1)S(1)}, bf16[24,4096]{1,0:T(8,128)(2,1)S(1)}, u32[]{:S(2)}, u32[]{:S(2)}) collective-permute-start(bf16[24,4096]{1,0:T(8,128)(2,1)S(1)} %get-tuple-element.101), channel_id=1, source_target_pairs={{0,250},{1,251},{2,248},{3,249},{4,254},{5,255},{6,252},{7,253},{8... | collective-permute-start | bytes 589832 | tf_op jit(solution)/shard_map/ppermute | solution.py:155
  114.0 18.2 %collective-permute-start.26 = (bf16[24,4096]{1,0:T(8,128)(2,1)S(1)}, bf16[24,4096]{1,0:T(8,128)(2,1)S(1)}, u32[]{:S(2)}, u32[]{:S(2)}) collective-permute-start(bf16[24,4096]{1,0:T(8,128)(2,1)S(1)} %get-tuple-element.100), channel_id=1, source_target_pairs={{0,252},{1,253},{2,246},{3,247},{4,240},{5,241},{6,250},{7,251},{8... | collective-permute-start | bytes 589832 | tf_op jit(solution)/shard_map/ppermute | solution.py:155
  121.1 12.8 %collective-permute-start.25 = (bf16[24,4096]{1,0:T(8,128)(2,1)S(1)}, bf16[24,4096]{1,0:T(8,128)(2,1)S(1)}, u32[]{:S(2)}, u32[]{:S(2)}) collective-permute-start(bf16[24,4096]{1,0:T(8,128)(2,1)S(1)} %get-tuple-element.99), channel_id=1, source_target_pairs={{0,254},{1,255},{2,244},{3,245},{4,242},{5,243},{6,248},{7,249},{8... | collective-permute-start | bytes 589832 | tf_op jit(solution)/shard_map/ppermute | solution.py:155
  (15 other events, 171.1 us)
